TPU v7x, 256 devices: a whole 4x4x8 slice. The times are simulated.
256 devices in a mesh: blk: 64 (over y_hi, z, x), grp: 4 (over y_lo, core).
Axes of the slice: x: 4, y: 4 (y_hi: 2, y_lo: 2; y = y_hi * 2 + y_lo), z: 8, core: 2. Of those that a mesh axis runs over, the one named last changes fastest.
Arguments:
- factors: bfloat16 [2, 24576, 24576], P(None, 'blk', 'grp'), may hold values from -0.0390625 to 0.0390625
- lower_inverse: float32 [2, 24576, 128], P(None, 'blk'), may hold values from -1 to 2
- upper_inverse: float32 [2, 24576, 128], P(None, 'blk'), may hold values from -1 to 2
- right_side: float32 [2, 24576, 512], P(None, 'blk', 'grp'), may hold values from -6 to 6
Outputs:
- solution: float32 [2, 24576, 512], P(None, 'blk', 'grp')
All inputs are finite; a program needn't handle non-finite values.
Results may differ from a plain program's by a relative error of at most 0.0027.
Values may be sent and summed in bfloat16 or wider, within the bound.
No kernel may reach another device: no remote copies, remote signals or barrier semaphores. Data moves between devices by JAX's collectives and lax.ppermute only.
A program may use at most 128 MiB of HBM per device.

v0:
```python
import jax
import jax.numpy as jnp
from jax import lax
from jax.experimental import pallas as pl
from jax.experimental.pallas import tpu as pltpu
from jax.sharding import PartitionSpec as P


INTERPRET = False
VMEM = 58 * 1024 * 1024
BOTH = ("blk", "grp")


def solve_blocks(inverse, resid):
    width = inverse.shape[1]
    count = inverse.shape[0] // width
    blocks = inverse.reshape(count, width, width)
    parts = resid.reshape(count, width, resid.shape[1])
    value = jnp.einsum(
        "nab,nbc->nac",
        blocks,
        parts,
        precision=lax.Precision.HIGHEST,
        preferred_element_type=jnp.float32,
    )
    return value.reshape(resid.shape)


def pairs(move):
    out = []
    for yh in range(2):
        for z in range(8):
            for x in range(4):
                for yl in range(2):
                    for c in range(2):
                        a, b, d, e, f = move(yh, z, x, yl, c)
                        out.append((((yh * 8 + z) * 4 + x) * 4 + yl * 2 + c, ((a * 8 + b) * 4 + d) * 4 + e * 2 + f))
    return out


def swap(flip, dz, dx):
    def move(yh, z, x, yl, c):
        zh, zl = z // 4, z % 4
        return yl ^ flip, (2 * zl + c + 6 + 4 * zh + dz) % 8, (x + dx) % 4, yh, zh

    return pairs(move)


def along_z(k):
    return pairs(lambda yh, z, x, yl, c: (yh, (z + k) % 8, x, yl, c))


def along_x(k):
    return pairs(lambda yh, z, x, yl, c: (yh, z, (x + k) % 4, yl, c))


def home(k):
    def move(yh, z, x, yl, c):
        g = (yl * 2 + c) ^ k
        return yh, z, x, g // 2, g % 2

    return pairs(move)


def send(value, perm):
    return lax.ppermute(value, BOTH, perm)


LOW, HIGH = (0, 4, 1, 5), (7, 3, 2, 6)
EVEN, ODD = (0, 2), (1, 3)


def product_kernel(place, factors, *refs):
    za, zb, outs = refs[0:8], refs[8:24], refs[24:28]
    acc, factor, whole, sem = refs[28:32]
    n = acc.shape[2]
    cols = factor.shape[1]
    step = cols // 16
    layer, z, x, yh, grp = place[0], place[1], place[2], place[3], place[4]

    def fetch(zl):
        at = pl.ds(zl * (4 * step), 4 * step)
        return pltpu.make_async_copy(factors.at[layer, :, at], factor.at[:, at], sem.at[1 + zl])

    def piece(ref, k, j, yl):
        e = lax.rem(z - k + 10 + 4 * lax.rem(grp, 2), 8)
        at = pl.multiple_of(lax.rem(x - j + 4, 4) * step, step)
        lane = pl.multiple_of((2 * yl + lax.rem(e, 2)) * n, n)
        target = whole.at[lax.div(e, 2), pl.ds(at, step), pl.ds(lane, n)]
        return pltpu.make_async_copy(ref, target, sem.at[0])

    pieces = []
    for j in range(4):
        for t, ks in enumerate((LOW, HIGH)):
            for i, k in enumerate(ks):
                pieces.append((za[2 * j + t].at[i], k, j, yh))
    for k in range(8):
        for t, js in enumerate((EVEN, ODD)):
            for i, j in enumerate(js):
                pieces.append((zb[2 * k + t].at[i], k, j, 1 - yh))
    for args in pieces:
        piece(*args).start()
    for zl in range(4):
        fetch(zl).start()
    for args in pieces:
        piece(*args).wait()
    for zl in range(4):
        fetch(zl).wait()

    def multiply(zl, value):
        at = pl.multiple_of(zl * (4 * step), 4 * step)
        return value + jnp.dot(factor[:, pl.ds(at, 4 * step)], whole[zl], preferred_element_type=jnp.float32)

    value = lax.fori_loop(0, 4, multiply, jnp.zeros((factor.shape[0], 4 * n), jnp.float32))
    for s in range(4):
        acc[s] = value[:, s * n : (s + 1) * n]
    for k in range(4):
        outs[k][...] = acc[lax.bitwise_xor(grp, k)]


def product(place, factors, za, zb):
    _, rows, cols = factors.shape
    n = za[0].shape[2]
    anywhere = pl.BlockSpec(memory_space=pl.ANY)
    vmem = pl.BlockSpec(memory_space=pltpu.VMEM)
    tile = jax.ShapeDtypeStruct((rows, n), jnp.float32)
    return pl.pallas_call(
        product_kernel,
        out_shape=[tile] * 4,
        in_specs=[pl.BlockSpec(memory_space=pltpu.SMEM)] + [anywhere] * (1 + len(za) + len(zb)),
        out_specs=[vmem] * 4,
        scratch_shapes=[
            pltpu.VMEM((4, rows, n), jnp.float32),
            pltpu.VMEM((rows, cols), jnp.bfloat16),
            pltpu.VMEM((4, cols // 4, 4 * n), jnp.bfloat16),
            pltpu.SemaphoreType.DMA((5,)),
        ],
        compiler_params=pltpu.CompilerParams(vmem_limit_bytes=VMEM),
        interpret=INTERPRET,
    )(place, factors, *za, *zb)


def coupling_of(place, factors, piece):
    two = jnp.stack([send(piece, swap(1, 0, 0)), send(piece, swap(1, 0, 2))])
    one = jnp.stack([send(piece, swap(0, 0, 0)), send(piece, swap(0, 4, 0))])
    even, odd = [two] + [None] * 7, [send(two, along_x(1))] + [None] * 7
    for k in range(1, 4):
        for rows in (even, odd):
            rows[k] = send(rows[k - 1], along_z(1))
            rows[8 - k] = send(rows[(9 - k) % 8], along_z(7))
    even[4] = send(even[3], along_z(1))
    odd[4] = send(odd[5], along_z(7))
    up, down = send(one, along_z(1)), send(one, along_z(7))
    up2 = send(up, along_z(1))
    low, high = jnp.concatenate([one, up]), jnp.concatenate([down, up2])
    low1, low3 = send(low, along_x(1)), send(low, along_x(3))
    high1, high3 = send(high, along_x(1)), send(high, along_x(3))
    low2 = send(low1, along_x(1))
    high2 = send(high3, along_x(3))
    za = [low, high, low1, high1, low2, high2, low3, high3]
    zb = [row for pair in zip(even, odd) for row in pair]
    parts = product(place, factors, za, zb)
    total = parts[0]
    for k in (3, 2, 1):
        total = total + send(parts[k], home(k))
    return total


def local(factors, lower_inverse, upper_inverse, right_side):
    blk = lax.axis_index("blk")
    forward_first = solve_blocks(lower_inverse[0], right_side[0])
    resid = jnp.stack([right_side[1], forward_first])

    def sweep(layer, carry):
        piece, _, last = carry
        place = jnp.stack([layer, blk // 4 % 8, blk % 4, blk // 32, lax.axis_index("grp")]).astype(jnp.int32)
        value = resid[layer] - coupling_of(place, factors, piece)
        forward = solve_blocks(lower_inverse[1], value)
        value = jnp.where(layer == 0, forward, value)
        value = solve_blocks(upper_inverse[1 - layer], value)
        return value.astype(jnp.bfloat16), last, value

    start = (forward_first.astype(jnp.bfloat16), forward_first, forward_first)
    _, second, first = lax.fori_loop(0, 2, sweep, start)
    return jnp.stack([first, second])


def solution(mesh):
    in_specs = (
        P(None, "blk", "grp"),
        P(None, "blk", None),
        P(None, "blk", None),
        P(None, "blk", "grp"),
    )
    out_specs = P(None, "blk", "grp")
    return jax.shard_map(local, mesh=mesh, in_specs=in_specs, out_specs=out_specs, check_vma=False)
```

profile of v0, /device:TPU:2, one launch (start us, length us, event | category | flops | bytes accessed | tf_op | source)
XLA Modules:
  0.0 192.0 jit_solution(11673342745482361692)
XLA Ops:
  0.0 1.0 fusion
  3.2 187.1 %while.21 = (s32[]{:T(128)}, bf16[384,128]{1,0:T(8,128)(2,1)S(1)}, f32[384,128]{1,0:T(8,128)}, f32[384,128]{1,0:T(8,128)S(1)}, f32[2,384,128]{2,1,0:T(8,128)}, /...) while((s32[]{:T(128)}, bf16[384,128]{1,0:T(8,128)(2,1)S(1)}, ...), condition=%wide.region_1.2_spmd, body=%wide.region_0.1_spmd.sunk | while | flops 151879680 | bytes 54757340 | solution.py:184
  3.2 3.3 %collective-permute-start = (bf16[384,128]{1,0:T(8,128)(2,1)S(1)}, bf16[384,128]{1,0:T(8,128)(2,1)S(1)}, u32[]{:S(2)}, u32[]{:S(2)}) collective-permute-start(bf16[384,128]{1,0:T(8,128)(2,1)S(1)} %get-tuple-element.621), channel_id=1, source_target_pairs={{0,32},{1,48},{2,160},{3,176},{4,36},{5,52},{6,164},{7,180},{8,40}... | collective-permute-start | bytes 294920 | tf_op jit(solution)/shard_map/while/body/eval_jaxpr/ppermute | solution.py:66
  6.6 5.0 %collective-permute-start.1 = (bf16[384,128]{1,0:T(8,128)(2,1)S(1)}, bf16[384,128]{1,0:T(8,128)(2,1)S(1)}, u32[]{:S(2)}, u32[]{:S(2)}) collective-permute-start(bf16[384,128]{1,0:T(8,128)(2,1)S(1)} %get-tuple-element.621), channel_id=1, source_target_pairs={{0,96},{1,112},{2,224},{3,240},{4,100},{5,116},{6,228},{7,244},{8,... | collective-permute-start | bytes 294920 | tf_op jit(solution)/shard_map/while/body/eval_jaxpr/ppermute | solution.py:66
  11.5 5.9 %collective-permute-start.11 = (bf16[384,128]{1,0:T(8,128)(2,1)S(1)}, bf16[384,128]{1,0:T(8,128)(2,1)S(1)}, u32[]{:S(2)}, u32[]{:S(2)}) collective-permute-start(bf16[384,128]{1,0:T(8,128)(2,1)S(1)} %get-tuple-element.621), channel_id=1, source_target_pairs={{0,232},{1,248},{2,104},{3,120},{4,236},{5,252},{6,108},{7,124},{8... | collective-permute-start | bytes 294920 | tf_op jit(solution)/shard_map/while/body/eval_jaxpr/ppermute | solution.py:66
  17.4 1.0 collective-permute-start.12
  19.2 1.4 collective-permute-done.11
  20.6 2.6 %collective-permute-done.12 = bf16[384,128]{1,0:T(8,128)(2,1)S(1)} collective-permute-done((bf16[384,128]{1,0:T(8,128)(2,1)S(1)}, bf16[384,128]{1,0:T(8,128)(2,1)S(1)}, u32[]{:S(2)}, u32[]{:S(2)}) %collective-permute-start.12) | collective-permute-done | bytes 98336 | tf_op jit(solution)/shard_map/while/body/eval_jaxpr/ppermute | solution.py:66
  23.4 4.0 %collective-permute-start.3 = (bf16[2,384,128]{2,1,0:T(8,128)(2,1)S(1)}, bf16[2,384,128]{2,1,0:T(8,128)(2,1)S(1)}, u32[]{:S(2)}, u32[]{:S(2)}) collective-permute-start(bf16[2,384,128]{2,1,0:T(8,128)(2,1)S(1)} %pad_maximum_fusion.8), channel_id=1, source_target_pairs={{0,112},{1,113},{2,114},{3,115},{4,116},{5,117},{6,118},{7,119},{8... | collective-permute-start | bytes 589832 | tf_op jit(solution)/shard_map/while/body/eval_jaxpr/ppermute | solution.py:66
  27.4 3.2 %collective-permute-start.25 = (bf16[2,384,128]{2,1,0:T(8,128)(2,1)S(1)}, bf16[2,384,128]{2,1,0:T(8,128)(2,1)S(1)}, u32[]{:S(2)}, u32[]{:S(2)}) collective-permute-start(bf16[2,384,128]{2,1,0:T(8,128)(2,1)S(1)} %pad_maximum_fusion.10.refs_8_), channel_id=1, source_target_pairs={{0,112},{1,113},{2,114},{3,115},{4,116},{5,117},{6,118},{7,119},{8... | collective-permute-start | bytes 589832 | tf_op jit(solution)/shard_map/while/body/eval_jaxpr/ppermute | solution.py:66
  31.0 2.9 %collective-permute-start.21 = (bf16[2,384,128]{2,1,0:T(8,128)(2,1)S(1)}, bf16[2,384,128]{2,1,0:T(8,128)(2,1)S(1)}, u32[]{:S(2)}, u32[]{:S(2)}) collective-permute-start(bf16[2,384,128]{2,1,0:T(8,128)(2,1)S(1)} %collective-permute-done.13.refs_9_), channel_id=1, source_target_pairs={{0,112},{1,113},{2,114},{3,115},{4,116},{5,117},{6,118},{7,119},{8... | collective-permute-start | bytes 589832 | tf_op jit(solution)/shard_map/while/body/eval_jaxpr/ppermute | solution.py:66
  34.0 1.7 collective-permute-start.5
  36.5 2.4 %collective-permute-done.4 = bf16[2,384,128]{2,1,0:T(8,128)(2,1)S(1)} collective-permute-done((bf16[2,384,128]{2,1,0:T(8,128)(2,1)S(1)}, bf16[2,384,128]{2,1,0:T(8,128)(2,1)S(1)}, u32[]{:S(2)}, u32[]{:S(2)}) %collective-permute-start.4) | collective-permute-done | bytes 196640 | tf_op jit(solution)/shard_map/while/body/eval_jaxpr/ppermute | solution.py:66
  39.9 2.9 %collective-permute-start.26 = (bf16[2,384,128]{2,1,0:T(8,128)(2,1)S(1)}, bf16[2,384,128]{2,1,0:T(8,128)(2,1)S(1)}, u32[]{:S(2)}, u32[]{:S(2)}) collective-permute-start(bf16[2,384,128]{2,1,0:T(8,128)(2,1)S(1)} %collective-permute-done.25.refs_22_), channel_id=1, source_target_pairs={{0,112},{1,113},{2,114},{3,115},{4,116},{5,117},{6,118},{7,119},{8... | collective-permute-start | bytes 589832 | tf_op jit(solution)/shard_map/while/body/eval_jaxpr/ppermute | solution.py:66
  42.8 2.5 %collective-permute-done.15.refs_11_ = bf16[2,384,128]{2,1,0:T(8,128)(2,1)S(1)} collective-permute-done((bf16[2,384,128]{2,1,0:T(8,128)(2,1)S(1)}, bf16[2,384,128]{2,1,0:T(8,128)(2,1)S(1)}, u32[]{:S(2)}, u32[]{:S(2)}) %collective-permute-start.15) | collective-permute-done | bytes 196640 | tf_op jit(solution)/shard_map/while/body/eval_jaxpr/ppermute | solution.py:66
  45.3 2.3 %collective-permute-start.8 = (bf16[4,384,128]{2,1,0:T(8,128)(2,1)S(1)}, bf16[4,384,128]{2,1,0:T(8,128)(2,1)S(1)}, u32[]{:S(2)}, u32[]{:S(2)}) collective-permute-start(bf16[4,384,128]{2,1,0:T(8,128)(2,1)S(1)} %constant_dynamic-update-slice_fusion.5.refs_1_), channel_id=1, source_target_pairs={{0,12},{1,13},{2,14},{3,15},{4,0},{5,1},{6,2},{7,3},{8,4},{9,5},{1... | collective-permute-start | bytes 1179656 | tf_op jit(solution)/shard_map/while/body/eval_jaxpr/ppermute | solution.py:66
  47.9 1.5 collective-permute-start.6
  50.4 1.1 collective-permute-start.17
  52.2 2.8 %collective-permute-done.22.refs_21_ = bf16[2,384,128]{2,1,0:T(8,128)(2,1)S(1)} collective-permute-done((bf16[2,384,128]{2,1,0:T(8,128)(2,1)S(1)}, bf16[2,384,128]{2,1,0:T(8,128)(2,1)S(1)}, u32[]{:S(2)}, u32[]{:S(2)}) %collective-permute-start.22) | collective-permute-done | bytes 196640 | tf_op jit(solution)/shard_map/while/body/eval_jaxpr/ppermute | solution.py:66
  55.1 2.2 %collective-permute-start.27 = (bf16[2,384,128]{2,1,0:T(8,128)(2,1)S(1)}, bf16[2,384,128]{2,1,0:T(8,128)(2,1)S(1)}, u32[]{:S(2)}, u32[]{:S(2)}) collective-permute-start(bf16[2,384,128]{2,1,0:T(8,128)(2,1)S(1)} %collective-permute-done.26.refs_20_), channel_id=1, source_target_pairs={{0,112},{1,113},{2,114},{3,115},{4,116},{5,117},{6,118},{7,119},{8... | collective-permute-start | bytes 589832 | tf_op jit(solution)/shard_map/while/body/eval_jaxpr/ppermute | solution.py:66
  58.0 1.9 collective-permute-start.7
  60.1 1.5 collective-permute-start.23
  62.0 1.4 collective-permute-start.19
  64.1 1.7 collective-permute-done.23.refs_19_
  65.9 2.7 %collective-permute-start.24 = (bf16[2,384,128]{2,1,0:T(8,128)(2,1)}, bf16[2,384,128]{2,1,0:T(8,128)(2,1)}, u32[]{:S(2)}, u32[]{:S(2)}) collective-permute-start(bf16[2,384,128]{2,1,0:T(8,128)(2,1)} %collective-permute-done.23.refs_19_), channel_id=1, source_target_pairs={{0,112},{1,113},{2,114},{3,115},{4,116},{5,117},{6,118},{7,119},{8... | collective-permute-start | bytes 589832 | tf_op jit(solution)/shard_map/while/body/eval_jaxpr/ppermute | solution.py:66
  69.7 2.1 %collective-permute-done.20.refs_16_ = bf16[2,384,128]{2,1,0:T(8,128)(2,1)} collective-permute-done((bf16[2,384,128]{2,1,0:T(8,128)(2,1)}, bf16[2,384,128]{2,1,0:T(8,128)(2,1)}, u32[]{:S(2)}, u32[]{:S(2)}) %collective-permute-start.20) | collective-permute-done | bytes 196640 | tf_op jit(solution)/shard_map/while/body/eval_jaxpr/ppermute | solution.py:66
  71.9 1.5 collective-permute-done.24.refs_17_
  74.1 9.4 %eval_jaxpr.10 = (f32[384,128]{1,0:T(8,128)}, f32[384,128]{1,0:T(8,128)}, f32[384,128]{1,0:T(8,128)}, f32[384,128]{1,0:T(8,128)}) custom-call(s32[5]{0:T(128)} %stack.143.place, bf16[2,384,6144]{2,1,0:T(8,128)(2,1)} %get-tuple-element.644.factors, bf16[4,384,128]{2,1,0:T(8,128)(2,1)} %copy-done, bf16[4,384,128]{2,1,0:T(8,128)(2,1)} %copy-done.1, ...), custom_call_target="tpu_custom_call" | custom-call | tf_op jit(solution)/shard_map/while/body/eval_jaxpr/pallas_call | solution.py:127
  83.7 3.1 %collective-permute-start.29 = (f32[384,128]{1,0:T(8,128)}, f32[384,128]{1,0:T(8,128)S(1)}, u32[]{:S(2)}, u32[]{:S(2)}) collective-permute-start(f32[384,128]{1,0:T(8,128)} %get-tuple-element.602), channel_id=1, source_target_pairs={{0,2},{1,3},{2,0},{3,1},{4,6},{5,7},{6,4},{7,5},{8,10},{9,11},{10,... | collective-permute-start | bytes 589832 | tf_op jit(solution)/shard_map/while/body/eval_jaxpr/ppermute | solution.py:66
  89.4 3.4 %collective-permute-done.29 = f32[384,128]{1,0:T(8,128)S(1)} collective-permute-done((f32[384,128]{1,0:T(8,128)}, f32[384,128]{1,0:T(8,128)S(1)}, u32[]{:S(2)}, u32[]{:S(2)}) %collective-permute-start.29) | collective-permute-done | bytes 196640 | tf_op jit(solution)/shard_map/while/body/eval_jaxpr/ppermute | solution.py:66
  92.7 3.6 %collective-permute-done.30 = f32[384,128]{1,0:T(8,128)S(1)} collective-permute-done((f32[384,128]{1,0:T(8,128)}, f32[384,128]{1,0:T(8,128)S(1)}, u32[]{:S(2)}, u32[]{:S(2)}) %collective-permute-start.30) | collective-permute-done | bytes 196640 | tf_op jit(solution)/shard_map/while/body/eval_jaxpr/ppermute | solution.py:66
  96.4 1.1 bitcast_subtract_fusion.2
  98.3 5.4 %collective-permute-start.1 = (bf16[384,128]{1,0:T(8,128)(2,1)S(1)}, bf16[384,128]{1,0:T(8,128)(2,1)S(1)}, u32[]{:S(2)}, u32[]{:S(2)}) collective-permute-start(bf16[384,128]{1,0:T(8,128)(2,1)S(1)} %get-tuple-element.621), channel_id=1, source_target_pairs={{0,96},{1,112},{2,224},{3,240},{4,100},{5,116},{6,228},{7,244},{8,... | collective-permute-start | bytes 294920 | tf_op jit(solution)/shard_map/while/body/eval_jaxpr/ppermute | solution.py:66
  103.7 6.3 %collective-permute-start.11 = (bf16[384,128]{1,0:T(8,128)(2,1)S(1)}, bf16[384,128]{1,0:T(8,128)(2,1)S(1)}, u32[]{:S(2)}, u32[]{:S(2)}) collective-permute-start(bf16[384,128]{1,0:T(8,128)(2,1)S(1)} %get-tuple-element.621), channel_id=1, source_target_pairs={{0,232},{1,248},{2,104},{3,120},{4,236},{5,252},{6,108},{7,124},{8... | collective-permute-start | bytes 294920 | tf_op jit(solution)/shard_map/while/body/eval_jaxpr/ppermute | solution.py:66
  111.0 2.2 %collective-permute-done.11 = bf16[384,128]{1,0:T(8,128)(2,1)S(1)} collective-permute-done((bf16[384,128]{1,0:T(8,128)(2,1)S(1)}, bf16[384,128]{1,0:T(8,128)(2,1)S(1)}, u32[]{:S(2)}, u32[]{:S(2)}) %collective-permute-start.11) | collective-permute-done | bytes 98336 | tf_op jit(solution)/shard_map/while/body/eval_jaxpr/ppermute | solution.py:66
  113.2 2.8 %collective-permute-done.12 = bf16[384,128]{1,0:T(8,128)(2,1)S(1)} collective-permute-done((bf16[384,128]{1,0:T(8,128)(2,1)S(1)}, bf16[384,128]{1,0:T(8,128)(2,1)S(1)}, u32[]{:S(2)}, u32[]{:S(2)}) %collective-permute-start.12) | collective-permute-done | bytes 98336 | tf_op jit(solution)/shard_map/while/body/eval_jaxpr/ppermute | solution.py:66
  116.0 2.1 %collective-permute-start.3 = (bf16[2,384,128]{2,1,0:T(8,128)(2,1)S(1)}, bf16[2,384,128]{2,1,0:T(8,128)(2,1)S(1)}, u32[]{:S(2)}, u32[]{:S(2)}) collective-permute-start(bf16[2,384,128]{2,1,0:T(8,128)(2,1)S(1)} %pad_maximum_fusion.8), channel_id=1, source_target_pairs={{0,112},{1,113},{2,114},{3,115},{4,116},{5,117},{6,118},{7,119},{8... | collective-permute-start | bytes 589832 | tf_op jit(solution)/shard_map/while/body/eval_jaxpr/ppermute | solution.py:66
  118.2 3.2 %collective-permute-start.25 = (bf16[2,384,128]{2,1,0:T(8,128)(2,1)S(1)}, bf16[2,384,128]{2,1,0:T(8,128)(2,1)S(1)}, u32[]{:S(2)}, u32[]{:S(2)}) collective-permute-start(bf16[2,384,128]{2,1,0:T(8,128)(2,1)S(1)} %pad_maximum_fusion.10.refs_8_), channel_id=1, source_target_pairs={{0,112},{1,113},{2,114},{3,115},{4,116},{5,117},{6,118},{7,119},{8... | collective-permute-start | bytes 589832 | tf_op jit(solution)/shard_map/while/body/eval_jaxpr/ppermute | solution.py:66
  121.4 1.6 collective-permute-done.13.refs_9_
  123.0 1.6 collective-permute-start.21
  124.7 1.2 collective-permute-start.5
  126.7 1.4 collective-permute-start.10
  129.4 1.6 collective-permute-start.16
  131.1 1.3 collective-permute-done.21.refs_23_
  132.3 1.5 collective-permute-start.26
  133.9 3.2 %collective-permute-done.15.refs_11_ = bf16[2,384,128]{2,1,0:T(8,128)(2,1)S(1)} collective-permute-done((bf16[2,384,128]{2,1,0:T(8,128)(2,1)S(1)}, bf16[2,384,128]{2,1,0:T(8,128)(2,1)S(1)}, u32[]{:S(2)}, u32[]{:S(2)}) %collective-permute-start.15) | collective-permute-done | bytes 196640 | tf_op jit(solution)/shard_map/while/body/eval_jaxpr/ppermute | solution.py:66
  137.1 2.9 %collective-permute-start.8 = (bf16[4,384,128]{2,1,0:T(8,128)(2,1)S(1)}, bf16[4,384,128]{2,1,0:T(8,128)(2,1)S(1)}, u32[]{:S(2)}, u32[]{:S(2)}) collective-permute-start(bf16[4,384,128]{2,1,0:T(8,128)(2,1)S(1)} %constant_dynamic-update-slice_fusion.5.refs_1_), channel_id=1, source_target_pairs={{0,12},{1,13},{2,14},{3,15},{4,0},{5,1},{6,2},{7,3},{8,4},{9,5},{1... | collective-permute-start | bytes 1179656 | tf_op jit(solution)/shard_map/while/body/eval_jaxpr/ppermute | solution.py:66
  140.5 2.7 %collective-permute-start.6 = (bf16[4,384,128]{2,1,0:T(8,128)(2,1)S(1)}, bf16[4,384,128]{2,1,0:T(8,128)(2,1)S(1)}, u32[]{:S(2)}, u32[]{:S(2)}) collective-permute-start(bf16[4,384,128]{2,1,0:T(8,128)(2,1)S(1)} %constant_dynamic-update-slice_fusion.5.refs_1_), channel_id=1, source_target_pairs={{0,4},{1,5},{2,6},{3,7},{4,8},{5,9},{6,10},{7,11},{8,12},{9,13},{1... | collective-permute-start | bytes 1179656 | tf_op jit(solution)/shard_map/while/body/eval_jaxpr/ppermute | solution.py:66
  143.2 1.9 %collective-permute-start.17 = (bf16[2,384,128]{2,1,0:T(8,128)(2,1)S(1)}, bf16[2,384,128]{2,1,0:T(8,128)(2,1)}, u32[]{:S(2)}, u32[]{:S(2)}) collective-permute-start(bf16[2,384,128]{2,1,0:T(8,128)(2,1)S(1)} %collective-permute-done.15.refs_11_), channel_id=1, source_target_pairs={{0,16},{1,17},{2,18},{3,19},{4,20},{5,21},{6,22},{7,23},{8,24},{9,... | collective-permute-start | bytes 589832 | tf_op jit(solution)/shard_map/while/body/eval_jaxpr/ppermute | solution.py:66
  145.3 4.4 %collective-permute-done.22.refs_21_ = bf16[2,384,128]{2,1,0:T(8,128)(2,1)S(1)} collective-permute-done((bf16[2,384,128]{2,1,0:T(8,128)(2,1)S(1)}, bf16[2,384,128]{2,1,0:T(8,128)(2,1)S(1)}, u32[]{:S(2)}, u32[]{:S(2)}) %collective-permute-start.22) | collective-permute-done | bytes 196640 | tf_op jit(solution)/shard_map/while/body/eval_jaxpr/ppermute | solution.py:66
  149.7 1.5 collective-permute-start.27
  151.2 1.2 collective-permute-done.17.refs_13_
  152.3 2.1 %collective-permute-start.7 = (bf16[4,384,128]{2,1,0:T(8,128)(2,1)S(1)}, bf16[4,384,128]{2,1,0:T(8,128)(2,1)S(1)}, u32[]{:S(2)}, u32[]{:S(2)}) collective-permute-start(bf16[4,384,128]{2,1,0:T(8,128)(2,1)S(1)} %collective-permute-done.5.refs_2_), channel_id=1, source_target_pairs={{0,4},{1,5},{2,6},{3,7},{4,8},{5,9},{6,10},{7,11},{8,12},{9,13},{1... | collective-permute-start | bytes 1179656 | tf_op jit(solution)/shard_map/while/body/eval_jaxpr/ppermute | solution.py:66
  155.5 1.9 %collective-permute-start.19 = (bf16[2,384,128]{2,1,0:T(8,128)(2,1)}, bf16[2,384,128]{2,1,0:T(8,128)(2,1)}, u32[]{:S(2)}, u32[]{:S(2)}) collective-permute-start(bf16[2,384,128]{2,1,0:T(8,128)(2,1)} %collective-permute-done.17.refs_13_), channel_id=1, source_target_pairs={{0,16},{1,17},{2,18},{3,19},{4,20},{5,21},{6,22},{7,23},{8,24},{9,... | collective-permute-start | bytes 589832 | tf_op jit(solution)/shard_map/while/body/eval_jaxpr/ppermute | solution.py:66
  158.0 3.1 %collective-permute-done.23.refs_19_ = bf16[2,384,128]{2,1,0:T(8,128)(2,1)} collective-permute-done((bf16[2,384,128]{2,1,0:T(8,128)(2,1)S(1)}, bf16[2,384,128]{2,1,0:T(8,128)(2,1)}, u32[]{:S(2)}, u32[]{:S(2)}) %collective-permute-start.23) | collective-permute-done | bytes 196640 | tf_op jit(solution)/shard_map/while/body/eval_jaxpr/ppermute | solution.py:66
  161.1 1.5 collective-permute-start.24
  163.3 1.5 collective-permute-done.19.refs_15_
  164.8 2.1 %collective-permute-done.20.refs_16_ = bf16[2,384,128]{2,1,0:T(8,128)(2,1)} collective-permute-done((bf16[2,384,128]{2,1,0:T(8,128)(2,1)}, bf16[2,384,128]{2,1,0:T(8,128)(2,1)}, u32[]{:S(2)}, u32[]{:S(2)}) %collective-permute-start.20) | collective-permute-done | bytes 196640 | tf_op jit(solution)/shard_map/while/body/eval_jaxpr/ppermute | solution.py:66
  167.8 9.4 %eval_jaxpr.10 = (f32[384,128]{1,0:T(8,128)}, f32[384,128]{1,0:T(8,128)}, f32[384,128]{1,0:T(8,128)}, f32[384,128]{1,0:T(8,128)}) custom-call(s32[5]{0:T(128)} %stack.143.place, bf16[2,384,6144]{2,1,0:T(8,128)(2,1)} %get-tuple-element.644.factors, bf16[4,384,128]{2,1,0:T(8,128)(2,1)} %copy-done, bf16[4,384,128]{2,1,0:T(8,128)(2,1)} %copy-done.1, ...), custom_call_target="tpu_custom_call" | custom-call | tf_op jit(solution)/shard_map/while/body/eval_jaxpr/pallas_call | solution.py:127
  177.4 1.7 collective-permute-start.30
  181.8 3.6 %collective-permute-done.29 = f32[384,128]{1,0:T(8,128)S(1)} collective-permute-done((f32[384,128]{1,0:T(8,128)}, f32[384,128]{1,0:T(8,128)S(1)}, u32[]{:S(2)}, u32[]{:S(2)}) %collective-permute-start.29) | collective-permute-done | bytes 196640 | tf_op jit(solution)/shard_map/while/body/eval_jaxpr/ppermute | solution.py:66
  185.4 3.1 %collective-permute-done.30 = f32[384,128]{1,0:T(8,128)S(1)} collective-permute-done((f32[384,128]{1,0:T(8,128)}, f32[384,128]{1,0:T(8,128)S(1)}, u32[]{:S(2)}, u32[]{:S(2)}) %collective-permute-start.30) | collective-permute-done | bytes 196640 | tf_op jit(solution)/shard_map/while/body/eval_jaxpr/ppermute | solution.py:66
  188.5 1.1 bitcast_subtract_fusion.2
  190.3 1.7 pad_maximum_fusion.4
  (172 shorter events, 25.2 us)
Async XLA Ops:
  3.2 15.2 %collective-permute-start = (bf16[384,128]{1,0:T(8,128)(2,1)S(1)}, bf16[384,128]{1,0:T(8,128)(2,1)S(1)}, u32[]{:S(2)}, u32[]{:S(2)}) collective-permute-start(bf16[384,128]{1,0:T(8,128)(2,1)S(1)} %get-tuple-element.621), channel_id=1, source_target_pairs={{0,32},{1,48},{2,160},{3,176},{4,36},{5,52},{6,164},{7,180},{8,40}... | collective-permute-start | bytes 294920 | tf_op jit(solution)/shard_map/while/body/eval_jaxpr/ppermute | solution.py:66
  6.6 11.9 %collective-permute-start.1 = (bf16[384,128]{1,0:T(8,128)(2,1)S(1)}, bf16[384,128]{1,0:T(8,128)(2,1)S(1)}, u32[]{:S(2)}, u32[]{:S(2)}) collective-permute-start(bf16[384,128]{1,0:T(8,128)(2,1)S(1)} %get-tuple-element.621), channel_id=1, source_target_pairs={{0,96},{1,112},{2,224},{3,240},{4,100},{5,116},{6,228},{7,244},{8,... | collective-permute-start | bytes 294920 | tf_op jit(solution)/shard_map/while/body/eval_jaxpr/ppermute | solution.py:66
  11.5 9.1 %collective-permute-start.11 = (bf16[384,128]{1,0:T(8,128)(2,1)S(1)}, bf16[384,128]{1,0:T(8,128)(2,1)S(1)}, u32[]{:S(2)}, u32[]{:S(2)}) collective-permute-start(bf16[384,128]{1,0:T(8,128)(2,1)S(1)} %get-tuple-element.621), channel_id=1, source_target_pairs={{0,232},{1,248},{2,104},{3,120},{4,236},{5,252},{6,108},{7,124},{8... | collective-permute-start | bytes 294920 | tf_op jit(solution)/shard_map/while/body/eval_jaxpr/ppermute | solution.py:66
  17.4 5.8 %collective-permute-start.12 = (bf16[384,128]{1,0:T(8,128)(2,1)S(1)}, bf16[384,128]{1,0:T(8,128)(2,1)S(1)}, u32[]{:S(2)}, u32[]{:S(2)}) collective-permute-start(bf16[384,128]{1,0:T(8,128)(2,1)S(1)} %get-tuple-element.621), channel_id=1, source_target_pairs={{0,224},{1,240},{2,96},{3,112},{4,228},{5,244},{6,100},{7,116},{8,... | collective-permute-start | bytes 294920 | tf_op jit(solution)/shard_map/while/body/eval_jaxpr/ppermute | solution.py:66
  18.5 12.2 %collective-permute-start.2 = (bf16[2,384,128]{2,1,0:T(8,128)(2,1)S(1)}, bf16[2,384,128]{2,1,0:T(8,128)(2,1)S(1)}, u32[]{:S(2)}, u32[]{:S(2)}) collective-permute-start(bf16[2,384,128]{2,1,0:T(8,128)(2,1)S(1)} %pad_maximum_fusion.8), channel_id=1, source_target_pairs={{0,16},{1,17},{2,18},{3,19},{4,20},{5,21},{6,22},{7,23},{8,24},{9,... | collective-permute-start | bytes 589832 | tf_op jit(solution)/shard_map/while/body/eval_jaxpr/ppermute | solution.py:66
  23.2 50.2 %copy-start.2 = (bf16[2,384,128]{2,1,0:T(8,128)(2,1)}, bf16[2,384,128]{2,1,0:T(8,128)(2,1)S(1)}, u32[]{:S(2)}) copy-start(bf16[2,384,128]{2,1,0:T(8,128)(2,1)S(1)} %pad_maximum_fusion.10.refs_8_) | copy-start | bytes 589828 | tf_op jit(solution)/shard_map/while
  23.2 7.8 %collective-permute-start.13 = (bf16[2,384,128]{2,1,0:T(8,128)(2,1)S(1)}, bf16[2,384,128]{2,1,0:T(8,128)(2,1)S(1)}, u32[]{:S(2)}, u32[]{:S(2)}) collective-permute-start(bf16[2,384,128]{2,1,0:T(8,128)(2,1)S(1)} %pad_maximum_fusion.10.refs_8_), channel_id=1, source_target_pairs={{0,4},{1,5},{2,6},{3,7},{4,8},{5,9},{6,10},{7,11},{8,12},{9,13},{1... | collective-permute-start | bytes 589832 | tf_op jit(solution)/shard_map/while/body/eval_jaxpr/ppermute | solution.py:66
  23.4 10.6 %collective-permute-start.3 = (bf16[2,384,128]{2,1,0:T(8,128)(2,1)S(1)}, bf16[2,384,128]{2,1,0:T(8,128)(2,1)S(1)}, u32[]{:S(2)}, u32[]{:S(2)}) collective-permute-start(bf16[2,384,128]{2,1,0:T(8,128)(2,1)S(1)} %pad_maximum_fusion.8), channel_id=1, source_target_pairs={{0,112},{1,113},{2,114},{3,115},{4,116},{5,117},{6,118},{7,119},{8... | collective-permute-start | bytes 589832 | tf_op jit(solution)/shard_map/while/body/eval_jaxpr/ppermute | solution.py:66
  27.4 8.3 %collective-permute-start.14 = (bf16[2,384,128]{2,1,0:T(8,128)(2,1)S(1)}, bf16[2,384,128]{2,1,0:T(8,128)(2,1)S(1)}, u32[]{:S(2)}, u32[]{:S(2)}) collective-permute-start(bf16[2,384,128]{2,1,0:T(8,128)(2,1)S(1)} %pad_maximum_fusion.10.refs_8_), channel_id=1, source_target_pairs={{0,16},{1,17},{2,18},{3,19},{4,20},{5,21},{6,22},{7,23},{8,24},{9,... | collective-permute-start | bytes 589832 | tf_op jit(solution)/shard_map/while/body/eval_jaxpr/ppermute | solution.py:66
  27.4 9.0 %collective-permute-start.25 = (bf16[2,384,128]{2,1,0:T(8,128)(2,1)S(1)}, bf16[2,384,128]{2,1,0:T(8,128)(2,1)S(1)}, u32[]{:S(2)}, u32[]{:S(2)}) collective-permute-start(bf16[2,384,128]{2,1,0:T(8,128)(2,1)S(1)} %pad_maximum_fusion.10.refs_8_), channel_id=1, source_target_pairs={{0,112},{1,113},{2,114},{3,115},{4,116},{5,117},{6,118},{7,119},{8... | collective-permute-start | bytes 589832 | tf_op jit(solution)/shard_map/while/body/eval_jaxpr/ppermute | solution.py:66
  30.7 8.2 %collective-permute-start.4 = (bf16[2,384,128]{2,1,0:T(8,128)(2,1)S(1)}, bf16[2,384,128]{2,1,0:T(8,128)(2,1)S(1)}, u32[]{:S(2)}, u32[]{:S(2)}) collective-permute-start(bf16[2,384,128]{2,1,0:T(8,128)(2,1)S(1)} %collective-permute-done.2), channel_id=1, source_target_pairs={{0,16},{1,17},{2,18},{3,19},{4,20},{5,21},{6,22},{7,23},{8,24},{9,... | collective-permute-start | bytes 589832 | tf_op jit(solution)/shard_map/while/body/eval_jaxpr/ppermute | solution.py:66
  31.0 8.9 %collective-permute-start.21 = (bf16[2,384,128]{2,1,0:T(8,128)(2,1)S(1)}, bf16[2,384,128]{2,1,0:T(8,128)(2,1)S(1)}, u32[]{:S(2)}, u32[]{:S(2)}) collective-permute-start(bf16[2,384,128]{2,1,0:T(8,128)(2,1)S(1)} %collective-permute-done.13.refs_9_), channel_id=1, source_target_pairs={{0,112},{1,113},{2,114},{3,115},{4,116},{5,117},{6,118},{7,119},{8... | collective-permute-start | bytes 589832 | tf_op jit(solution)/shard_map/while/body/eval_jaxpr/ppermute | solution.py:66
  34.0 16.4 %collective-permute-start.5 = (bf16[4,384,128]{2,1,0:T(8,128)(2,1)S(1)}, bf16[4,384,128]{2,1,0:T(8,128)(2,1)S(1)}, u32[]{:S(2)}, u32[]{:S(2)}) collective-permute-start(bf16[4,384,128]{2,1,0:T(8,128)(2,1)S(1)} %pad_maximum_fusion.9.refs_0_), channel_id=1, source_target_pairs={{0,4},{1,5},{2,6},{3,7},{4,8},{5,9},{6,10},{7,11},{8,12},{9,13},{1... | collective-permute-start | bytes 1179656 | tf_op jit(solution)/shard_map/while/body/eval_jaxpr/ppermute | solution.py:66
  35.7 15.7 %collective-permute-start.10 = (bf16[4,384,128]{2,1,0:T(8,128)(2,1)S(1)}, bf16[4,384,128]{2,1,0:T(8,128)(2,1)S(1)}, u32[]{:S(2)}, u32[]{:S(2)}) collective-permute-start(bf16[4,384,128]{2,1,0:T(8,128)(2,1)S(1)} %pad_maximum_fusion.9.refs_0_), channel_id=1, source_target_pairs={{0,12},{1,13},{2,14},{3,15},{4,0},{5,1},{6,2},{7,3},{8,4},{9,5},{1... | collective-permute-start | bytes 1179656 | tf_op jit(solution)/shard_map/while/body/eval_jaxpr/ppermute | solution.py:66
  36.5 8.9 %collective-permute-start.15 = (bf16[2,384,128]{2,1,0:T(8,128)(2,1)S(1)}, bf16[2,384,128]{2,1,0:T(8,128)(2,1)S(1)}, u32[]{:S(2)}, u32[]{:S(2)}) collective-permute-start(bf16[2,384,128]{2,1,0:T(8,128)(2,1)S(1)} %collective-permute-done.13.refs_9_), channel_id=1, source_target_pairs={{0,16},{1,17},{2,18},{3,19},{4,20},{5,21},{6,22},{7,23},{8,24},{9,... | collective-permute-start | bytes 589832 | tf_op jit(solution)/shard_map/while/body/eval_jaxpr/ppermute | solution.py:66
  38.9 9.0 %collective-permute-start.16 = (bf16[2,384,128]{2,1,0:T(8,128)(2,1)S(1)}, bf16[2,384,128]{2,1,0:T(8,128)(2,1)S(1)}, u32[]{:S(2)}, u32[]{:S(2)}) collective-permute-start(bf16[2,384,128]{2,1,0:T(8,128)(2,1)S(1)} %collective-permute-done.14.refs_10_), channel_id=1, source_target_pairs={{0,16},{1,17},{2,18},{3,19},{4,20},{5,21},{6,22},{7,23},{8,24},{9,... | collective-permute-start | bytes 589832 | tf_op jit(solution)/shard_map/while/body/eval_jaxpr/ppermute | solution.py:66
  39.9 9.5 %collective-permute-start.26 = (bf16[2,384,128]{2,1,0:T(8,128)(2,1)S(1)}, bf16[2,384,128]{2,1,0:T(8,128)(2,1)S(1)}, u32[]{:S(2)}, u32[]{:S(2)}) collective-permute-start(bf16[2,384,128]{2,1,0:T(8,128)(2,1)S(1)} %collective-permute-done.25.refs_22_), channel_id=1, source_target_pairs={{0,112},{1,113},{2,114},{3,115},{4,116},{5,117},{6,118},{7,119},{8... | collective-permute-start | bytes 589832 | tf_op jit(solution)/shard_map/while/body/eval_jaxpr/ppermute | solution.py:66
  45.3 16.3 %collective-permute-start.8 = (bf16[4,384,128]{2,1,0:T(8,128)(2,1)S(1)}, bf16[4,384,128]{2,1,0:T(8,128)(2,1)S(1)}, u32[]{:S(2)}, u32[]{:S(2)}) collective-permute-start(bf16[4,384,128]{2,1,0:T(8,128)(2,1)S(1)} %constant_dynamic-update-slice_fusion.5.refs_1_), channel_id=1, source_target_pairs={{0,12},{1,13},{2,14},{3,15},{4,0},{5,1},{6,2},{7,3},{8,4},{9,5},{1... | collective-permute-start | bytes 1179656 | tf_op jit(solution)/shard_map/while/body/eval_jaxpr/ppermute | solution.py:66
  47.9 15.5 %collective-permute-start.6 = (bf16[4,384,128]{2,1,0:T(8,128)(2,1)S(1)}, bf16[4,384,128]{2,1,0:T(8,128)(2,1)S(1)}, u32[]{:S(2)}, u32[]{:S(2)}) collective-permute-start(bf16[4,384,128]{2,1,0:T(8,128)(2,1)S(1)} %constant_dynamic-update-slice_fusion.5.refs_1_), channel_id=1, source_target_pairs={{0,4},{1,5},{2,6},{3,7},{4,8},{5,9},{6,10},{7,11},{8,12},{9,13},{1... | collective-permute-start | bytes 1179656 | tf_op jit(solution)/shard_map/while/body/eval_jaxpr/ppermute | solution.py:66
  49.4 5.7 %collective-permute-start.22 = (bf16[2,384,128]{2,1,0:T(8,128)(2,1)S(1)}, bf16[2,384,128]{2,1,0:T(8,128)(2,1)S(1)}, u32[]{:S(2)}, u32[]{:S(2)}) collective-permute-start(bf16[2,384,128]{2,1,0:T(8,128)(2,1)S(1)} %collective-permute-done.21.refs_23_), channel_id=1, source_target_pairs={{0,112},{1,113},{2,114},{3,115},{4,116},{5,117},{6,118},{7,119},{8... | collective-permute-start | bytes 589832 | tf_op jit(solution)/shard_map/while/body/eval_jaxpr/ppermute | solution.py:66
  50.4 7.6 %collective-permute-start.17 = (bf16[2,384,128]{2,1,0:T(8,128)(2,1)S(1)}, bf16[2,384,128]{2,1,0:T(8,128)(2,1)}, u32[]{:S(2)}, u32[]{:S(2)}) collective-permute-start(bf16[2,384,128]{2,1,0:T(8,128)(2,1)S(1)} %collective-permute-done.15.refs_11_), channel_id=1, source_target_pairs={{0,16},{1,17},{2,18},{3,19},{4,20},{5,21},{6,22},{7,23},{8,24},{9,... | collective-permute-start | bytes 589832 | tf_op jit(solution)/shard_map/while/body/eval_jaxpr/ppermute | solution.py:66
  51.4 8.6 %collective-permute-start.18 = (bf16[2,384,128]{2,1,0:T(8,128)(2,1)S(1)}, bf16[2,384,128]{2,1,0:T(8,128)(2,1)}, u32[]{:S(2)}, u32[]{:S(2)}) collective-permute-start(bf16[2,384,128]{2,1,0:T(8,128)(2,1)S(1)} %collective-permute-done.16.refs_12_), channel_id=1, source_target_pairs={{0,16},{1,17},{2,18},{3,19},{4,20},{5,21},{6,22},{7,23},{8,24},{9,... | collective-permute-start | bytes 589832 | tf_op jit(solution)/shard_map/while/body/eval_jaxpr/ppermute | solution.py:66
  55.1 6.9 %collective-permute-start.27 = (bf16[2,384,128]{2,1,0:T(8,128)(2,1)S(1)}, bf16[2,384,128]{2,1,0:T(8,128)(2,1)S(1)}, u32[]{:S(2)}, u32[]{:S(2)}) collective-permute-start(bf16[2,384,128]{2,1,0:T(8,128)(2,1)S(1)} %collective-permute-done.26.refs_20_), channel_id=1, source_target_pairs={{0,112},{1,113},{2,114},{3,115},{4,116},{5,117},{6,118},{7,119},{8... | collective-permute-start | bytes 589832 | tf_op jit(solution)/shard_map/while/body/eval_jaxpr/ppermute | solution.py:66
  58.0 13.9 %collective-permute-start.7 = (bf16[4,384,128]{2,1,0:T(8,128)(2,1)S(1)}, bf16[4,384,128]{2,1,0:T(8,128)(2,1)S(1)}, u32[]{:S(2)}, u32[]{:S(2)}) collective-permute-start(bf16[4,384,128]{2,1,0:T(8,128)(2,1)S(1)} %collective-permute-done.5.refs_2_), channel_id=1, source_target_pairs={{0,4},{1,5},{2,6},{3,7},{4,8},{5,9},{6,10},{7,11},{8,12},{9,13},{1... | collective-permute-start | bytes 1179656 | tf_op jit(solution)/shard_map/while/body/eval_jaxpr/ppermute | solution.py:66
  60.1 5.8 %collective-permute-start.23 = (bf16[2,384,128]{2,1,0:T(8,128)(2,1)S(1)}, bf16[2,384,128]{2,1,0:T(8,128)(2,1)}, u32[]{:S(2)}, u32[]{:S(2)}) collective-permute-start(bf16[2,384,128]{2,1,0:T(8,128)(2,1)S(1)} %collective-permute-done.22.refs_21_), channel_id=1, source_target_pairs={{0,112},{1,113},{2,114},{3,115},{4,116},{5,117},{6,118},{7,119},{8... | collective-permute-start | bytes 589832 | tf_op jit(solution)/shard_map/while/body/eval_jaxpr/ppermute | solution.py:66
  61.6 11.8 %collective-permute-start.9 = (bf16[4,384,128]{2,1,0:T(8,128)(2,1)S(1)}, bf16[4,384,128]{2,1,0:T(8,128)(2,1)S(1)}, u32[]{:S(2)}, u32[]{:S(2)}) collective-permute-start(bf16[4,384,128]{2,1,0:T(8,128)(2,1)S(1)} %collective-permute-done.8.refs_7_), channel_id=1, source_target_pairs={{0,12},{1,13},{2,14},{3,15},{4,0},{5,1},{6,2},{7,3},{8,4},{9,5},{1... | collective-permute-start | bytes 1179656 | tf_op jit(solution)/shard_map/while/body/eval_jaxpr/ppermute | solution.py:66
  62.0 7.7 %collective-permute-start.19 = (bf16[2,384,128]{2,1,0:T(8,128)(2,1)}, bf16[2,384,128]{2,1,0:T(8,128)(2,1)}, u32[]{:S(2)}, u32[]{:S(2)}) collective-permute-start(bf16[2,384,128]{2,1,0:T(8,128)(2,1)} %collective-permute-done.17.refs_13_), channel_id=1, source_target_pairs={{0,16},{1,17},{2,18},{3,19},{4,20},{5,21},{6,22},{7,23},{8,24},{9,... | collective-permute-start | bytes 589832 | tf_op jit(solution)/shard_map/while/body/eval_jaxpr/ppermute | solution.py:66
  63.4 8.4 %collective-permute-start.20 = (bf16[2,384,128]{2,1,0:T(8,128)(2,1)}, bf16[2,384,128]{2,1,0:T(8,128)(2,1)}, u32[]{:S(2)}, u32[]{:S(2)}) collective-permute-start(bf16[2,384,128]{2,1,0:T(8,128)(2,1)} %collective-permute-done.18.refs_14_), channel_id=1, source_target_pairs={{0,16},{1,17},{2,18},{3,19},{4,20},{5,21},{6,22},{7,23},{8,24},{9,... | collective-permute-start | bytes 589832 | tf_op jit(solution)/shard_map/while/body/eval_jaxpr/ppermute | solution.py:66
  65.9 7.5 %collective-permute-start.24 = (bf16[2,384,128]{2,1,0:T(8,128)(2,1)}, bf16[2,384,128]{2,1,0:T(8,128)(2,1)}, u32[]{:S(2)}, u32[]{:S(2)}) collective-permute-start(bf16[2,384,128]{2,1,0:T(8,128)(2,1)} %collective-permute-done.23.refs_19_), channel_id=1, source_target_pairs={{0,112},{1,113},{2,114},{3,115},{4,116},{5,117},{6,118},{7,119},{8... | collective-permute-start | bytes 589832 | tf_op jit(solution)/shard_map/while/body/eval_jaxpr/ppermute | solution.py:66
  83.6 5.8 %collective-permute-start.28 = (f32[384,128]{1,0:T(8,128)}, f32[384,128]{1,0:T(8,128)S(1)}, u32[]{:S(2)}, u32[]{:S(2)}) collective-permute-start(f32[384,128]{1,0:T(8,128)} %get-tuple-element.601), channel_id=1, source_target_pairs={{0,1},{1,0},{2,3},{3,2},{4,5},{5,4},{6,7},{7,6},{8,9},{9,8},{10,11... | collective-permute-start | bytes 589832 | tf_op jit(solution)/shard_map/while/body/eval_jaxpr/ppermute | solution.py:66
  83.7 9.1 %collective-permute-start.29 = (f32[384,128]{1,0:T(8,128)}, f32[384,128]{1,0:T(8,128)S(1)}, u32[]{:S(2)}, u32[]{:S(2)}) collective-permute-start(f32[384,128]{1,0:T(8,128)} %get-tuple-element.602), channel_id=1, source_target_pairs={{0,2},{1,3},{2,0},{3,1},{4,6},{5,7},{6,4},{7,5},{8,10},{9,11},{10,... | collective-permute-start | bytes 589832 | tf_op jit(solution)/shard_map/while/body/eval_jaxpr/ppermute | solution.py:66
  86.8 9.6 %collective-permute-start.30 = (f32[384,128]{1,0:T(8,128)}, f32[384,128]{1,0:T(8,128)S(1)}, u32[]{:S(2)}, u32[]{:S(2)}) collective-permute-start(f32[384,128]{1,0:T(8,128)} %get-tuple-element.604), channel_id=1, source_target_pairs={{0,3},{1,2},{2,1},{3,0},{4,7},{5,6},{6,5},{7,4},{8,11},{9,10},{10,... | collective-permute-start | bytes 589832 | tf_op jit(solution)/shard_map/while/body/eval_jaxpr/ppermute | solution.py:66
  98.2 11.8 %collective-permute-start = (bf16[384,128]{1,0:T(8,128)(2,1)S(1)}, bf16[384,128]{1,0:T(8,128)(2,1)S(1)}, u32[]{:S(2)}, u32[]{:S(2)}) collective-permute-start(bf16[384,128]{1,0:T(8,128)(2,1)S(1)} %get-tuple-element.621), channel_id=1, source_target_pairs={{0,32},{1,48},{2,160},{3,176},{4,36},{5,52},{6,164},{7,180},{8,40}... | collective-permute-start | bytes 294920 | tf_op jit(solution)/shard_map/while/body/eval_jaxpr/ppermute | solution.py:66
  98.3 11.7 %collective-permute-start.1 = (bf16[384,128]{1,0:T(8,128)(2,1)S(1)}, bf16[384,128]{1,0:T(8,128)(2,1)S(1)}, u32[]{:S(2)}, u32[]{:S(2)}) collective-permute-start(bf16[384,128]{1,0:T(8,128)(2,1)S(1)} %get-tuple-element.621), channel_id=1, source_target_pairs={{0,96},{1,112},{2,224},{3,240},{4,100},{5,116},{6,228},{7,244},{8,... | collective-permute-start | bytes 294920 | tf_op jit(solution)/shard_map/while/body/eval_jaxpr/ppermute | solution.py:66
  103.7 9.5 %collective-permute-start.11 = (bf16[384,128]{1,0:T(8,128)(2,1)S(1)}, bf16[384,128]{1,0:T(8,128)(2,1)S(1)}, u32[]{:S(2)}, u32[]{:S(2)}) collective-permute-start(bf16[384,128]{1,0:T(8,128)(2,1)S(1)} %get-tuple-element.621), channel_id=1, source_target_pairs={{0,232},{1,248},{2,104},{3,120},{4,236},{5,252},{6,108},{7,124},{8... | collective-permute-start | bytes 294920 | tf_op jit(solution)/shard_map/while/body/eval_jaxpr/ppermute | solution.py:66
  110.0 6.0 %collective-permute-start.12 = (bf16[384,128]{1,0:T(8,128)(2,1)S(1)}, bf16[384,128]{1,0:T(8,128)(2,1)S(1)}, u32[]{:S(2)}, u32[]{:S(2)}) collective-permute-start(bf16[384,128]{1,0:T(8,128)(2,1)S(1)} %get-tuple-element.621), channel_id=1, source_target_pairs={{0,224},{1,240},{2,96},{3,112},{4,228},{5,244},{6,100},{7,116},{8,... | collective-permute-start | bytes 294920 | tf_op jit(solution)/shard_map/while/body/eval_jaxpr/ppermute | solution.py:66
  110.0 11.4 %collective-permute-start.2 = (bf16[2,384,128]{2,1,0:T(8,128)(2,1)S(1)}, bf16[2,384,128]{2,1,0:T(8,128)(2,1)S(1)}, u32[]{:S(2)}, u32[]{:S(2)}) collective-permute-start(bf16[2,384,128]{2,1,0:T(8,128)(2,1)S(1)} %pad_maximum_fusion.8), channel_id=1, source_target_pairs={{0,16},{1,17},{2,18},{3,19},{4,20},{5,21},{6,22},{7,23},{8,24},{9,... | collective-permute-start | bytes 589832 | tf_op jit(solution)/shard_map/while/body/eval_jaxpr/ppermute | solution.py:66
  115.9 51.1 %copy-start.2 = (bf16[2,384,128]{2,1,0:T(8,128)(2,1)}, bf16[2,384,128]{2,1,0:T(8,128)(2,1)S(1)}, u32[]{:S(2)}) copy-start(bf16[2,384,128]{2,1,0:T(8,128)(2,1)S(1)} %pad_maximum_fusion.10.refs_8_) | copy-start | bytes 589828 | tf_op jit(solution)/shard_map/while
  116.0 7.1 %collective-permute-start.13 = (bf16[2,384,128]{2,1,0:T(8,128)(2,1)S(1)}, bf16[2,384,128]{2,1,0:T(8,128)(2,1)S(1)}, u32[]{:S(2)}, u32[]{:S(2)}) collective-permute-start(bf16[2,384,128]{2,1,0:T(8,128)(2,1)S(1)} %pad_maximum_fusion.10.refs_8_), channel_id=1, source_target_pairs={{0,4},{1,5},{2,6},{3,7},{4,8},{5,9},{6,10},{7,11},{8,12},{9,13},{1... | collective-permute-start | bytes 589832 | tf_op jit(solution)/shard_map/while/body/eval_jaxpr/ppermute | solution.py:66
  116.0 8.7 %collective-permute-start.3 = (bf16[2,384,128]{2,1,0:T(8,128)(2,1)S(1)}, bf16[2,384,128]{2,1,0:T(8,128)(2,1)S(1)}, u32[]{:S(2)}, u32[]{:S(2)}) collective-permute-start(bf16[2,384,128]{2,1,0:T(8,128)(2,1)S(1)} %pad_maximum_fusion.8), channel_id=1, source_target_pairs={{0,112},{1,113},{2,114},{3,115},{4,116},{5,117},{6,118},{7,119},{8... | collective-permute-start | bytes 589832 | tf_op jit(solution)/shard_map/while/body/eval_jaxpr/ppermute | solution.py:66
  118.2 8.6 %collective-permute-start.14 = (bf16[2,384,128]{2,1,0:T(8,128)(2,1)S(1)}, bf16[2,384,128]{2,1,0:T(8,128)(2,1)S(1)}, u32[]{:S(2)}, u32[]{:S(2)}) collective-permute-start(bf16[2,384,128]{2,1,0:T(8,128)(2,1)S(1)} %pad_maximum_fusion.10.refs_8_), channel_id=1, source_target_pairs={{0,16},{1,17},{2,18},{3,19},{4,20},{5,21},{6,22},{7,23},{8,24},{9,... | collective-permute-start | bytes 589832 | tf_op jit(solution)/shard_map/while/body/eval_jaxpr/ppermute | solution.py:66
  118.2 9.9 %collective-permute-start.25 = (bf16[2,384,128]{2,1,0:T(8,128)(2,1)S(1)}, bf16[2,384,128]{2,1,0:T(8,128)(2,1)S(1)}, u32[]{:S(2)}, u32[]{:S(2)}) collective-permute-start(bf16[2,384,128]{2,1,0:T(8,128)(2,1)S(1)} %pad_maximum_fusion.10.refs_8_), channel_id=1, source_target_pairs={{0,112},{1,113},{2,114},{3,115},{4,116},{5,117},{6,118},{7,119},{8... | collective-permute-start | bytes 589832 | tf_op jit(solution)/shard_map/while/body/eval_jaxpr/ppermute | solution.py:66
  121.4 8.0 %collective-permute-start.4 = (bf16[2,384,128]{2,1,0:T(8,128)(2,1)S(1)}, bf16[2,384,128]{2,1,0:T(8,128)(2,1)S(1)}, u32[]{:S(2)}, u32[]{:S(2)}) collective-permute-start(bf16[2,384,128]{2,1,0:T(8,128)(2,1)S(1)} %collective-permute-done.2), channel_id=1, source_target_pairs={{0,16},{1,17},{2,18},{3,19},{4,20},{5,21},{6,22},{7,23},{8,24},{9,... | collective-permute-start | bytes 589832 | tf_op jit(solution)/shard_map/while/body/eval_jaxpr/ppermute | solution.py:66
  123.0 9.3 %collective-permute-start.21 = (bf16[2,384,128]{2,1,0:T(8,128)(2,1)S(1)}, bf16[2,384,128]{2,1,0:T(8,128)(2,1)S(1)}, u32[]{:S(2)}, u32[]{:S(2)}) collective-permute-start(bf16[2,384,128]{2,1,0:T(8,128)(2,1)S(1)} %collective-permute-done.13.refs_9_), channel_id=1, source_target_pairs={{0,112},{1,113},{2,114},{3,115},{4,116},{5,117},{6,118},{7,119},{8... | collective-permute-start | bytes 589832 | tf_op jit(solution)/shard_map/while/body/eval_jaxpr/ppermute | solution.py:66
  124.7 18.5 %collective-permute-start.5 = (bf16[4,384,128]{2,1,0:T(8,128)(2,1)S(1)}, bf16[4,384,128]{2,1,0:T(8,128)(2,1)S(1)}, u32[]{:S(2)}, u32[]{:S(2)}) collective-permute-start(bf16[4,384,128]{2,1,0:T(8,128)(2,1)S(1)} %pad_maximum_fusion.9.refs_0_), channel_id=1, source_target_pairs={{0,4},{1,5},{2,6},{3,7},{4,8},{5,9},{6,10},{7,11},{8,12},{9,13},{1... | collective-permute-start | bytes 1179656 | tf_op jit(solution)/shard_map/while/body/eval_jaxpr/ppermute | solution.py:66
  126.7 18.4 %collective-permute-start.10 = (bf16[4,384,128]{2,1,0:T(8,128)(2,1)S(1)}, bf16[4,384,128]{2,1,0:T(8,128)(2,1)S(1)}, u32[]{:S(2)}, u32[]{:S(2)}) collective-permute-start(bf16[4,384,128]{2,1,0:T(8,128)(2,1)S(1)} %pad_maximum_fusion.9.refs_0_), channel_id=1, source_target_pairs={{0,12},{1,13},{2,14},{3,15},{4,0},{5,1},{6,2},{7,3},{8,4},{9,5},{1... | collective-permute-start | bytes 1179656 | tf_op jit(solution)/shard_map/while/body/eval_jaxpr/ppermute | solution.py:66
  128.1 9.0 %collective-permute-start.15 = (bf16[2,384,128]{2,1,0:T(8,128)(2,1)S(1)}, bf16[2,384,128]{2,1,0:T(8,128)(2,1)S(1)}, u32[]{:S(2)}, u32[]{:S(2)}) collective-permute-start(bf16[2,384,128]{2,1,0:T(8,128)(2,1)S(1)} %collective-permute-done.13.refs_9_), channel_id=1, source_target_pairs={{0,16},{1,17},{2,18},{3,19},{4,20},{5,21},{6,22},{7,23},{8,24},{9,... | collective-permute-start | bytes 589832 | tf_op jit(solution)/shard_map/while/body/eval_jaxpr/ppermute | solution.py:66
  129.4 11.0 %collective-permute-start.16 = (bf16[2,384,128]{2,1,0:T(8,128)(2,1)S(1)}, bf16[2,384,128]{2,1,0:T(8,128)(2,1)S(1)}, u32[]{:S(2)}, u32[]{:S(2)}) collective-permute-start(bf16[2,384,128]{2,1,0:T(8,128)(2,1)S(1)} %collective-permute-done.14.refs_10_), channel_id=1, source_target_pairs={{0,16},{1,17},{2,18},{3,19},{4,20},{5,21},{6,22},{7,23},{8,24},{9,... | collective-permute-start | bytes 589832 | tf_op jit(solution)/shard_map/while/body/eval_jaxpr/ppermute | solution.py:66
  132.3 10.8 %collective-permute-start.26 = (bf16[2,384,128]{2,1,0:T(8,128)(2,1)S(1)}, bf16[2,384,128]{2,1,0:T(8,128)(2,1)S(1)}, u32[]{:S(2)}, u32[]{:S(2)}) collective-permute-start(bf16[2,384,128]{2,1,0:T(8,128)(2,1)S(1)} %collective-permute-done.25.refs_22_), channel_id=1, source_target_pairs={{0,112},{1,113},{2,114},{3,115},{4,116},{5,117},{6,118},{7,119},{8... | collective-permute-start | bytes 589832 | tf_op jit(solution)/shard_map/while/body/eval_jaxpr/ppermute | solution.py:66
  137.1 18.2 %collective-permute-start.8 = (bf16[4,384,128]{2,1,0:T(8,128)(2,1)S(1)}, bf16[4,384,128]{2,1,0:T(8,128)(2,1)S(1)}, u32[]{:S(2)}, u32[]{:S(2)}) collective-permute-start(bf16[4,384,128]{2,1,0:T(8,128)(2,1)S(1)} %constant_dynamic-update-slice_fusion.5.refs_1_), channel_id=1, source_target_pairs={{0,12},{1,13},{2,14},{3,15},{4,0},{5,1},{6,2},{7,3},{8,4},{9,5},{1... | collective-permute-start | bytes 1179656 | tf_op jit(solution)/shard_map/while/body/eval_jaxpr/ppermute | solution.py:66
  140.5 17.0 %collective-permute-start.6 = (bf16[4,384,128]{2,1,0:T(8,128)(2,1)S(1)}, bf16[4,384,128]{2,1,0:T(8,128)(2,1)S(1)}, u32[]{:S(2)}, u32[]{:S(2)}) collective-permute-start(bf16[4,384,128]{2,1,0:T(8,128)(2,1)S(1)} %constant_dynamic-update-slice_fusion.5.refs_1_), channel_id=1, source_target_pairs={{0,4},{1,5},{2,6},{3,7},{4,8},{5,9},{6,10},{7,11},{8,12},{9,13},{1... | collective-permute-start | bytes 1179656 | tf_op jit(solution)/shard_map/while/body/eval_jaxpr/ppermute | solution.py:66
  143.1 6.5 %collective-permute-start.22 = (bf16[2,384,128]{2,1,0:T(8,128)(2,1)S(1)}, bf16[2,384,128]{2,1,0:T(8,128)(2,1)S(1)}, u32[]{:S(2)}, u32[]{:S(2)}) collective-permute-start(bf16[2,384,128]{2,1,0:T(8,128)(2,1)S(1)} %collective-permute-done.21.refs_23_), channel_id=1, source_target_pairs={{0,112},{1,113},{2,114},{3,115},{4,116},{5,117},{6,118},{7,119},{8... | collective-permute-start | bytes 589832 | tf_op jit(solution)/shard_map/while/body/eval_jaxpr/ppermute | solution.py:66
  143.2 9.1 %collective-permute-start.17 = (bf16[2,384,128]{2,1,0:T(8,128)(2,1)S(1)}, bf16[2,384,128]{2,1,0:T(8,128)(2,1)}, u32[]{:S(2)}, u32[]{:S(2)}) collective-permute-start(bf16[2,384,128]{2,1,0:T(8,128)(2,1)S(1)} %collective-permute-done.15.refs_11_), channel_id=1, source_target_pairs={{0,16},{1,17},{2,18},{3,19},{4,20},{5,21},{6,22},{7,23},{8,24},{9,... | collective-permute-start | bytes 589832 | tf_op jit(solution)/shard_map/while/body/eval_jaxpr/ppermute | solution.py:66
  145.2 10.1 %collective-permute-start.18 = (bf16[2,384,128]{2,1,0:T(8,128)(2,1)S(1)}, bf16[2,384,128]{2,1,0:T(8,128)(2,1)}, u32[]{:S(2)}, u32[]{:S(2)}) collective-permute-start(bf16[2,384,128]{2,1,0:T(8,128)(2,1)S(1)} %collective-permute-done.16.refs_12_), channel_id=1, source_target_pairs={{0,16},{1,17},{2,18},{3,19},{4,20},{5,21},{6,22},{7,23},{8,24},{9,... | collective-permute-start | bytes 589832 | tf_op jit(solution)/shard_map/while/body/eval_jaxpr/ppermute | solution.py:66
  149.7 5.9 %collective-permute-start.27 = (bf16[2,384,128]{2,1,0:T(8,128)(2,1)S(1)}, bf16[2,384,128]{2,1,0:T(8,128)(2,1)S(1)}, u32[]{:S(2)}, u32[]{:S(2)}) collective-permute-start(bf16[2,384,128]{2,1,0:T(8,128)(2,1)S(1)} %collective-permute-done.26.refs_20_), channel_id=1, source_target_pairs={{0,112},{1,113},{2,114},{3,115},{4,116},{5,117},{6,118},{7,119},{8... | collective-permute-start | bytes 589832 | tf_op jit(solution)/shard_map/while/body/eval_jaxpr/ppermute | solution.py:66
  152.3 14.6 %collective-permute-start.7 = (bf16[4,384,128]{2,1,0:T(8,128)(2,1)S(1)}, bf16[4,384,128]{2,1,0:T(8,128)(2,1)S(1)}, u32[]{:S(2)}, u32[]{:S(2)}) collective-permute-start(bf16[4,384,128]{2,1,0:T(8,128)(2,1)S(1)} %collective-permute-done.5.refs_2_), channel_id=1, source_target_pairs={{0,4},{1,5},{2,6},{3,7},{4,8},{5,9},{6,10},{7,11},{8,12},{9,13},{1... | collective-permute-start | bytes 1179656 | tf_op jit(solution)/shard_map/while/body/eval_jaxpr/ppermute | solution.py:66
  155.3 5.8 %collective-permute-start.23 = (bf16[2,384,128]{2,1,0:T(8,128)(2,1)S(1)}, bf16[2,384,128]{2,1,0:T(8,128)(2,1)}, u32[]{:S(2)}, u32[]{:S(2)}) collective-permute-start(bf16[2,384,128]{2,1,0:T(8,128)(2,1)S(1)} %collective-permute-done.22.refs_21_), channel_id=1, source_target_pairs={{0,112},{1,113},{2,114},{3,115},{4,116},{5,117},{6,118},{7,119},{8... | collective-permute-start | bytes 589832 | tf_op jit(solution)/shard_map/while/body/eval_jaxpr/ppermute | solution.py:66
  155.3 11.8 %collective-permute-start.9 = (bf16[4,384,128]{2,1,0:T(8,128)(2,1)S(1)}, bf16[4,384,128]{2,1,0:T(8,128)(2,1)S(1)}, u32[]{:S(2)}, u32[]{:S(2)}) collective-permute-start(bf16[4,384,128]{2,1,0:T(8,128)(2,1)S(1)} %collective-permute-done.8.refs_7_), channel_id=1, source_target_pairs={{0,12},{1,13},{2,14},{3,15},{4,0},{5,1},{6,2},{7,3},{8,4},{9,5},{1... | collective-permute-start | bytes 1179656 | tf_op jit(solution)/shard_map/while/body/eval_jaxpr/ppermute | solution.py:66
  155.5 9.3 %collective-permute-start.19 = (bf16[2,384,128]{2,1,0:T(8,128)(2,1)}, bf16[2,384,128]{2,1,0:T(8,128)(2,1)}, u32[]{:S(2)}, u32[]{:S(2)}) collective-permute-start(bf16[2,384,128]{2,1,0:T(8,128)(2,1)} %collective-permute-done.17.refs_13_), channel_id=1, source_target_pairs={{0,16},{1,17},{2,18},{3,19},{4,20},{5,21},{6,22},{7,23},{8,24},{9,... | collective-permute-start | bytes 589832 | tf_op jit(solution)/shard_map/while/body/eval_jaxpr/ppermute | solution.py:66
  157.5 9.4 %collective-permute-start.20 = (bf16[2,384,128]{2,1,0:T(8,128)(2,1)}, bf16[2,384,128]{2,1,0:T(8,128)(2,1)}, u32[]{:S(2)}, u32[]{:S(2)}) collective-permute-start(bf16[2,384,128]{2,1,0:T(8,128)(2,1)} %collective-permute-done.18.refs_14_), channel_id=1, source_target_pairs={{0,16},{1,17},{2,18},{3,19},{4,20},{5,21},{6,22},{7,23},{8,24},{9,... | collective-permute-start | bytes 589832 | tf_op jit(solution)/shard_map/while/body/eval_jaxpr/ppermute | solution.py:66
  161.1 6.0 %collective-permute-start.24 = (bf16[2,384,128]{2,1,0:T(8,128)(2,1)}, bf16[2,384,128]{2,1,0:T(8,128)(2,1)}, u32[]{:S(2)}, u32[]{:S(2)}) collective-permute-start(bf16[2,384,128]{2,1,0:T(8,128)(2,1)} %collective-permute-done.23.refs_19_), channel_id=1, source_target_pairs={{0,112},{1,113},{2,114},{3,115},{4,116},{5,117},{6,118},{7,119},{8... | collective-permute-start | bytes 589832 | tf_op jit(solution)/shard_map/while/body/eval_jaxpr/ppermute | solution.py:66
  177.2 4.5 %collective-permute-start.28 = (f32[384,128]{1,0:T(8,128)}, f32[384,128]{1,0:T(8,128)S(1)}, u32[]{:S(2)}, u32[]{:S(2)}) collective-permute-start(f32[384,128]{1,0:T(8,128)} %get-tuple-element.601), channel_id=1, source_target_pairs={{0,1},{1,0},{2,3},{3,2},{4,5},{5,4},{6,7},{7,6},{8,9},{9,8},{10,11... | collective-permute-start | bytes 589832 | tf_op jit(solution)/shard_map/while/body/eval_jaxpr/ppermute | solution.py:66
  177.3 8.1 %collective-permute-start.29 = (f32[384,128]{1,0:T(8,128)}, f32[384,128]{1,0:T(8,128)S(1)}, u32[]{:S(2)}, u32[]{:S(2)}) collective-permute-start(f32[384,128]{1,0:T(8,128)} %get-tuple-element.602), channel_id=1, source_target_pairs={{0,2},{1,3},{2,0},{3,1},{4,6},{5,7},{6,4},{7,5},{8,10},{9,11},{10,... | collective-permute-start | bytes 589832 | tf_op jit(solution)/shard_map/while/body/eval_jaxpr/ppermute | solution.py:66
  177.4 11.1 %collective-permute-start.30 = (f32[384,128]{1,0:T(8,128)}, f32[384,128]{1,0:T(8,128)S(1)}, u32[]{:S(2)}, u32[]{:S(2)}) collective-permute-start(f32[384,128]{1,0:T(8,128)} %get-tuple-element.604), channel_id=1, source_target_pairs={{0,3},{1,2},{2,1},{3,0},{4,7},{5,6},{6,5},{7,4},{8,11},{9,10},{10,... | collective-permute-start | bytes 589832 | tf_op jit(solution)/shard_map/while/body/eval_jaxpr/ppermute | solution.py:66
  (35 other events, 702.6 us)
where the time goes:
time: 195 us; the launch traced here: 192 us
  starting transfers between devices  96.9 us (50%)
  waiting for transfers between devices  59 us (30%)
  Pallas kernels  18.9 us (10%)
  local copies, waits for them, and re-layouts  10 us (5%)
  other arithmetic  4.88 us (3%)
    ppermute x62, starting transfers between devices, send(): return lax.ppermute(value, BOTH, perm)  96.9 us
    ppermute x62, waiting for transfers between devices, send(): return lax.ppermute(value, BOTH, perm)  59 us
    pallas_call x2, Pallas kernels, product(): pl.pallas_call(product_kernel, out_shape=[tile] * 4, in_specs=[pl.BlockSp...  18.9 us
  transfers between devices with their start and end apart: 62, of which 32 were waited for; matrix products, arithmetic and copies ran while one was open for 4% of the time, Pallas kernels for 0%

commit v1 on v0

v1 whole, which is shorter than its diff:
```python
import functools

import jax
import jax.numpy as jnp
from jax import lax
from jax.experimental import pallas as pl
from jax.experimental.pallas import tpu as pltpu
from jax.sharding import PartitionSpec as P


INTERPRET = False
VMEM = 58 * 1024 * 1024
BOTH = ("blk", "grp")


def solve_blocks(inverse, resid):
    width = inverse.shape[1]
    count = inverse.shape[0] // width
    blocks = inverse.reshape(count, width, width)
    parts = resid.reshape(count, width, resid.shape[1])
    value = jnp.einsum(
        "nab,nbc->nac",
        blocks,
        parts,
        precision=lax.Precision.HIGHEST,
        preferred_element_type=jnp.float32,
    )
    return value.reshape(resid.shape)


def pairs(move):
    out = []
    for yh in range(2):
        for z in range(8):
            for x in range(4):
                for yl in range(2):
                    for c in range(2):
                        a, b, d, e, f = move(yh, z, x, yl, c)
                        out.append((((yh * 8 + z) * 4 + x) * 4 + yl * 2 + c, ((a * 8 + b) * 4 + d) * 4 + e * 2 + f))
    return out


def swap(flip, dz, dx):
    def move(yh, z, x, yl, c):
        zh, zl = z // 4, z % 4
        return yl ^ flip, (2 * zl + c + 6 + 4 * zh + dz) % 8, (x + dx) % 4, yh, zh

    return pairs(move)


def along_z(k):
    return pairs(lambda yh, z, x, yl, c: (yh, (z + k) % 8, x, yl, c))


def along_x(k):
    return pairs(lambda yh, z, x, yl, c: (yh, z, (x + k) % 4, yl, c))


def home(k):
    def move(yh, z, x, yl, c):
        g = (yl * 2 + c) ^ k
        return yh, z, x, g // 2, g % 2

    return pairs(move)


def send(value, perm):
    return lax.ppermute(value, BOTH, perm)


LOW, HIGH = (0, 4, 1, 5), (7, 3, 2, 6)
EVEN, ODD = (0, 2), (1, 3)


def product_kernel(place, sweep, factors, *refs, home_half):
    za, zb, outs = refs[0:8], refs[8:24], refs[24:26]
    acc, factor, whole, sem = refs[26:30]
    n = acc.shape[2]
    cols = factor.shape[1]
    step = cols // 16
    layer, z, x, yh, grp = sweep[0], place[0], place[1], place[2], place[3]
    core = lax.rem(grp, 2)
    wanted = lax.div(grp, 2) if home_half else 1 - lax.div(grp, 2)

    def turn(k):
        return lax.rem(z - k + 10 + 4 * core, 8)

    def visit(v):
        return lax.rem(lax.div(turn(0), 2) + jnp.where(v == 1, 3, jnp.where(v == 0, 0, v - 1)), 4)

    def fetch(v):
        at = pl.ds(pl.multiple_of(visit(v) * (4 * step), 4 * step), 4 * step)
        return pltpu.make_async_copy(factors.at[layer, :, at], factor.at[:, at], sem.at[4 + v])

    def piece(ref, k, j):
        e = turn(k)
        at = pl.multiple_of(lax.rem(x - j + 4, 4) * step, step)
        lane = pl.multiple_of(lax.rem(e, 2) * n, n)
        target = whole.at[lax.div(e, 2), pl.ds(at, step), pl.ds(lane, n)]
        pltpu.make_async_copy(ref, target, sem.at[lax.div(e, 2)]).start()

    fetch(0).start()
    order = (0, 1, 7, 2, 6, 3, 5, 4)

    @pl.when(wanted == yh)
    def _():
        for k in order:
            t, ks = (0, LOW) if k in LOW else (1, HIGH)
            for j in range(4):
                piece(za[2 * j + t].at[ks.index(k)], k, j)

    @pl.when(wanted != yh)
    def _():
        for k in order:
            for t, js in enumerate((EVEN, ODD)):
                for i, j in enumerate(js):
                    piece(zb[2 * k + t].at[i], k, j)

    for v in range(1, 4):
        fetch(v).start()

    def multiply(v, value):
        zl = visit(v)
        fetch(v).wait()
        pltpu.make_async_copy(whole.at[zl], whole.at[zl], sem.at[zl]).wait()
        at = pl.multiple_of(zl * (4 * step), 4 * step)
        return value + jnp.dot(factor[:, pl.ds(at, 4 * step)], whole[zl], preferred_element_type=jnp.float32)

    value = lax.fori_loop(0, 4, multiply, jnp.zeros((factor.shape[0], 2 * n), jnp.float32))
    for s in range(2):
        acc[s] = value[:, s * n : (s + 1) * n]
    outs[0][...] = acc[core]
    outs[1][...] = acc[1 - core]


def product(place, layer, factors, za, zb, home_half):
    _, rows, cols = factors.shape
    n = za[0].shape[2]
    anywhere = pl.BlockSpec(memory_space=pl.ANY)
    vmem = pl.BlockSpec(memory_space=pltpu.VMEM)
    tile = jax.ShapeDtypeStruct((rows, n), jnp.float32)
    return pl.pallas_call(
        functools.partial(product_kernel, home_half=home_half),
        out_shape=[tile] * 2,
        in_specs=[pl.BlockSpec(memory_space=pltpu.SMEM)] * 2 + [anywhere] * (1 + len(za) + len(zb)),
        out_specs=[vmem] * 2,
        scratch_shapes=[
            pltpu.VMEM((2, rows, n), jnp.float32),
            pltpu.VMEM((rows, cols), jnp.bfloat16),
            pltpu.VMEM((4, cols // 4, 2 * n), jnp.bfloat16),
            pltpu.SemaphoreType.DMA((8,)),
        ],
        compiler_params=pltpu.CompilerParams(vmem_limit_bytes=VMEM),
        interpret=INTERPRET,
    )(place, layer.reshape(1), factors, *za, *zb)


def coupling_of(place, layer, factors, piece):
    two = jnp.stack([send(piece, swap(1, 0, 0)), send(piece, swap(1, 0, 2))])
    one = jnp.stack([send(piece, swap(0, 0, 0)), send(piece, swap(0, 4, 0))])
    even, odd = [two] + [None] * 7, [send(two, along_x(1))] + [None] * 7
    for k in range(1, 4):
        for rows in (even, odd):
            rows[k] = send(rows[k - 1], along_z(1))
            rows[8 - k] = send(rows[(9 - k) % 8], along_z(7))
    even[4] = send(even[3], along_z(1))
    odd[4] = send(odd[5], along_z(7))
    up, down = send(one, along_z(1)), send(one, along_z(7))
    up2 = send(up, along_z(1))
    low, high = jnp.concatenate([one, up]), jnp.concatenate([down, up2])
    low1, low3 = send(low, along_x(1)), send(low, along_x(3))
    high1, high3 = send(high, along_x(1)), send(high, along_x(3))
    low2 = send(low1, along_x(1))
    high2 = send(high3, along_x(3))
    za = [low, high, low1, high1, low2, high2, low3, high3]
    zb = [row for pair in zip(even, odd) for row in pair]
    away, beyond = product(place, layer, factors, za, zb, False)
    beyond, away = send(beyond, home(3)), send(away, home(2))
    near, partner = product(place, layer, factors, za, zb, True)
    total = near + send(partner, home(1)) + beyond + away
    return total


def local(factors, lower_inverse, upper_inverse, right_side):
    blk = lax.axis_index("blk")
    place = jnp.stack([blk // 4 % 8, blk % 4, blk // 32, lax.axis_index("grp")]).astype(jnp.int32)
    forward_first = solve_blocks(lower_inverse[0], right_side[0])

    def sweep(layer, carry):
        piece, out = carry
        coupling = coupling_of(place, layer, factors, piece)
        value = jnp.where(layer == 0, right_side[1], forward_first) - coupling
        forward = solve_blocks(lower_inverse[1], value)
        value = jnp.where(layer == 0, forward, value)
        value = solve_blocks(upper_inverse[1 - layer], value)
        return value.astype(jnp.bfloat16), lax.dynamic_update_index_in_dim(out, value, 1 - layer, 0)

    start = (forward_first.astype(jnp.bfloat16), jnp.zeros_like(right_side))
    return lax.fori_loop(0, 2, sweep, start)[1]


def solution(mesh):
    in_specs = (
        P(None, "blk", "grp"),
        P(None, "blk", None),
        P(None, "blk", None),
        P(None, "blk", "grp"),
    )
    out_specs = P(None, "blk", "grp")
    return jax.shard_map(local, mesh=mesh, in_specs=in_specs, out_specs=out_specs, check_vma=False)
```

time: 195 us -> 196 us (level)
  waiting for transfers between devices: 59 us -> 64.6 us
  other arithmetic: 4.88 us -> 0.41 us
  Pallas kernels: 18.9 us -> 22.2 us
  local copies, waits for them, and re-layouts: 10 us -> 7.73 us
    ppermute x62, waiting for transfers between devices: 59 us -> 64.6 us  [send(): return lax.ppermute(value, BOTH, perm)]
    pallas_call x2 -> x4, Pallas kernels: 18.9 us -> 22.2 us  [product(): pl.pallas_call(functools.partial(product_kernel, home_half=home_half), ou...]
    another operation x2 -> x1, other arithmetic: 2.5 us -> 0.08 us  [local(): jnp.stack([blk // 4 % 8, blk % 4, blk // 32, lax.axis_index('grp')])]
    sub x2, other arithmetic: 2.14 us -> 0.12 us  [sweep(): value = jnp.where(layer == 0, right_side[1], forward_first) - coupling]
    while x76 -> x126, local copies, waits for them, and re-layouts: 2.84 us -> 4.26 us
  transfers between devices with their start and end apart: 62 -> 62, of which waited for: 32 -> 32; matrix products, arithmetic and copies ran while one was open for 4% -> 0% of each run, Pallas kernels for 0% -> 6%
where the time goes in v1:
time: 196 us; the launch traced here: 194 us
  starting transfers between devices  96.8 us (49%)
  waiting for transfers between devices  64.6 us (33%)
  Pallas kernels  22.2 us (11%)
  local copies, waits for them, and re-layouts  7.73 us (4%)
    ppermute x62, starting transfers between devices, send(): return lax.ppermute(value, BOTH, perm)  96.8 us
    ppermute x62, waiting for transfers between devices, send(): return lax.ppermute(value, BOTH, perm)  64.6 us
    pallas_call x4, Pallas kernels, product(): pl.pallas_call(functools.partial(product_kernel, home_half=home_half), ou...  22.2 us
    while x126, local copies, waits for them, and re-layouts  4.26 us
  transfers between devices with their start and end apart: 62, of which 32 were waited for; matrix products, arithmetic and copies ran while one was open for 0% of the time, Pallas kernels for 6%

profile of v1, /device:TPU:2, one launch (start us, length us, event | category | flops | bytes accessed | tf_op | source)
XLA Modules:
  0.0 194.3 jit_solution(4378495571105048073)
XLA Ops:
  3.8 190.6 %while.17 = (s32[]{:T(128)}, bf16[384,128]{1,0:T(8,128)(2,1)S(1)}, f32[2,384,128]{2,1,0:T(8,128)}, f32[2,384,128]{2,1,0:T(8,128)}, f32[2,384,128]{2,1,0:T(8,128)...) while((s32[]{:T(128)}, bf16[384,128]{1,0:T(8,128)(2,1)S(1)}, ...), condition=%wide.region_1.2_spmd, body=%wide.region_0.1_spmd.sunk | while | flops 151928832 | bytes 68913392 | solution.py:199
  3.8 3.3 %collective-permute-start = (bf16[384,128]{1,0:T(8,128)(2,1)S(1)}, bf16[384,128]{1,0:T(8,128)(2,1)S(1)}, u32[]{:S(2)}, u32[]{:S(2)}) collective-permute-start(bf16[384,128]{1,0:T(8,128)(2,1)S(1)} %get-tuple-element.326), channel_id=1, source_target_pairs={{0,32},{1,48},{2,160},{3,176},{4,36},{5,52},{6,164},{7,180},{8,40}... | collective-permute-start | bytes 294920 | tf_op jit(solution)/shard_map/while/body/eval_jaxpr/ppermute | solution.py:68
  7.0 4.9 %collective-permute-start.1 = (bf16[384,128]{1,0:T(8,128)(2,1)S(1)}, bf16[384,128]{1,0:T(8,128)(2,1)S(1)}, u32[]{:S(2)}, u32[]{:S(2)}) collective-permute-start(bf16[384,128]{1,0:T(8,128)(2,1)S(1)} %get-tuple-element.326), channel_id=1, source_target_pairs={{0,96},{1,112},{2,224},{3,240},{4,100},{5,116},{6,228},{7,244},{8,... | collective-permute-start | bytes 294920 | tf_op jit(solution)/shard_map/while/body/eval_jaxpr/ppermute | solution.py:68
  12.0 5.9 %collective-permute-start.11 = (bf16[384,128]{1,0:T(8,128)(2,1)S(1)}, bf16[384,128]{1,0:T(8,128)(2,1)S(1)}, u32[]{:S(2)}, u32[]{:S(2)}) collective-permute-start(bf16[384,128]{1,0:T(8,128)(2,1)S(1)} %get-tuple-element.326), channel_id=1, source_target_pairs={{0,232},{1,248},{2,104},{3,120},{4,236},{5,252},{6,108},{7,124},{8... | collective-permute-start | bytes 294920 | tf_op jit(solution)/shard_map/while/body/eval_jaxpr/ppermute | solution.py:68
  17.9 1.0 collective-permute-start.12
  19.7 1.4 collective-permute-done.11
  21.1 2.6 %collective-permute-done.12 = bf16[384,128]{1,0:T(8,128)(2,1)S(1)} collective-permute-done((bf16[384,128]{1,0:T(8,128)(2,1)S(1)}, bf16[384,128]{1,0:T(8,128)(2,1)S(1)}, u32[]{:S(2)}, u32[]{:S(2)}) %collective-permute-start.12) | collective-permute-done | bytes 98336 | tf_op jit(solution)/shard_map/while/body/eval_jaxpr/ppermute | solution.py:68
  23.9 4.0 %collective-permute-start.3 = (bf16[2,384,128]{2,1,0:T(8,128)(2,1)S(1)}, bf16[2,384,128]{2,1,0:T(8,128)(2,1)S(1)}, u32[]{:S(2)}, u32[]{:S(2)}) collective-permute-start(bf16[2,384,128]{2,1,0:T(8,128)(2,1)S(1)} %pad_maximum_fusion.6), channel_id=1, source_target_pairs={{0,112},{1,113},{2,114},{3,115},{4,116},{5,117},{6,118},{7,119},{8... | collective-permute-start | bytes 589832 | tf_op jit(solution)/shard_map/while/body/eval_jaxpr/ppermute | solution.py:68
  27.9 3.2 %collective-permute-start.25 = (bf16[2,384,128]{2,1,0:T(8,128)(2,1)S(1)}, bf16[2,384,128]{2,1,0:T(8,128)(2,1)S(1)}, u32[]{:S(2)}, u32[]{:S(2)}) collective-permute-start(bf16[2,384,128]{2,1,0:T(8,128)(2,1)S(1)} %pad_maximum_fusion.8.refs_8_), channel_id=1, source_target_pairs={{0,112},{1,113},{2,114},{3,115},{4,116},{5,117},{6,118},{7,119},{8... | collective-permute-start | bytes 589832 | tf_op jit(solution)/shard_map/while/body/eval_jaxpr/ppermute | solution.py:68
  31.5 2.9 %collective-permute-start.21 = (bf16[2,384,128]{2,1,0:T(8,128)(2,1)S(1)}, bf16[2,384,128]{2,1,0:T(8,128)(2,1)S(1)}, u32[]{:S(2)}, u32[]{:S(2)}) collective-permute-start(bf16[2,384,128]{2,1,0:T(8,128)(2,1)S(1)} %collective-permute-done.13.refs_9_), channel_id=1, source_target_pairs={{0,112},{1,113},{2,114},{3,115},{4,116},{5,117},{6,118},{7,119},{8... | collective-permute-start | bytes 589832 | tf_op jit(solution)/shard_map/while/body/eval_jaxpr/ppermute | solution.py:68
  34.5 1.7 collective-permute-start.5
  36.9 2.4 %collective-permute-done.4 = bf16[2,384,128]{2,1,0:T(8,128)(2,1)S(1)} collective-permute-done((bf16[2,384,128]{2,1,0:T(8,128)(2,1)S(1)}, bf16[2,384,128]{2,1,0:T(8,128)(2,1)S(1)}, u32[]{:S(2)}, u32[]{:S(2)}) %collective-permute-start.4) | collective-permute-done | bytes 196640 | tf_op jit(solution)/shard_map/while/body/eval_jaxpr/ppermute | solution.py:68
  40.3 2.9 %collective-permute-start.26 = (bf16[2,384,128]{2,1,0:T(8,128)(2,1)S(1)}, bf16[2,384,128]{2,1,0:T(8,128)(2,1)S(1)}, u32[]{:S(2)}, u32[]{:S(2)}) collective-permute-start(bf16[2,384,128]{2,1,0:T(8,128)(2,1)S(1)} %collective-permute-done.25.refs_22_), channel_id=1, source_target_pairs={{0,112},{1,113},{2,114},{3,115},{4,116},{5,117},{6,118},{7,119},{8... | collective-permute-start | bytes 589832 | tf_op jit(solution)/shard_map/while/body/eval_jaxpr/ppermute | solution.py:68
  43.3 2.6 %collective-permute-done.15.refs_11_ = bf16[2,384,128]{2,1,0:T(8,128)(2,1)S(1)} collective-permute-done((bf16[2,384,128]{2,1,0:T(8,128)(2,1)S(1)}, bf16[2,384,128]{2,1,0:T(8,128)(2,1)S(1)}, u32[]{:S(2)}, u32[]{:S(2)}) %collective-permute-start.15) | collective-permute-done | bytes 196640 | tf_op jit(solution)/shard_map/while/body/eval_jaxpr/ppermute | solution.py:68
  45.8 2.3 %collective-permute-start.8 = (bf16[4,384,128]{2,1,0:T(8,128)(2,1)S(1)}, bf16[4,384,128]{2,1,0:T(8,128)(2,1)S(1)}, u32[]{:S(2)}, u32[]{:S(2)}) collective-permute-start(bf16[4,384,128]{2,1,0:T(8,128)(2,1)S(1)} %constant_dynamic-update-slice_fusion.5.refs_1_), channel_id=1, source_target_pairs={{0,12},{1,13},{2,14},{3,15},{4,0},{5,1},{6,2},{7,3},{8,4},{9,5},{1... | collective-permute-start | bytes 1179656 | tf_op jit(solution)/shard_map/while/body/eval_jaxpr/ppermute | solution.py:68
  48.4 1.5 collective-permute-start.6
  49.9 1.0 collective-permute-start.22
  50.9 1.0 collective-permute-start.17
  52.7 2.8 %collective-permute-done.22.refs_21_ = bf16[2,384,128]{2,1,0:T(8,128)(2,1)S(1)} collective-permute-done((bf16[2,384,128]{2,1,0:T(8,128)(2,1)S(1)}, bf16[2,384,128]{2,1,0:T(8,128)(2,1)S(1)}, u32[]{:S(2)}, u32[]{:S(2)}) %collective-permute-start.22) | collective-permute-done | bytes 196640 | tf_op jit(solution)/shard_map/while/body/eval_jaxpr/ppermute | solution.py:68
  55.6 2.2 %collective-permute-start.27 = (bf16[2,384,128]{2,1,0:T(8,128)(2,1)S(1)}, bf16[2,384,128]{2,1,0:T(8,128)(2,1)S(1)}, u32[]{:S(2)}, u32[]{:S(2)}) collective-permute-start(bf16[2,384,128]{2,1,0:T(8,128)(2,1)S(1)} %collective-permute-done.26.refs_20_), channel_id=1, source_target_pairs={{0,112},{1,113},{2,114},{3,115},{4,116},{5,117},{6,118},{7,119},{8... | collective-permute-start | bytes 589832 | tf_op jit(solution)/shard_map/while/body/eval_jaxpr/ppermute | solution.py:68
  58.4 1.9 collective-permute-start.7
  60.5 1.5 collective-permute-start.23
  62.4 1.4 collective-permute-start.19
  64.5 1.6 collective-permute-done.23.refs_19_
  66.1 2.7 %collective-permute-start.24 = (bf16[2,384,128]{2,1,0:T(8,128)(2,1)S(1)}, bf16[2,384,128]{2,1,0:T(8,128)(2,1)S(1)}, u32[]{:S(2)}, u32[]{:S(2)}) collective-permute-start(bf16[2,384,128]{2,1,0:T(8,128)(2,1)S(1)} %collective-permute-done.23.refs_19_), channel_id=1, source_target_pairs={{0,112},{1,113},{2,114},{3,115},{4,116},{5,117},{6,118},{7,119},{8... | collective-permute-start | bytes 589832 | tf_op jit(solution)/shard_map/while/body/eval_jaxpr/ppermute | solution.py:68
  69.7 2.1 %collective-permute-done.20.refs_16_ = bf16[2,384,128]{2,1,0:T(8,128)(2,1)S(1)} collective-permute-done((bf16[2,384,128]{2,1,0:T(8,128)(2,1)S(1)}, bf16[2,384,128]{2,1,0:T(8,128)(2,1)S(1)}, u32[]{:S(2)}, u32[]{:S(2)}) %collective-permute-start.20) | collective-permute-done | bytes 196640 | tf_op jit(solution)/shard_map/while/body/eval_jaxpr/ppermute | solution.py:68
  71.9 1.4 collective-permute-done.24.refs_17_
  74.7 5.5 %eval_jaxpr.17 = (f32[384,128]{1,0:T(8,128)}, f32[384,128]{1,0:T(8,128)}) custom-call(s32[4]{0:T(128)S(1)} %get-tuple-element.343.place, s32[1]{0:T(128)} %bitcast.59.sweep, bf16[2,384,6144]{2,1,0:T(8,128)(2,1)} %get-tuple-element.344.factors, bf16[4,384,128]{2,1,0:T(8,128)(2,1)} %copy-done, bf16[4,384,128]{2,1,0:T(8,128)(2,1)} %copy-done.1, ...), custom_call_target="tpu_custom_call" | custom-call | tf_op jit(solution)/shard_map/while/body/eval_jaxpr/pallas_call | solution.py:142
  80.4 5.6 %eval_jaxpr.16 = (f32[384,128]{1,0:T(8,128)}, f32[384,128]{1,0:T(8,128)}) custom-call(s32[4]{0:T(128)S(1)} %get-tuple-element.343.place, s32[1]{0:T(128)} %bitcast.59.sweep, bf16[2,384,6144]{2,1,0:T(8,128)(2,1)} %get-tuple-element.344.factors, bf16[4,384,128]{2,1,0:T(8,128)(2,1)} %copy-done, bf16[4,384,128]{2,1,0:T(8,128)(2,1)} %copy-done.1, ...), custom_call_target="tpu_custom_call" | custom-call | tf_op jit(solution)/shard_map/while/body/eval_jaxpr/pallas_call | solution.py:142
  86.0 3.4 %collective-permute-start.28 = (f32[384,128]{1,0:T(8,128)}, f32[384,128]{1,0:T(8,128)S(1)}, u32[]{:S(2)}, u32[]{:S(2)}) collective-permute-start(f32[384,128]{1,0:T(8,128)} %get-tuple-element.307), channel_id=1, source_target_pairs={{0,2},{1,3},{2,0},{3,1},{4,6},{5,7},{6,4},{7,5},{8,10},{9,11},{10,... | collective-permute-start | bytes 589832 | tf_op jit(solution)/shard_map/while/body/eval_jaxpr/ppermute | solution.py:68
  89.6 5.7 %collective-permute-done.28 = f32[384,128]{1,0:T(8,128)S(1)} collective-permute-done((f32[384,128]{1,0:T(8,128)}, f32[384,128]{1,0:T(8,128)S(1)}, u32[]{:S(2)}, u32[]{:S(2)}) %collective-permute-start.28) | collective-permute-done | bytes 196640 | tf_op jit(solution)/shard_map/while/body/eval_jaxpr/ppermute | solution.py:68
  95.3 3.8 %collective-permute-done.29 = f32[384,128]{1,0:T(8,128)S(1)} collective-permute-done((f32[384,128]{1,0:T(8,128)}, f32[384,128]{1,0:T(8,128)S(1)}, u32[]{:S(2)}, u32[]{:S(2)}) %collective-permute-start.29) | collective-permute-done | bytes 196640 | tf_op jit(solution)/shard_map/while/body/eval_jaxpr/ppermute | solution.py:68
  100.7 5.2 %collective-permute-start.1 = (bf16[384,128]{1,0:T(8,128)(2,1)S(1)}, bf16[384,128]{1,0:T(8,128)(2,1)S(1)}, u32[]{:S(2)}, u32[]{:S(2)}) collective-permute-start(bf16[384,128]{1,0:T(8,128)(2,1)S(1)} %get-tuple-element.326), channel_id=1, source_target_pairs={{0,96},{1,112},{2,224},{3,240},{4,100},{5,116},{6,228},{7,244},{8,... | collective-permute-start | bytes 294920 | tf_op jit(solution)/shard_map/while/body/eval_jaxpr/ppermute | solution.py:68
  105.9 6.3 %collective-permute-start.11 = (bf16[384,128]{1,0:T(8,128)(2,1)S(1)}, bf16[384,128]{1,0:T(8,128)(2,1)S(1)}, u32[]{:S(2)}, u32[]{:S(2)}) collective-permute-start(bf16[384,128]{1,0:T(8,128)(2,1)S(1)} %get-tuple-element.326), channel_id=1, source_target_pairs={{0,232},{1,248},{2,104},{3,120},{4,236},{5,252},{6,108},{7,124},{8... | collective-permute-start | bytes 294920 | tf_op jit(solution)/shard_map/while/body/eval_jaxpr/ppermute | solution.py:68
  113.2 2.2 %collective-permute-done.11 = bf16[384,128]{1,0:T(8,128)(2,1)S(1)} collective-permute-done((bf16[384,128]{1,0:T(8,128)(2,1)S(1)}, bf16[384,128]{1,0:T(8,128)(2,1)S(1)}, u32[]{:S(2)}, u32[]{:S(2)}) %collective-permute-start.11) | collective-permute-done | bytes 98336 | tf_op jit(solution)/shard_map/while/body/eval_jaxpr/ppermute | solution.py:68
  115.4 2.7 %collective-permute-done.12 = bf16[384,128]{1,0:T(8,128)(2,1)S(1)} collective-permute-done((bf16[384,128]{1,0:T(8,128)(2,1)S(1)}, bf16[384,128]{1,0:T(8,128)(2,1)S(1)}, u32[]{:S(2)}, u32[]{:S(2)}) %collective-permute-start.12) | collective-permute-done | bytes 98336 | tf_op jit(solution)/shard_map/while/body/eval_jaxpr/ppermute | solution.py:68
  118.2 2.4 %collective-permute-start.3 = (bf16[2,384,128]{2,1,0:T(8,128)(2,1)S(1)}, bf16[2,384,128]{2,1,0:T(8,128)(2,1)S(1)}, u32[]{:S(2)}, u32[]{:S(2)}) collective-permute-start(bf16[2,384,128]{2,1,0:T(8,128)(2,1)S(1)} %pad_maximum_fusion.6), channel_id=1, source_target_pairs={{0,112},{1,113},{2,114},{3,115},{4,116},{5,117},{6,118},{7,119},{8... | collective-permute-start | bytes 589832 | tf_op jit(solution)/shard_map/while/body/eval_jaxpr/ppermute | solution.py:68
  120.6 3.2 %collective-permute-start.25 = (bf16[2,384,128]{2,1,0:T(8,128)(2,1)S(1)}, bf16[2,384,128]{2,1,0:T(8,128)(2,1)S(1)}, u32[]{:S(2)}, u32[]{:S(2)}) collective-permute-start(bf16[2,384,128]{2,1,0:T(8,128)(2,1)S(1)} %pad_maximum_fusion.8.refs_8_), channel_id=1, source_target_pairs={{0,112},{1,113},{2,114},{3,115},{4,116},{5,117},{6,118},{7,119},{8... | collective-permute-start | bytes 589832 | tf_op jit(solution)/shard_map/while/body/eval_jaxpr/ppermute | solution.py:68
  123.8 1.3 collective-permute-done.13.refs_9_
  125.1 1.9 collective-permute-start.21
  128.0 1.2 collective-permute-done.14.refs_10_
  129.2 1.1 collective-permute-start.10
  131.9 1.4 collective-permute-start.16
  133.2 1.0 collective-permute-done.21.refs_23_
  134.2 2.1 %collective-permute-start.26 = (bf16[2,384,128]{2,1,0:T(8,128)(2,1)S(1)}, bf16[2,384,128]{2,1,0:T(8,128)(2,1)S(1)}, u32[]{:S(2)}, u32[]{:S(2)}) collective-permute-start(bf16[2,384,128]{2,1,0:T(8,128)(2,1)S(1)} %collective-permute-done.25.refs_22_), channel_id=1, source_target_pairs={{0,112},{1,113},{2,114},{3,115},{4,116},{5,117},{6,118},{7,119},{8... | collective-permute-start | bytes 589832 | tf_op jit(solution)/shard_map/while/body/eval_jaxpr/ppermute | solution.py:68
  136.3 3.0 %collective-permute-done.15.refs_11_ = bf16[2,384,128]{2,1,0:T(8,128)(2,1)S(1)} collective-permute-done((bf16[2,384,128]{2,1,0:T(8,128)(2,1)S(1)}, bf16[2,384,128]{2,1,0:T(8,128)(2,1)S(1)}, u32[]{:S(2)}, u32[]{:S(2)}) %collective-permute-start.15) | collective-permute-done | bytes 196640 | tf_op jit(solution)/shard_map/while/body/eval_jaxpr/ppermute | solution.py:68
  139.3 3.1 %collective-permute-start.8 = (bf16[4,384,128]{2,1,0:T(8,128)(2,1)S(1)}, bf16[4,384,128]{2,1,0:T(8,128)(2,1)S(1)}, u32[]{:S(2)}, u32[]{:S(2)}) collective-permute-start(bf16[4,384,128]{2,1,0:T(8,128)(2,1)S(1)} %constant_dynamic-update-slice_fusion.5.refs_1_), channel_id=1, source_target_pairs={{0,12},{1,13},{2,14},{3,15},{4,0},{5,1},{6,2},{7,3},{8,4},{9,5},{1... | collective-permute-start | bytes 1179656 | tf_op jit(solution)/shard_map/while/body/eval_jaxpr/ppermute | solution.py:68
  142.9 2.3 %collective-permute-start.6 = (bf16[4,384,128]{2,1,0:T(8,128)(2,1)S(1)}, bf16[4,384,128]{2,1,0:T(8,128)(2,1)S(1)}, u32[]{:S(2)}, u32[]{:S(2)}) collective-permute-start(bf16[4,384,128]{2,1,0:T(8,128)(2,1)S(1)} %constant_dynamic-update-slice_fusion.5.refs_1_), channel_id=1, source_target_pairs={{0,4},{1,5},{2,6},{3,7},{4,8},{5,9},{6,10},{7,11},{8,12},{9,13},{1... | collective-permute-start | bytes 1179656 | tf_op jit(solution)/shard_map/while/body/eval_jaxpr/ppermute | solution.py:68
  145.5 1.7 collective-permute-start.17
  147.3 4.5 %collective-permute-done.22.refs_21_ = bf16[2,384,128]{2,1,0:T(8,128)(2,1)S(1)} collective-permute-done((bf16[2,384,128]{2,1,0:T(8,128)(2,1)S(1)}, bf16[2,384,128]{2,1,0:T(8,128)(2,1)S(1)}, u32[]{:S(2)}, u32[]{:S(2)}) %collective-permute-start.22) | collective-permute-done | bytes 196640 | tf_op jit(solution)/shard_map/while/body/eval_jaxpr/ppermute | solution.py:68
  151.8 1.5 collective-permute-start.27
  153.3 1.1 collective-permute-done.17.refs_13_
  154.4 1.8 collective-permute-start.7
  156.2 1.1 collective-permute-done.18.refs_14_
  157.6 1.9 collective-permute-start.19
  159.9 3.1 %collective-permute-done.23.refs_19_ = bf16[2,384,128]{2,1,0:T(8,128)(2,1)S(1)} collective-permute-done((bf16[2,384,128]{2,1,0:T(8,128)(2,1)S(1)}, bf16[2,384,128]{2,1,0:T(8,128)(2,1)S(1)}, u32[]{:S(2)}, u32[]{:S(2)}) %collective-permute-start.23) | collective-permute-done | bytes 196640 | tf_op jit(solution)/shard_map/while/body/eval_jaxpr/ppermute | solution.py:68
  163.0 1.5 collective-permute-start.24
  164.5 2.0 %collective-permute-done.19.refs_15_ = bf16[2,384,128]{2,1,0:T(8,128)(2,1)S(1)} collective-permute-done((bf16[2,384,128]{2,1,0:T(8,128)(2,1)S(1)}, bf16[2,384,128]{2,1,0:T(8,128)(2,1)S(1)}, u32[]{:S(2)}, u32[]{:S(2)}) %collective-permute-start.19) | collective-permute-done | bytes 196640 | tf_op jit(solution)/shard_map/while/body/eval_jaxpr/ppermute | solution.py:68
  166.5 2.1 %collective-permute-done.20.refs_16_ = bf16[2,384,128]{2,1,0:T(8,128)(2,1)S(1)} collective-permute-done((bf16[2,384,128]{2,1,0:T(8,128)(2,1)S(1)}, bf16[2,384,128]{2,1,0:T(8,128)(2,1)S(1)}, u32[]{:S(2)}, u32[]{:S(2)}) %collective-permute-start.20) | collective-permute-done | bytes 196640 | tf_op jit(solution)/shard_map/while/body/eval_jaxpr/ppermute | solution.py:68
  170.2 5.5 %eval_jaxpr.17 = (f32[384,128]{1,0:T(8,128)}, f32[384,128]{1,0:T(8,128)}) custom-call(s32[4]{0:T(128)S(1)} %get-tuple-element.343.place, s32[1]{0:T(128)} %bitcast.59.sweep, bf16[2,384,6144]{2,1,0:T(8,128)(2,1)} %get-tuple-element.344.factors, bf16[4,384,128]{2,1,0:T(8,128)(2,1)} %copy-done, bf16[4,384,128]{2,1,0:T(8,128)(2,1)} %copy-done.1, ...), custom_call_target="tpu_custom_call" | custom-call | tf_op jit(solution)/shard_map/while/body/eval_jaxpr/pallas_call | solution.py:142
  175.9 5.6 %eval_jaxpr.16 = (f32[384,128]{1,0:T(8,128)}, f32[384,128]{1,0:T(8,128)}) custom-call(s32[4]{0:T(128)S(1)} %get-tuple-element.343.place, s32[1]{0:T(128)} %bitcast.59.sweep, bf16[2,384,6144]{2,1,0:T(8,128)(2,1)} %get-tuple-element.344.factors, bf16[4,384,128]{2,1,0:T(8,128)(2,1)} %copy-done, bf16[4,384,128]{2,1,0:T(8,128)(2,1)} %copy-done.1, ...), custom_call_target="tpu_custom_call" | custom-call | tf_op jit(solution)/shard_map/while/body/eval_jaxpr/pallas_call | solution.py:142
  181.6 1.8 collective-permute-start.29
  183.5 6.1 %collective-permute-done.28 = f32[384,128]{1,0:T(8,128)S(1)} collective-permute-done((f32[384,128]{1,0:T(8,128)}, f32[384,128]{1,0:T(8,128)S(1)}, u32[]{:S(2)}, u32[]{:S(2)}) %collective-permute-start.28) | collective-permute-done | bytes 196640 | tf_op jit(solution)/shard_map/while/body/eval_jaxpr/ppermute | solution.py:68
  189.6 3.2 %collective-permute-done.29 = f32[384,128]{1,0:T(8,128)S(1)} collective-permute-done((f32[384,128]{1,0:T(8,128)}, f32[384,128]{1,0:T(8,128)S(1)}, u32[]{:S(2)}, u32[]{:S(2)}) %collective-permute-start.29) | collective-permute-done | bytes 196640 | tf_op jit(solution)/shard_map/while/body/eval_jaxpr/ppermute | solution.py:68
  (221 shorter events, 22.2 us)
Async XLA Ops:
  3.8 15.1 %collective-permute-start = (bf16[384,128]{1,0:T(8,128)(2,1)S(1)}, bf16[384,128]{1,0:T(8,128)(2,1)S(1)}, u32[]{:S(2)}, u32[]{:S(2)}) collective-permute-start(bf16[384,128]{1,0:T(8,128)(2,1)S(1)} %get-tuple-element.326), channel_id=1, source_target_pairs={{0,32},{1,48},{2,160},{3,176},{4,36},{5,52},{6,164},{7,180},{8,40}... | collective-permute-start | bytes 294920 | tf_op jit(solution)/shard_map/while/body/eval_jaxpr/ppermute | solution.py:68
  7.0 11.8 %collective-permute-start.1 = (bf16[384,128]{1,0:T(8,128)(2,1)S(1)}, bf16[384,128]{1,0:T(8,128)(2,1)S(1)}, u32[]{:S(2)}, u32[]{:S(2)}) collective-permute-start(bf16[384,128]{1,0:T(8,128)(2,1)S(1)} %get-tuple-element.326), channel_id=1, source_target_pairs={{0,96},{1,112},{2,224},{3,240},{4,100},{5,116},{6,228},{7,244},{8,... | collective-permute-start | bytes 294920 | tf_op jit(solution)/shard_map/while/body/eval_jaxpr/ppermute | solution.py:68
  12.0 9.1 %collective-permute-start.11 = (bf16[384,128]{1,0:T(8,128)(2,1)S(1)}, bf16[384,128]{1,0:T(8,128)(2,1)S(1)}, u32[]{:S(2)}, u32[]{:S(2)}) collective-permute-start(bf16[384,128]{1,0:T(8,128)(2,1)S(1)} %get-tuple-element.326), channel_id=1, source_target_pairs={{0,232},{1,248},{2,104},{3,120},{4,236},{5,252},{6,108},{7,124},{8... | collective-permute-start | bytes 294920 | tf_op jit(solution)/shard_map/while/body/eval_jaxpr/ppermute | solution.py:68
  17.9 5.8 %collective-permute-start.12 = (bf16[384,128]{1,0:T(8,128)(2,1)S(1)}, bf16[384,128]{1,0:T(8,128)(2,1)S(1)}, u32[]{:S(2)}, u32[]{:S(2)}) collective-permute-start(bf16[384,128]{1,0:T(8,128)(2,1)S(1)} %get-tuple-element.326), channel_id=1, source_target_pairs={{0,224},{1,240},{2,96},{3,112},{4,228},{5,244},{6,100},{7,116},{8,... | collective-permute-start | bytes 294920 | tf_op jit(solution)/shard_map/while/body/eval_jaxpr/ppermute | solution.py:68
  18.9 12.2 %collective-permute-start.2 = (bf16[2,384,128]{2,1,0:T(8,128)(2,1)S(1)}, bf16[2,384,128]{2,1,0:T(8,128)(2,1)S(1)}, u32[]{:S(2)}, u32[]{:S(2)}) collective-permute-start(bf16[2,384,128]{2,1,0:T(8,128)(2,1)S(1)} %pad_maximum_fusion.6), channel_id=1, source_target_pairs={{0,16},{1,17},{2,18},{3,19},{4,20},{5,21},{6,22},{7,23},{8,24},{9,... | collective-permute-start | bytes 589832 | tf_op jit(solution)/shard_map/while/body/eval_jaxpr/ppermute | solution.py:68
  23.7 50.3 %copy-start.2 = (bf16[2,384,128]{2,1,0:T(8,128)(2,1)}, bf16[2,384,128]{2,1,0:T(8,128)(2,1)S(1)}, u32[]{:S(2)}) copy-start(bf16[2,384,128]{2,1,0:T(8,128)(2,1)S(1)} %pad_maximum_fusion.8.refs_8_) | copy-start | bytes 589828 | tf_op jit(solution)/shard_map/while
  23.7 7.8 %collective-permute-start.13 = (bf16[2,384,128]{2,1,0:T(8,128)(2,1)S(1)}, bf16[2,384,128]{2,1,0:T(8,128)(2,1)S(1)}, u32[]{:S(2)}, u32[]{:S(2)}) collective-permute-start(bf16[2,384,128]{2,1,0:T(8,128)(2,1)S(1)} %pad_maximum_fusion.8.refs_8_), channel_id=1, source_target_pairs={{0,4},{1,5},{2,6},{3,7},{4,8},{5,9},{6,10},{7,11},{8,12},{9,13},{1... | collective-permute-start | bytes 589832 | tf_op jit(solution)/shard_map/while/body/eval_jaxpr/ppermute | solution.py:68
  23.9 10.6 %collective-permute-start.3 = (bf16[2,384,128]{2,1,0:T(8,128)(2,1)S(1)}, bf16[2,384,128]{2,1,0:T(8,128)(2,1)S(1)}, u32[]{:S(2)}, u32[]{:S(2)}) collective-permute-start(bf16[2,384,128]{2,1,0:T(8,128)(2,1)S(1)} %pad_maximum_fusion.6), channel_id=1, source_target_pairs={{0,112},{1,113},{2,114},{3,115},{4,116},{5,117},{6,118},{7,119},{8... | collective-permute-start | bytes 589832 | tf_op jit(solution)/shard_map/while/body/eval_jaxpr/ppermute | solution.py:68
  27.9 8.3 %collective-permute-start.14 = (bf16[2,384,128]{2,1,0:T(8,128)(2,1)S(1)}, bf16[2,384,128]{2,1,0:T(8,128)(2,1)S(1)}, u32[]{:S(2)}, u32[]{:S(2)}) collective-permute-start(bf16[2,384,128]{2,1,0:T(8,128)(2,1)S(1)} %pad_maximum_fusion.8.refs_8_), channel_id=1, source_target_pairs={{0,16},{1,17},{2,18},{3,19},{4,20},{5,21},{6,22},{7,23},{8,24},{9,... | collective-permute-start | bytes 589832 | tf_op jit(solution)/shard_map/while/body/eval_jaxpr/ppermute | solution.py:68
  27.9 9.0 %collective-permute-start.25 = (bf16[2,384,128]{2,1,0:T(8,128)(2,1)S(1)}, bf16[2,384,128]{2,1,0:T(8,128)(2,1)S(1)}, u32[]{:S(2)}, u32[]{:S(2)}) collective-permute-start(bf16[2,384,128]{2,1,0:T(8,128)(2,1)S(1)} %pad_maximum_fusion.8.refs_8_), channel_id=1, source_target_pairs={{0,112},{1,113},{2,114},{3,115},{4,116},{5,117},{6,118},{7,119},{8... | collective-permute-start | bytes 589832 | tf_op jit(solution)/shard_map/while/body/eval_jaxpr/ppermute | solution.py:68
  31.1 8.2 %collective-permute-start.4 = (bf16[2,384,128]{2,1,0:T(8,128)(2,1)S(1)}, bf16[2,384,128]{2,1,0:T(8,128)(2,1)S(1)}, u32[]{:S(2)}, u32[]{:S(2)}) collective-permute-start(bf16[2,384,128]{2,1,0:T(8,128)(2,1)S(1)} %collective-permute-done.2), channel_id=1, source_target_pairs={{0,16},{1,17},{2,18},{3,19},{4,20},{5,21},{6,22},{7,23},{8,24},{9,... | collective-permute-start | bytes 589832 | tf_op jit(solution)/shard_map/while/body/eval_jaxpr/ppermute | solution.py:68
  31.5 8.9 %collective-permute-start.21 = (bf16[2,384,128]{2,1,0:T(8,128)(2,1)S(1)}, bf16[2,384,128]{2,1,0:T(8,128)(2,1)S(1)}, u32[]{:S(2)}, u32[]{:S(2)}) collective-permute-start(bf16[2,384,128]{2,1,0:T(8,128)(2,1)S(1)} %collective-permute-done.13.refs_9_), channel_id=1, source_target_pairs={{0,112},{1,113},{2,114},{3,115},{4,116},{5,117},{6,118},{7,119},{8... | collective-permute-start | bytes 589832 | tf_op jit(solution)/shard_map/while/body/eval_jaxpr/ppermute | solution.py:68
  34.5 16.4 %collective-permute-start.5 = (bf16[4,384,128]{2,1,0:T(8,128)(2,1)S(1)}, bf16[4,384,128]{2,1,0:T(8,128)(2,1)S(1)}, u32[]{:S(2)}, u32[]{:S(2)}) collective-permute-start(bf16[4,384,128]{2,1,0:T(8,128)(2,1)S(1)} %pad_maximum_fusion.7.refs_0_), channel_id=1, source_target_pairs={{0,4},{1,5},{2,6},{3,7},{4,8},{5,9},{6,10},{7,11},{8,12},{9,13},{1... | collective-permute-start | bytes 1179656 | tf_op jit(solution)/shard_map/while/body/eval_jaxpr/ppermute | solution.py:68
  36.2 15.7 %collective-permute-start.10 = (bf16[4,384,128]{2,1,0:T(8,128)(2,1)S(1)}, bf16[4,384,128]{2,1,0:T(8,128)(2,1)S(1)}, u32[]{:S(2)}, u32[]{:S(2)}) collective-permute-start(bf16[4,384,128]{2,1,0:T(8,128)(2,1)S(1)} %pad_maximum_fusion.7.refs_0_), channel_id=1, source_target_pairs={{0,12},{1,13},{2,14},{3,15},{4,0},{5,1},{6,2},{7,3},{8,4},{9,5},{1... | collective-permute-start | bytes 1179656 | tf_op jit(solution)/shard_map/while/body/eval_jaxpr/ppermute | solution.py:68
  36.9 8.9 %collective-permute-start.15 = (bf16[2,384,128]{2,1,0:T(8,128)(2,1)S(1)}, bf16[2,384,128]{2,1,0:T(8,128)(2,1)S(1)}, u32[]{:S(2)}, u32[]{:S(2)}) collective-permute-start(bf16[2,384,128]{2,1,0:T(8,128)(2,1)S(1)} %collective-permute-done.13.refs_9_), channel_id=1, source_target_pairs={{0,16},{1,17},{2,18},{3,19},{4,20},{5,21},{6,22},{7,23},{8,24},{9,... | collective-permute-start | bytes 589832 | tf_op jit(solution)/shard_map/while/body/eval_jaxpr/ppermute | solution.py:68
  39.4 9.0 %collective-permute-start.16 = (bf16[2,384,128]{2,1,0:T(8,128)(2,1)S(1)}, bf16[2,384,128]{2,1,0:T(8,128)(2,1)S(1)}, u32[]{:S(2)}, u32[]{:S(2)}) collective-permute-start(bf16[2,384,128]{2,1,0:T(8,128)(2,1)S(1)} %collective-permute-done.14.refs_10_), channel_id=1, source_target_pairs={{0,16},{1,17},{2,18},{3,19},{4,20},{5,21},{6,22},{7,23},{8,24},{9,... | collective-permute-start | bytes 589832 | tf_op jit(solution)/shard_map/while/body/eval_jaxpr/ppermute | solution.py:68
  40.3 9.5 %collective-permute-start.26 = (bf16[2,384,128]{2,1,0:T(8,128)(2,1)S(1)}, bf16[2,384,128]{2,1,0:T(8,128)(2,1)S(1)}, u32[]{:S(2)}, u32[]{:S(2)}) collective-permute-start(bf16[2,384,128]{2,1,0:T(8,128)(2,1)S(1)} %collective-permute-done.25.refs_22_), channel_id=1, source_target_pairs={{0,112},{1,113},{2,114},{3,115},{4,116},{5,117},{6,118},{7,119},{8... | collective-permute-start | bytes 589832 | tf_op jit(solution)/shard_map/while/body/eval_jaxpr/ppermute | solution.py:68
  45.8 16.2 %collective-permute-start.8 = (bf16[4,384,128]{2,1,0:T(8,128)(2,1)S(1)}, bf16[4,384,128]{2,1,0:T(8,128)(2,1)S(1)}, u32[]{:S(2)}, u32[]{:S(2)}) collective-permute-start(bf16[4,384,128]{2,1,0:T(8,128)(2,1)S(1)} %constant_dynamic-update-slice_fusion.5.refs_1_), channel_id=1, source_target_pairs={{0,12},{1,13},{2,14},{3,15},{4,0},{5,1},{6,2},{7,3},{8,4},{9,5},{1... | collective-permute-start | bytes 1179656 | tf_op jit(solution)/shard_map/while/body/eval_jaxpr/ppermute | solution.py:68
  48.4 15.4 %collective-permute-start.6 = (bf16[4,384,128]{2,1,0:T(8,128)(2,1)S(1)}, bf16[4,384,128]{2,1,0:T(8,128)(2,1)S(1)}, u32[]{:S(2)}, u32[]{:S(2)}) collective-permute-start(bf16[4,384,128]{2,1,0:T(8,128)(2,1)S(1)} %constant_dynamic-update-slice_fusion.5.refs_1_), channel_id=1, source_target_pairs={{0,4},{1,5},{2,6},{3,7},{4,8},{5,9},{6,10},{7,11},{8,12},{9,13},{1... | collective-permute-start | bytes 1179656 | tf_op jit(solution)/shard_map/while/body/eval_jaxpr/ppermute | solution.py:68
  49.9 5.7 %collective-permute-start.22 = (bf16[2,384,128]{2,1,0:T(8,128)(2,1)S(1)}, bf16[2,384,128]{2,1,0:T(8,128)(2,1)S(1)}, u32[]{:S(2)}, u32[]{:S(2)}) collective-permute-start(bf16[2,384,128]{2,1,0:T(8,128)(2,1)S(1)} %collective-permute-done.21.refs_23_), channel_id=1, source_target_pairs={{0,112},{1,113},{2,114},{3,115},{4,116},{5,117},{6,118},{7,119},{8... | collective-permute-start | bytes 589832 | tf_op jit(solution)/shard_map/while/body/eval_jaxpr/ppermute | solution.py:68
  50.9 7.5 %collective-permute-start.17 = (bf16[2,384,128]{2,1,0:T(8,128)(2,1)S(1)}, bf16[2,384,128]{2,1,0:T(8,128)(2,1)S(1)}, u32[]{:S(2)}, u32[]{:S(2)}) collective-permute-start(bf16[2,384,128]{2,1,0:T(8,128)(2,1)S(1)} %collective-permute-done.15.refs_11_), channel_id=1, source_target_pairs={{0,16},{1,17},{2,18},{3,19},{4,20},{5,21},{6,22},{7,23},{8,24},{9,... | collective-permute-start | bytes 589832 | tf_op jit(solution)/shard_map/while/body/eval_jaxpr/ppermute | solution.py:68
  51.9 8.5 %collective-permute-start.18 = (bf16[2,384,128]{2,1,0:T(8,128)(2,1)S(1)}, bf16[2,384,128]{2,1,0:T(8,128)(2,1)S(1)}, u32[]{:S(2)}, u32[]{:S(2)}) collective-permute-start(bf16[2,384,128]{2,1,0:T(8,128)(2,1)S(1)} %collective-permute-done.16.refs_12_), channel_id=1, source_target_pairs={{0,16},{1,17},{2,18},{3,19},{4,20},{5,21},{6,22},{7,23},{8,24},{9,... | collective-permute-start | bytes 589832 | tf_op jit(solution)/shard_map/while/body/eval_jaxpr/ppermute | solution.py:68
  55.6 6.8 %collective-permute-start.27 = (bf16[2,384,128]{2,1,0:T(8,128)(2,1)S(1)}, bf16[2,384,128]{2,1,0:T(8,128)(2,1)S(1)}, u32[]{:S(2)}, u32[]{:S(2)}) collective-permute-start(bf16[2,384,128]{2,1,0:T(8,128)(2,1)S(1)} %collective-permute-done.26.refs_20_), channel_id=1, source_target_pairs={{0,112},{1,113},{2,114},{3,115},{4,116},{5,117},{6,118},{7,119},{8... | collective-permute-start | bytes 589832 | tf_op jit(solution)/shard_map/while/body/eval_jaxpr/ppermute | solution.py:68
  58.4 13.5 %collective-permute-start.7 = (bf16[4,384,128]{2,1,0:T(8,128)(2,1)S(1)}, bf16[4,384,128]{2,1,0:T(8,128)(2,1)S(1)}, u32[]{:S(2)}, u32[]{:S(2)}) collective-permute-start(bf16[4,384,128]{2,1,0:T(8,128)(2,1)S(1)} %collective-permute-done.5.refs_2_), channel_id=1, source_target_pairs={{0,4},{1,5},{2,6},{3,7},{4,8},{5,9},{6,10},{7,11},{8,12},{9,13},{1... | collective-permute-start | bytes 1179656 | tf_op jit(solution)/shard_map/while/body/eval_jaxpr/ppermute | solution.py:68
  60.5 5.7 %collective-permute-start.23 = (bf16[2,384,128]{2,1,0:T(8,128)(2,1)S(1)}, bf16[2,384,128]{2,1,0:T(8,128)(2,1)S(1)}, u32[]{:S(2)}, u32[]{:S(2)}) collective-permute-start(bf16[2,384,128]{2,1,0:T(8,128)(2,1)S(1)} %collective-permute-done.22.refs_21_), channel_id=1, source_target_pairs={{0,112},{1,113},{2,114},{3,115},{4,116},{5,117},{6,118},{7,119},{8... | collective-permute-start | bytes 589832 | tf_op jit(solution)/shard_map/while/body/eval_jaxpr/ppermute | solution.py:68
  62.0 11.3 %collective-permute-start.9 = (bf16[4,384,128]{2,1,0:T(8,128)(2,1)S(1)}, bf16[4,384,128]{2,1,0:T(8,128)(2,1)S(1)}, u32[]{:S(2)}, u32[]{:S(2)}) collective-permute-start(bf16[4,384,128]{2,1,0:T(8,128)(2,1)S(1)} %collective-permute-done.8.refs_7_), channel_id=1, source_target_pairs={{0,12},{1,13},{2,14},{3,15},{4,0},{5,1},{6,2},{7,3},{8,4},{9,5},{1... | collective-permute-start | bytes 1179656 | tf_op jit(solution)/shard_map/while/body/eval_jaxpr/ppermute | solution.py:68
  62.4 7.3 %collective-permute-start.19 = (bf16[2,384,128]{2,1,0:T(8,128)(2,1)S(1)}, bf16[2,384,128]{2,1,0:T(8,128)(2,1)S(1)}, u32[]{:S(2)}, u32[]{:S(2)}) collective-permute-start(bf16[2,384,128]{2,1,0:T(8,128)(2,1)S(1)} %collective-permute-done.17.refs_13_), channel_id=1, source_target_pairs={{0,16},{1,17},{2,18},{3,19},{4,20},{5,21},{6,22},{7,23},{8,24},{9,... | collective-permute-start | bytes 589832 | tf_op jit(solution)/shard_map/while/body/eval_jaxpr/ppermute | solution.py:68
  63.8 8.0 %collective-permute-start.20 = (bf16[2,384,128]{2,1,0:T(8,128)(2,1)S(1)}, bf16[2,384,128]{2,1,0:T(8,128)(2,1)S(1)}, u32[]{:S(2)}, u32[]{:S(2)}) collective-permute-start(bf16[2,384,128]{2,1,0:T(8,128)(2,1)S(1)} %collective-permute-done.18.refs_14_), channel_id=1, source_target_pairs={{0,16},{1,17},{2,18},{3,19},{4,20},{5,21},{6,22},{7,23},{8,24},{9,... | collective-permute-start | bytes 589832 | tf_op jit(solution)/shard_map/while/body/eval_jaxpr/ppermute | solution.py:68
  66.1 7.2 %collective-permute-start.24 = (bf16[2,384,128]{2,1,0:T(8,128)(2,1)S(1)}, bf16[2,384,128]{2,1,0:T(8,128)(2,1)S(1)}, u32[]{:S(2)}, u32[]{:S(2)}) collective-permute-start(bf16[2,384,128]{2,1,0:T(8,128)(2,1)S(1)} %collective-permute-done.23.refs_19_), channel_id=1, source_target_pairs={{0,112},{1,113},{2,114},{3,115},{4,116},{5,117},{6,118},{7,119},{8... | collective-permute-start | bytes 589832 | tf_op jit(solution)/shard_map/while/body/eval_jaxpr/ppermute | solution.py:68
  80.3 9.3 %collective-permute-start.30 = (f32[384,128]{1,0:T(8,128)}, f32[384,128]{1,0:T(8,128)S(1)}, u32[]{:S(2)}, u32[]{:S(2)}) collective-permute-start(f32[384,128]{1,0:T(8,128)} %get-tuple-element.310), channel_id=1, source_target_pairs={{0,1},{1,0},{2,3},{3,2},{4,5},{5,4},{6,7},{7,6},{8,9},{9,8},{10,11... | collective-permute-start | bytes 589832 | tf_op jit(solution)/shard_map/while/body/eval_jaxpr/ppermute | solution.py:68
  86.0 9.3 %collective-permute-start.28 = (f32[384,128]{1,0:T(8,128)}, f32[384,128]{1,0:T(8,128)S(1)}, u32[]{:S(2)}, u32[]{:S(2)}) collective-permute-start(f32[384,128]{1,0:T(8,128)} %get-tuple-element.307), channel_id=1, source_target_pairs={{0,2},{1,3},{2,0},{3,1},{4,6},{5,7},{6,4},{7,5},{8,10},{9,11},{10,... | collective-permute-start | bytes 589832 | tf_op jit(solution)/shard_map/while/body/eval_jaxpr/ppermute | solution.py:68
  89.4 9.7 %collective-permute-start.29 = (f32[384,128]{1,0:T(8,128)}, f32[384,128]{1,0:T(8,128)S(1)}, u32[]{:S(2)}, u32[]{:S(2)}) collective-permute-start(f32[384,128]{1,0:T(8,128)} %get-tuple-element.308), channel_id=1, source_target_pairs={{0,3},{1,2},{2,1},{3,0},{4,7},{5,6},{6,5},{7,4},{8,11},{9,10},{10,... | collective-permute-start | bytes 589832 | tf_op jit(solution)/shard_map/while/body/eval_jaxpr/ppermute | solution.py:68
  100.7 11.5 %collective-permute-start = (bf16[384,128]{1,0:T(8,128)(2,1)S(1)}, bf16[384,128]{1,0:T(8,128)(2,1)S(1)}, u32[]{:S(2)}, u32[]{:S(2)}) collective-permute-start(bf16[384,128]{1,0:T(8,128)(2,1)S(1)} %get-tuple-element.326), channel_id=1, source_target_pairs={{0,32},{1,48},{2,160},{3,176},{4,36},{5,52},{6,164},{7,180},{8,40}... | collective-permute-start | bytes 294920 | tf_op jit(solution)/shard_map/while/body/eval_jaxpr/ppermute | solution.py:68
  100.7 11.5 %collective-permute-start.1 = (bf16[384,128]{1,0:T(8,128)(2,1)S(1)}, bf16[384,128]{1,0:T(8,128)(2,1)S(1)}, u32[]{:S(2)}, u32[]{:S(2)}) collective-permute-start(bf16[384,128]{1,0:T(8,128)(2,1)S(1)} %get-tuple-element.326), channel_id=1, source_target_pairs={{0,96},{1,112},{2,224},{3,240},{4,100},{5,116},{6,228},{7,244},{8,... | collective-permute-start | bytes 294920 | tf_op jit(solution)/shard_map/while/body/eval_jaxpr/ppermute | solution.py:68
  105.9 9.5 %collective-permute-start.11 = (bf16[384,128]{1,0:T(8,128)(2,1)S(1)}, bf16[384,128]{1,0:T(8,128)(2,1)S(1)}, u32[]{:S(2)}, u32[]{:S(2)}) collective-permute-start(bf16[384,128]{1,0:T(8,128)(2,1)S(1)} %get-tuple-element.326), channel_id=1, source_target_pairs={{0,232},{1,248},{2,104},{3,120},{4,236},{5,252},{6,108},{7,124},{8... | collective-permute-start | bytes 294920 | tf_op jit(solution)/shard_map/while/body/eval_jaxpr/ppermute | solution.py:68
  112.2 5.9 %collective-permute-start.12 = (bf16[384,128]{1,0:T(8,128)(2,1)S(1)}, bf16[384,128]{1,0:T(8,128)(2,1)S(1)}, u32[]{:S(2)}, u32[]{:S(2)}) collective-permute-start(bf16[384,128]{1,0:T(8,128)(2,1)S(1)} %get-tuple-element.326), channel_id=1, source_target_pairs={{0,224},{1,240},{2,96},{3,112},{4,228},{5,244},{6,100},{7,116},{8,... | collective-permute-start | bytes 294920 | tf_op jit(solution)/shard_map/while/body/eval_jaxpr/ppermute | solution.py:68
  112.3 11.6 %collective-permute-start.2 = (bf16[2,384,128]{2,1,0:T(8,128)(2,1)S(1)}, bf16[2,384,128]{2,1,0:T(8,128)(2,1)S(1)}, u32[]{:S(2)}, u32[]{:S(2)}) collective-permute-start(bf16[2,384,128]{2,1,0:T(8,128)(2,1)S(1)} %pad_maximum_fusion.6), channel_id=1, source_target_pairs={{0,16},{1,17},{2,18},{3,19},{4,20},{5,21},{6,22},{7,23},{8,24},{9,... | collective-permute-start | bytes 589832 | tf_op jit(solution)/shard_map/while/body/eval_jaxpr/ppermute | solution.py:68
  118.1 51.3 %copy-start.2 = (bf16[2,384,128]{2,1,0:T(8,128)(2,1)}, bf16[2,384,128]{2,1,0:T(8,128)(2,1)S(1)}, u32[]{:S(2)}) copy-start(bf16[2,384,128]{2,1,0:T(8,128)(2,1)S(1)} %pad_maximum_fusion.8.refs_8_) | copy-start | bytes 589828 | tf_op jit(solution)/shard_map/while
  118.1 7.0 %collective-permute-start.13 = (bf16[2,384,128]{2,1,0:T(8,128)(2,1)S(1)}, bf16[2,384,128]{2,1,0:T(8,128)(2,1)S(1)}, u32[]{:S(2)}, u32[]{:S(2)}) collective-permute-start(bf16[2,384,128]{2,1,0:T(8,128)(2,1)S(1)} %pad_maximum_fusion.8.refs_8_), channel_id=1, source_target_pairs={{0,4},{1,5},{2,6},{3,7},{4,8},{5,9},{6,10},{7,11},{8,12},{9,13},{1... | collective-permute-start | bytes 589832 | tf_op jit(solution)/shard_map/while/body/eval_jaxpr/ppermute | solution.py:68
  118.2 8.9 %collective-permute-start.3 = (bf16[2,384,128]{2,1,0:T(8,128)(2,1)S(1)}, bf16[2,384,128]{2,1,0:T(8,128)(2,1)S(1)}, u32[]{:S(2)}, u32[]{:S(2)}) collective-permute-start(bf16[2,384,128]{2,1,0:T(8,128)(2,1)S(1)} %pad_maximum_fusion.6), channel_id=1, source_target_pairs={{0,112},{1,113},{2,114},{3,115},{4,116},{5,117},{6,118},{7,119},{8... | collective-permute-start | bytes 589832 | tf_op jit(solution)/shard_map/while/body/eval_jaxpr/ppermute | solution.py:68
  120.6 8.6 %collective-permute-start.14 = (bf16[2,384,128]{2,1,0:T(8,128)(2,1)S(1)}, bf16[2,384,128]{2,1,0:T(8,128)(2,1)S(1)}, u32[]{:S(2)}, u32[]{:S(2)}) collective-permute-start(bf16[2,384,128]{2,1,0:T(8,128)(2,1)S(1)} %pad_maximum_fusion.8.refs_8_), channel_id=1, source_target_pairs={{0,16},{1,17},{2,18},{3,19},{4,20},{5,21},{6,22},{7,23},{8,24},{9,... | collective-permute-start | bytes 589832 | tf_op jit(solution)/shard_map/while/body/eval_jaxpr/ppermute | solution.py:68
  120.6 9.7 %collective-permute-start.25 = (bf16[2,384,128]{2,1,0:T(8,128)(2,1)S(1)}, bf16[2,384,128]{2,1,0:T(8,128)(2,1)S(1)}, u32[]{:S(2)}, u32[]{:S(2)}) collective-permute-start(bf16[2,384,128]{2,1,0:T(8,128)(2,1)S(1)} %pad_maximum_fusion.8.refs_8_), channel_id=1, source_target_pairs={{0,112},{1,113},{2,114},{3,115},{4,116},{5,117},{6,118},{7,119},{8... | collective-permute-start | bytes 589832 | tf_op jit(solution)/shard_map/while/body/eval_jaxpr/ppermute | solution.py:68
  123.8 8.0 %collective-permute-start.4 = (bf16[2,384,128]{2,1,0:T(8,128)(2,1)S(1)}, bf16[2,384,128]{2,1,0:T(8,128)(2,1)S(1)}, u32[]{:S(2)}, u32[]{:S(2)}) collective-permute-start(bf16[2,384,128]{2,1,0:T(8,128)(2,1)S(1)} %collective-permute-done.2), channel_id=1, source_target_pairs={{0,16},{1,17},{2,18},{3,19},{4,20},{5,21},{6,22},{7,23},{8,24},{9,... | collective-permute-start | bytes 589832 | tf_op jit(solution)/shard_map/while/body/eval_jaxpr/ppermute | solution.py:68
  125.1 9.0 %collective-permute-start.21 = (bf16[2,384,128]{2,1,0:T(8,128)(2,1)S(1)}, bf16[2,384,128]{2,1,0:T(8,128)(2,1)S(1)}, u32[]{:S(2)}, u32[]{:S(2)}) collective-permute-start(bf16[2,384,128]{2,1,0:T(8,128)(2,1)S(1)} %collective-permute-done.13.refs_9_), channel_id=1, source_target_pairs={{0,112},{1,113},{2,114},{3,115},{4,116},{5,117},{6,118},{7,119},{8... | collective-permute-start | bytes 589832 | tf_op jit(solution)/shard_map/while/body/eval_jaxpr/ppermute | solution.py:68
  127.1 18.3 %collective-permute-start.5 = (bf16[4,384,128]{2,1,0:T(8,128)(2,1)S(1)}, bf16[4,384,128]{2,1,0:T(8,128)(2,1)S(1)}, u32[]{:S(2)}, u32[]{:S(2)}) collective-permute-start(bf16[4,384,128]{2,1,0:T(8,128)(2,1)S(1)} %pad_maximum_fusion.7.refs_0_), channel_id=1, source_target_pairs={{0,4},{1,5},{2,6},{3,7},{4,8},{5,9},{6,10},{7,11},{8,12},{9,13},{1... | collective-permute-start | bytes 1179656 | tf_op jit(solution)/shard_map/while/body/eval_jaxpr/ppermute | solution.py:68
  129.2 18.0 %collective-permute-start.10 = (bf16[4,384,128]{2,1,0:T(8,128)(2,1)S(1)}, bf16[4,384,128]{2,1,0:T(8,128)(2,1)S(1)}, u32[]{:S(2)}, u32[]{:S(2)}) collective-permute-start(bf16[4,384,128]{2,1,0:T(8,128)(2,1)S(1)} %pad_maximum_fusion.7.refs_0_), channel_id=1, source_target_pairs={{0,12},{1,13},{2,14},{3,15},{4,0},{5,1},{6,2},{7,3},{8,4},{9,5},{1... | collective-permute-start | bytes 1179656 | tf_op jit(solution)/shard_map/while/body/eval_jaxpr/ppermute | solution.py:68
  130.3 9.0 %collective-permute-start.15 = (bf16[2,384,128]{2,1,0:T(8,128)(2,1)S(1)}, bf16[2,384,128]{2,1,0:T(8,128)(2,1)S(1)}, u32[]{:S(2)}, u32[]{:S(2)}) collective-permute-start(bf16[2,384,128]{2,1,0:T(8,128)(2,1)S(1)} %collective-permute-done.13.refs_9_), channel_id=1, source_target_pairs={{0,16},{1,17},{2,18},{3,19},{4,20},{5,21},{6,22},{7,23},{8,24},{9,... | collective-permute-start | bytes 589832 | tf_op jit(solution)/shard_map/while/body/eval_jaxpr/ppermute | solution.py:68
  131.9 11.0 %collective-permute-start.16 = (bf16[2,384,128]{2,1,0:T(8,128)(2,1)S(1)}, bf16[2,384,128]{2,1,0:T(8,128)(2,1)S(1)}, u32[]{:S(2)}, u32[]{:S(2)}) collective-permute-start(bf16[2,384,128]{2,1,0:T(8,128)(2,1)S(1)} %collective-permute-done.14.refs_10_), channel_id=1, source_target_pairs={{0,16},{1,17},{2,18},{3,19},{4,20},{5,21},{6,22},{7,23},{8,24},{9,... | collective-permute-start | bytes 589832 | tf_op jit(solution)/shard_map/while/body/eval_jaxpr/ppermute | solution.py:68
  134.2 11.0 %collective-permute-start.26 = (bf16[2,384,128]{2,1,0:T(8,128)(2,1)S(1)}, bf16[2,384,128]{2,1,0:T(8,128)(2,1)S(1)}, u32[]{:S(2)}, u32[]{:S(2)}) collective-permute-start(bf16[2,384,128]{2,1,0:T(8,128)(2,1)S(1)} %collective-permute-done.25.refs_22_), channel_id=1, source_target_pairs={{0,112},{1,113},{2,114},{3,115},{4,116},{5,117},{6,118},{7,119},{8... | collective-permute-start | bytes 589832 | tf_op jit(solution)/shard_map/while/body/eval_jaxpr/ppermute | solution.py:68
  139.3 18.0 %collective-permute-start.8 = (bf16[4,384,128]{2,1,0:T(8,128)(2,1)S(1)}, bf16[4,384,128]{2,1,0:T(8,128)(2,1)S(1)}, u32[]{:S(2)}, u32[]{:S(2)}) collective-permute-start(bf16[4,384,128]{2,1,0:T(8,128)(2,1)S(1)} %constant_dynamic-update-slice_fusion.5.refs_1_), channel_id=1, source_target_pairs={{0,12},{1,13},{2,14},{3,15},{4,0},{5,1},{6,2},{7,3},{8,4},{9,5},{1... | collective-permute-start | bytes 1179656 | tf_op jit(solution)/shard_map/while/body/eval_jaxpr/ppermute | solution.py:68
  142.9 16.6 %collective-permute-start.6 = (bf16[4,384,128]{2,1,0:T(8,128)(2,1)S(1)}, bf16[4,384,128]{2,1,0:T(8,128)(2,1)S(1)}, u32[]{:S(2)}, u32[]{:S(2)}) collective-permute-start(bf16[4,384,128]{2,1,0:T(8,128)(2,1)S(1)} %constant_dynamic-update-slice_fusion.5.refs_1_), channel_id=1, source_target_pairs={{0,4},{1,5},{2,6},{3,7},{4,8},{5,9},{6,10},{7,11},{8,12},{9,13},{1... | collective-permute-start | bytes 1179656 | tf_op jit(solution)/shard_map/while/body/eval_jaxpr/ppermute | solution.py:68
  145.2 6.6 %collective-permute-start.22 = (bf16[2,384,128]{2,1,0:T(8,128)(2,1)S(1)}, bf16[2,384,128]{2,1,0:T(8,128)(2,1)S(1)}, u32[]{:S(2)}, u32[]{:S(2)}) collective-permute-start(bf16[2,384,128]{2,1,0:T(8,128)(2,1)S(1)} %collective-permute-done.21.refs_23_), channel_id=1, source_target_pairs={{0,112},{1,113},{2,114},{3,115},{4,116},{5,117},{6,118},{7,119},{8... | collective-permute-start | bytes 589832 | tf_op jit(solution)/shard_map/while/body/eval_jaxpr/ppermute | solution.py:68
  145.5 9.0 %collective-permute-start.17 = (bf16[2,384,128]{2,1,0:T(8,128)(2,1)S(1)}, bf16[2,384,128]{2,1,0:T(8,128)(2,1)S(1)}, u32[]{:S(2)}, u32[]{:S(2)}) collective-permute-start(bf16[2,384,128]{2,1,0:T(8,128)(2,1)S(1)} %collective-permute-done.15.refs_11_), channel_id=1, source_target_pairs={{0,16},{1,17},{2,18},{3,19},{4,20},{5,21},{6,22},{7,23},{8,24},{9,... | collective-permute-start | bytes 589832 | tf_op jit(solution)/shard_map/while/body/eval_jaxpr/ppermute | solution.py:68
  147.2 10.1 %collective-permute-start.18 = (bf16[2,384,128]{2,1,0:T(8,128)(2,1)S(1)}, bf16[2,384,128]{2,1,0:T(8,128)(2,1)S(1)}, u32[]{:S(2)}, u32[]{:S(2)}) collective-permute-start(bf16[2,384,128]{2,1,0:T(8,128)(2,1)S(1)} %collective-permute-done.16.refs_12_), channel_id=1, source_target_pairs={{0,16},{1,17},{2,18},{3,19},{4,20},{5,21},{6,22},{7,23},{8,24},{9,... | collective-permute-start | bytes 589832 | tf_op jit(solution)/shard_map/while/body/eval_jaxpr/ppermute | solution.py:68
  151.8 5.8 %collective-permute-start.27 = (bf16[2,384,128]{2,1,0:T(8,128)(2,1)S(1)}, bf16[2,384,128]{2,1,0:T(8,128)(2,1)S(1)}, u32[]{:S(2)}, u32[]{:S(2)}) collective-permute-start(bf16[2,384,128]{2,1,0:T(8,128)(2,1)S(1)} %collective-permute-done.26.refs_20_), channel_id=1, source_target_pairs={{0,112},{1,113},{2,114},{3,115},{4,116},{5,117},{6,118},{7,119},{8... | collective-permute-start | bytes 589832 | tf_op jit(solution)/shard_map/while/body/eval_jaxpr/ppermute | solution.py:68
  154.4 14.1 %collective-permute-start.7 = (bf16[4,384,128]{2,1,0:T(8,128)(2,1)S(1)}, bf16[4,384,128]{2,1,0:T(8,128)(2,1)S(1)}, u32[]{:S(2)}, u32[]{:S(2)}) collective-permute-start(bf16[4,384,128]{2,1,0:T(8,128)(2,1)S(1)} %collective-permute-done.5.refs_2_), channel_id=1, source_target_pairs={{0,4},{1,5},{2,6},{3,7},{4,8},{5,9},{6,10},{7,11},{8,12},{9,13},{1... | collective-permute-start | bytes 1179656 | tf_op jit(solution)/shard_map/while/body/eval_jaxpr/ppermute | solution.py:68
  157.3 5.7 %collective-permute-start.23 = (bf16[2,384,128]{2,1,0:T(8,128)(2,1)S(1)}, bf16[2,384,128]{2,1,0:T(8,128)(2,1)S(1)}, u32[]{:S(2)}, u32[]{:S(2)}) collective-permute-start(bf16[2,384,128]{2,1,0:T(8,128)(2,1)S(1)} %collective-permute-done.22.refs_21_), channel_id=1, source_target_pairs={{0,112},{1,113},{2,114},{3,115},{4,116},{5,117},{6,118},{7,119},{8... | collective-permute-start | bytes 589832 | tf_op jit(solution)/shard_map/while/body/eval_jaxpr/ppermute | solution.py:68
  157.4 11.3 %collective-permute-start.9 = (bf16[4,384,128]{2,1,0:T(8,128)(2,1)S(1)}, bf16[4,384,128]{2,1,0:T(8,128)(2,1)S(1)}, u32[]{:S(2)}, u32[]{:S(2)}) collective-permute-start(bf16[4,384,128]{2,1,0:T(8,128)(2,1)S(1)} %collective-permute-done.8.refs_7_), channel_id=1, source_target_pairs={{0,12},{1,13},{2,14},{3,15},{4,0},{5,1},{6,2},{7,3},{8,4},{9,5},{1... | collective-permute-start | bytes 1179656 | tf_op jit(solution)/shard_map/while/body/eval_jaxpr/ppermute | solution.py:68
  157.6 8.9 %collective-permute-start.19 = (bf16[2,384,128]{2,1,0:T(8,128)(2,1)S(1)}, bf16[2,384,128]{2,1,0:T(8,128)(2,1)S(1)}, u32[]{:S(2)}, u32[]{:S(2)}) collective-permute-start(bf16[2,384,128]{2,1,0:T(8,128)(2,1)S(1)} %collective-permute-done.17.refs_13_), channel_id=1, source_target_pairs={{0,16},{1,17},{2,18},{3,19},{4,20},{5,21},{6,22},{7,23},{8,24},{9,... | collective-permute-start | bytes 589832 | tf_op jit(solution)/shard_map/while/body/eval_jaxpr/ppermute | solution.py:68
  159.5 9.0 %collective-permute-start.20 = (bf16[2,384,128]{2,1,0:T(8,128)(2,1)S(1)}, bf16[2,384,128]{2,1,0:T(8,128)(2,1)S(1)}, u32[]{:S(2)}, u32[]{:S(2)}) collective-permute-start(bf16[2,384,128]{2,1,0:T(8,128)(2,1)S(1)} %collective-permute-done.18.refs_14_), channel_id=1, source_target_pairs={{0,16},{1,17},{2,18},{3,19},{4,20},{5,21},{6,22},{7,23},{8,24},{9,... | collective-permute-start | bytes 589832 | tf_op jit(solution)/shard_map/while/body/eval_jaxpr/ppermute | solution.py:68
  163.0 5.7 %collective-permute-start.24 = (bf16[2,384,128]{2,1,0:T(8,128)(2,1)S(1)}, bf16[2,384,128]{2,1,0:T(8,128)(2,1)S(1)}, u32[]{:S(2)}, u32[]{:S(2)}) collective-permute-start(bf16[2,384,128]{2,1,0:T(8,128)(2,1)S(1)} %collective-permute-done.23.refs_19_), channel_id=1, source_target_pairs={{0,112},{1,113},{2,114},{3,115},{4,116},{5,117},{6,118},{7,119},{8... | collective-permute-start | bytes 589832 | tf_op jit(solution)/shard_map/while/body/eval_jaxpr/ppermute | solution.py:68
  175.8 7.7 %collective-permute-start.30 = (f32[384,128]{1,0:T(8,128)}, f32[384,128]{1,0:T(8,128)S(1)}, u32[]{:S(2)}, u32[]{:S(2)}) collective-permute-start(f32[384,128]{1,0:T(8,128)} %get-tuple-element.310), channel_id=1, source_target_pairs={{0,1},{1,0},{2,3},{3,2},{4,5},{5,4},{6,7},{7,6},{8,9},{9,8},{10,11... | collective-permute-start | bytes 589832 | tf_op jit(solution)/shard_map/while/body/eval_jaxpr/ppermute | solution.py:68
  181.5 8.1 %collective-permute-start.28 = (f32[384,128]{1,0:T(8,128)}, f32[384,128]{1,0:T(8,128)S(1)}, u32[]{:S(2)}, u32[]{:S(2)}) collective-permute-start(f32[384,128]{1,0:T(8,128)} %get-tuple-element.307), channel_id=1, source_target_pairs={{0,2},{1,3},{2,0},{3,1},{4,6},{5,7},{6,4},{7,5},{8,10},{9,11},{10,... | collective-permute-start | bytes 589832 | tf_op jit(solution)/shard_map/while/body/eval_jaxpr/ppermute | solution.py:68
  181.6 11.2 %collective-permute-start.29 = (f32[384,128]{1,0:T(8,128)}, f32[384,128]{1,0:T(8,128)S(1)}, u32[]{:S(2)}, u32[]{:S(2)}) collective-permute-start(f32[384,128]{1,0:T(8,128)} %get-tuple-element.308), channel_id=1, source_target_pairs={{0,3},{1,2},{2,1},{3,0},{4,7},{5,6},{6,5},{7,4},{8,11},{9,10},{10,... | collective-permute-start | bytes 589832 | tf_op jit(solution)/shard_map/while/body/eval_jaxpr/ppermute | solution.py:68
  (61 other events, 1080.2 us)

commit v2 on v1

--- a/solution.py
+++ b/solution.py
@@ -113,7 +113,7 @@
     def _():
         for k in order:
             for t, js in enumerate((EVEN, ODD)):
-                for i, j in enumerate(js):
+                for i, j in enumerate(js[::-1] if t and k > 3 else js):
                     piece(zb[2 * k + t].at[i], k, j)
 
     for v in range(1, 4):
@@ -160,7 +160,10 @@
     one = jnp.stack([send(piece, swap(0, 0, 0)), send(piece, swap(0, 4, 0))])
     even, odd = [two] + [None] * 7, [send(two, along_x(1))] + [None] * 7
     for k in range(1, 4):
-        for rows in (even, odd):
+        for name, rows in (("e", even), ("o", odd)):
+            if name == "o" and k == 1:
+                rows[1], rows[7] = send(even[1], along_x(1)), send(even[7], along_x(3))
+                continue
             rows[k] = send(rows[k - 1], along_z(1))
             rows[8 - k] = send(rows[(9 - k) % 8], along_z(7))
     even[4] = send(even[3], along_z(1))

time: 196 us -> 205 us (1.046)
  waiting for transfers between devices: 64.6 us -> 84.4 us
  starting transfers between devices: 96.8 us -> 84.6 us
    ppermute x62, waiting for transfers between devices: 64.6 us -> 84.4 us  [send(): return lax.ppermute(value, BOTH, perm)]
    ppermute x62, starting transfers between devices: 96.8 us -> 84.6 us  [send(): return lax.ppermute(value, BOTH, perm)]
where the time goes in v2:
time: 205 us; the launch traced here: 202 us
  starting transfers between devices  84.6 us (41%)
  waiting for transfers between devices  84.4 us (41%)
  Pallas kernels  22.2 us (11%)
  local copies, waits for them, and re-layouts  7.7 us (4%)
    ppermute x62, starting transfers between devices, send(): return lax.ppermute(value, BOTH, perm)  84.6 us
    ppermute x62, waiting for transfers between devices, send(): return lax.ppermute(value, BOTH, perm)  84.4 us
    pallas_call x4, Pallas kernels, product(): pl.pallas_call(functools.partial(product_kernel, home_half=home_half), ou...  22.2 us
    while x126, local copies, waits for them, and re-layouts  4.23 us
  transfers between devices with their start and end apart: 62, of which 32 were waited for; matrix products, arithmetic and copies ran while one was open for 0% of the time, Pallas kernels for 6%

profile of v2, /device:TPU:2, one launch (start us, length us, event | category | flops | bytes accessed | tf_op | source)
XLA Modules:
  0.0 202.0 jit_solution(16588852181891015914)
XLA Ops:
  3.8 198.2 %while.17 = (s32[]{:T(128)}, bf16[384,128]{1,0:T(8,128)(2,1)S(1)}, f32[2,384,128]{2,1,0:T(8,128)}, f32[2,384,128]{2,1,0:T(8,128)}, f32[2,384,128]{2,1,0:T(8,128)...) while((s32[]{:T(128)}, bf16[384,128]{1,0:T(8,128)(2,1)S(1)}, ...), condition=%wide.region_1.2_spmd, body=%wide.region_0.1_spmd.sunk | while | flops 151928832 | bytes 68913392 | solution.py:202
  3.8 3.3 %collective-permute-start = (bf16[384,128]{1,0:T(8,128)(2,1)S(1)}, bf16[384,128]{1,0:T(8,128)(2,1)S(1)}, u32[]{:S(2)}, u32[]{:S(2)}) collective-permute-start(bf16[384,128]{1,0:T(8,128)(2,1)S(1)} %get-tuple-element.326), channel_id=1, source_target_pairs={{0,32},{1,48},{2,160},{3,176},{4,36},{5,52},{6,164},{7,180},{8,40}... | collective-permute-start | bytes 294920 | tf_op jit(solution)/shard_map/while/body/eval_jaxpr/ppermute | solution.py:68
  7.0 4.9 %collective-permute-start.1 = (bf16[384,128]{1,0:T(8,128)(2,1)S(1)}, bf16[384,128]{1,0:T(8,128)(2,1)S(1)}, u32[]{:S(2)}, u32[]{:S(2)}) collective-permute-start(bf16[384,128]{1,0:T(8,128)(2,1)S(1)} %get-tuple-element.326), channel_id=1, source_target_pairs={{0,96},{1,112},{2,224},{3,240},{4,100},{5,116},{6,228},{7,244},{8,... | collective-permute-start | bytes 294920 | tf_op jit(solution)/shard_map/while/body/eval_jaxpr/ppermute | solution.py:68
  12.0 5.9 %collective-permute-start.11 = (bf16[384,128]{1,0:T(8,128)(2,1)S(1)}, bf16[384,128]{1,0:T(8,128)(2,1)S(1)}, u32[]{:S(2)}, u32[]{:S(2)}) collective-permute-start(bf16[384,128]{1,0:T(8,128)(2,1)S(1)} %get-tuple-element.326), channel_id=1, source_target_pairs={{0,232},{1,248},{2,104},{3,120},{4,236},{5,252},{6,108},{7,124},{8... | collective-permute-start | bytes 294920 | tf_op jit(solution)/shard_map/while/body/eval_jaxpr/ppermute | solution.py:68
  19.7 1.4 collective-permute-done.11
  21.1 2.6 %collective-permute-done.12 = bf16[384,128]{1,0:T(8,128)(2,1)S(1)} collective-permute-done((bf16[384,128]{1,0:T(8,128)(2,1)S(1)}, bf16[384,128]{1,0:T(8,128)(2,1)S(1)}, u32[]{:S(2)}, u32[]{:S(2)}) %collective-permute-start.12) | collective-permute-done | bytes 98336 | tf_op jit(solution)/shard_map/while/body/eval_jaxpr/ppermute | solution.py:68
  23.7 3.9 %collective-permute-start.21 = (bf16[2,384,128]{2,1,0:T(8,128)(2,1)S(1)}, bf16[2,384,128]{2,1,0:T(8,128)(2,1)S(1)}, u32[]{:S(2)}, u32[]{:S(2)}) collective-permute-start(bf16[2,384,128]{2,1,0:T(8,128)(2,1)S(1)} %pad_maximum_fusion.8.refs_8_), channel_id=1, source_target_pairs={{0,112},{1,113},{2,114},{3,115},{4,116},{5,117},{6,118},{7,119},{8... | collective-permute-start | bytes 589832 | tf_op jit(solution)/shard_map/while/body/eval_jaxpr/ppermute | solution.py:68
  27.9 1.7 collective-permute-start.14
  31.0 1.9 collective-permute-done.21.refs_22_
  32.9 1.4 collective-permute-start.22
  34.4 1.3 collective-permute-done.3
  35.7 1.2 collective-permute-done.14.refs_10_
  36.8 1.4 collective-permute-start.10
  38.9 1.7 collective-permute-done.4
  40.6 3.6 %collective-permute-start.26 = (bf16[2,384,128]{2,1,0:T(8,128)(2,1)S(1)}, bf16[2,384,128]{2,1,0:T(8,128)(2,1)S(1)}, u32[]{:S(2)}, u32[]{:S(2)}) collective-permute-start(bf16[2,384,128]{2,1,0:T(8,128)(2,1)S(1)} %collective-permute-done.21.refs_22_), channel_id=1, source_target_pairs={{0,112},{1,113},{2,114},{3,115},{4,116},{5,117},{6,118},{7,119},{8... | collective-permute-start | bytes 589832 | tf_op jit(solution)/shard_map/while/body/eval_jaxpr/ppermute | solution.py:68
  44.3 6.9 %collective-permute-done.15.refs_11_ = bf16[2,384,128]{2,1,0:T(8,128)(2,1)S(1)} collective-permute-done((bf16[2,384,128]{2,1,0:T(8,128)(2,1)S(1)}, bf16[2,384,128]{2,1,0:T(8,128)(2,1)S(1)}, u32[]{:S(2)}, u32[]{:S(2)}) %collective-permute-start.15) | collective-permute-done | bytes 196640 | tf_op jit(solution)/shard_map/while/body/eval_jaxpr/ppermute | solution.py:68
  51.1 2.4 %collective-permute-start.8 = (bf16[4,384,128]{2,1,0:T(8,128)(2,1)S(1)}, bf16[4,384,128]{2,1,0:T(8,128)(2,1)S(1)}, u32[]{:S(2)}, u32[]{:S(2)}) collective-permute-start(bf16[4,384,128]{2,1,0:T(8,128)(2,1)S(1)} %constant_dynamic-update-slice_fusion.5.refs_1_), channel_id=1, source_target_pairs={{0,12},{1,13},{2,14},{3,15},{4,0},{5,1},{6,2},{7,3},{8,4},{9,5},{1... | collective-permute-start | bytes 1179656 | tf_op jit(solution)/shard_map/while/body/eval_jaxpr/ppermute | solution.py:68
  53.5 2.0 %collective-permute-start.23 = (bf16[2,384,128]{2,1,0:T(8,128)(2,1)S(1)}, bf16[2,384,128]{2,1,0:T(8,128)(2,1)S(1)}, u32[]{:S(2)}, u32[]{:S(2)}) collective-permute-start(bf16[2,384,128]{2,1,0:T(8,128)(2,1)S(1)} %collective-permute-done.22.refs_23_), channel_id=1, source_target_pairs={{0,112},{1,113},{2,114},{3,115},{4,116},{5,117},{6,118},{7,119},{8... | collective-permute-start | bytes 589832 | tf_op jit(solution)/shard_map/while/body/eval_jaxpr/ppermute | solution.py:68
  55.6 1.6 collective-permute-start.18
  57.3 2.3 %collective-permute-done.23.refs_21_ = bf16[2,384,128]{2,1,0:T(8,128)(2,1)S(1)} collective-permute-done((bf16[2,384,128]{2,1,0:T(8,128)(2,1)S(1)}, bf16[2,384,128]{2,1,0:T(8,128)(2,1)S(1)}, u32[]{:S(2)}, u32[]{:S(2)}) %collective-permute-start.23) | collective-permute-done | bytes 196640 | tf_op jit(solution)/shard_map/while/body/eval_jaxpr/ppermute | solution.py:68
  59.5 2.9 %collective-permute-start.27 = (bf16[2,384,128]{2,1,0:T(8,128)(2,1)S(1)}, bf16[2,384,128]{2,1,0:T(8,128)(2,1)S(1)}, u32[]{:S(2)}, u32[]{:S(2)}) collective-permute-start(bf16[2,384,128]{2,1,0:T(8,128)(2,1)S(1)} %collective-permute-done.26.refs_20_), channel_id=1, source_target_pairs={{0,112},{1,113},{2,114},{3,115},{4,116},{5,117},{6,118},{7,119},{8... | collective-permute-start | bytes 589832 | tf_op jit(solution)/shard_map/while/body/eval_jaxpr/ppermute | solution.py:68
  62.5 1.5 collective-permute-done.17.refs_13_
  63.9 2.1 %collective-permute-done.18.refs_14_ = bf16[2,384,128]{2,1,0:T(8,128)(2,1)S(1)} collective-permute-done((bf16[2,384,128]{2,1,0:T(8,128)(2,1)S(1)}, bf16[2,384,128]{2,1,0:T(8,128)(2,1)S(1)}, u32[]{:S(2)}, u32[]{:S(2)}) %collective-permute-start.18) | collective-permute-done | bytes 196640 | tf_op jit(solution)/shard_map/while/body/eval_jaxpr/ppermute | solution.py:68
  66.0 1.7 collective-permute-start.24
  67.8 1.6 collective-permute-start.9
  70.1 2.5 %collective-permute-done.24.refs_19_ = bf16[2,384,128]{2,1,0:T(8,128)(2,1)S(1)} collective-permute-done((bf16[2,384,128]{2,1,0:T(8,128)(2,1)S(1)}, bf16[2,384,128]{2,1,0:T(8,128)(2,1)S(1)}, u32[]{:S(2)}, u32[]{:S(2)}) %collective-permute-start.24) | collective-permute-done | bytes 196640 | tf_op jit(solution)/shard_map/while/body/eval_jaxpr/ppermute | solution.py:68
  72.6 2.1 %collective-permute-start.25 = (bf16[2,384,128]{2,1,0:T(8,128)(2,1)S(1)}, bf16[2,384,128]{2,1,0:T(8,128)(2,1)S(1)}, u32[]{:S(2)}, u32[]{:S(2)}) collective-permute-start(bf16[2,384,128]{2,1,0:T(8,128)(2,1)S(1)} %collective-permute-done.24.refs_19_), channel_id=1, source_target_pairs={{0,112},{1,113},{2,114},{3,115},{4,116},{5,117},{6,118},{7,119},{8... | collective-permute-start | bytes 589832 | tf_op jit(solution)/shard_map/while/body/eval_jaxpr/ppermute | solution.py:68
  74.7 2.0 collective-permute-done.19.refs_15_
  76.7 2.1 %collective-permute-done.20.refs_16_ = bf16[2,384,128]{2,1,0:T(8,128)(2,1)S(1)} collective-permute-done((bf16[2,384,128]{2,1,0:T(8,128)(2,1)S(1)}, bf16[2,384,128]{2,1,0:T(8,128)(2,1)S(1)}, u32[]{:S(2)}, u32[]{:S(2)}) %collective-permute-start.20) | collective-permute-done | bytes 196640 | tf_op jit(solution)/shard_map/while/body/eval_jaxpr/ppermute | solution.py:68
  80.3 5.5 %eval_jaxpr.17 = (f32[384,128]{1,0:T(8,128)}, f32[384,128]{1,0:T(8,128)}) custom-call(s32[4]{0:T(128)S(1)} %get-tuple-element.343.place, s32[1]{0:T(128)} %bitcast.59.sweep, bf16[2,384,6144]{2,1,0:T(8,128)(2,1)} %get-tuple-element.344.factors, bf16[4,384,128]{2,1,0:T(8,128)(2,1)} %copy-done, bf16[4,384,128]{2,1,0:T(8,128)(2,1)} %copy-done.1, ...), custom_call_target="tpu_custom_call" | custom-call | tf_op jit(solution)/shard_map/while/body/eval_jaxpr/pallas_call | solution.py:142
  86.0 5.6 %eval_jaxpr.16 = (f32[384,128]{1,0:T(8,128)}, f32[384,128]{1,0:T(8,128)}) custom-call(s32[4]{0:T(128)S(1)} %get-tuple-element.343.place, s32[1]{0:T(128)} %bitcast.59.sweep, bf16[2,384,6144]{2,1,0:T(8,128)(2,1)} %get-tuple-element.344.factors, bf16[4,384,128]{2,1,0:T(8,128)(2,1)} %copy-done, bf16[4,384,128]{2,1,0:T(8,128)(2,1)} %copy-done.1, ...), custom_call_target="tpu_custom_call" | custom-call | tf_op jit(solution)/shard_map/while/body/eval_jaxpr/pallas_call | solution.py:142
  91.6 2.9 %collective-permute-start.28 = (f32[384,128]{1,0:T(8,128)}, f32[384,128]{1,0:T(8,128)S(1)}, u32[]{:S(2)}, u32[]{:S(2)}) collective-permute-start(f32[384,128]{1,0:T(8,128)} %get-tuple-element.307), channel_id=1, source_target_pairs={{0,2},{1,3},{2,0},{3,1},{4,6},{5,7},{6,4},{7,5},{8,10},{9,11},{10,... | collective-permute-start | bytes 589832 | tf_op jit(solution)/shard_map/while/body/eval_jaxpr/ppermute | solution.py:68
  94.7 5.7 %collective-permute-done.28 = f32[384,128]{1,0:T(8,128)S(1)} collective-permute-done((f32[384,128]{1,0:T(8,128)}, f32[384,128]{1,0:T(8,128)S(1)}, u32[]{:S(2)}, u32[]{:S(2)}) %collective-permute-start.28) | collective-permute-done | bytes 196640 | tf_op jit(solution)/shard_map/while/body/eval_jaxpr/ppermute | solution.py:68
  100.4 3.8 %collective-permute-done.29 = f32[384,128]{1,0:T(8,128)S(1)} collective-permute-done((f32[384,128]{1,0:T(8,128)}, f32[384,128]{1,0:T(8,128)S(1)}, u32[]{:S(2)}, u32[]{:S(2)}) %collective-permute-start.29) | collective-permute-done | bytes 196640 | tf_op jit(solution)/shard_map/while/body/eval_jaxpr/ppermute | solution.py:68
  105.7 3.7 %collective-permute-start.1 = (bf16[384,128]{1,0:T(8,128)(2,1)S(1)}, bf16[384,128]{1,0:T(8,128)(2,1)S(1)}, u32[]{:S(2)}, u32[]{:S(2)}) collective-permute-start(bf16[384,128]{1,0:T(8,128)(2,1)S(1)} %get-tuple-element.326), channel_id=1, source_target_pairs={{0,96},{1,112},{2,224},{3,240},{4,100},{5,116},{6,228},{7,244},{8,... | collective-permute-start | bytes 294920 | tf_op jit(solution)/shard_map/while/body/eval_jaxpr/ppermute | solution.py:68
  109.5 6.6 %collective-permute-start.11 = (bf16[384,128]{1,0:T(8,128)(2,1)S(1)}, bf16[384,128]{1,0:T(8,128)(2,1)S(1)}, u32[]{:S(2)}, u32[]{:S(2)}) collective-permute-start(bf16[384,128]{1,0:T(8,128)(2,1)S(1)} %get-tuple-element.326), channel_id=1, source_target_pairs={{0,232},{1,248},{2,104},{3,120},{4,236},{5,252},{6,108},{7,124},{8... | collective-permute-start | bytes 294920 | tf_op jit(solution)/shard_map/while/body/eval_jaxpr/ppermute | solution.py:68
  116.1 1.4 collective-permute-start.2
  117.5 1.7 collective-permute-done.11
  119.2 2.9 %collective-permute-done.12 = bf16[384,128]{1,0:T(8,128)(2,1)S(1)} collective-permute-done((bf16[384,128]{1,0:T(8,128)(2,1)S(1)}, bf16[384,128]{1,0:T(8,128)(2,1)S(1)}, u32[]{:S(2)}, u32[]{:S(2)}) %collective-permute-start.12) | collective-permute-done | bytes 98336 | tf_op jit(solution)/shard_map/while/body/eval_jaxpr/ppermute | solution.py:68
  122.2 2.3 %collective-permute-start.21 = (bf16[2,384,128]{2,1,0:T(8,128)(2,1)S(1)}, bf16[2,384,128]{2,1,0:T(8,128)(2,1)S(1)}, u32[]{:S(2)}, u32[]{:S(2)}) collective-permute-start(bf16[2,384,128]{2,1,0:T(8,128)(2,1)S(1)} %pad_maximum_fusion.8.refs_8_), channel_id=1, source_target_pairs={{0,112},{1,113},{2,114},{3,115},{4,116},{5,117},{6,118},{7,119},{8... | collective-permute-start | bytes 589832 | tf_op jit(solution)/shard_map/while/body/eval_jaxpr/ppermute | solution.py:68
  124.4 1.1 collective-permute-start.3
  126.9 3.0 %collective-permute-done.21.refs_22_ = bf16[2,384,128]{2,1,0:T(8,128)(2,1)S(1)} collective-permute-done((bf16[2,384,128]{2,1,0:T(8,128)(2,1)S(1)}, bf16[2,384,128]{2,1,0:T(8,128)(2,1)S(1)}, u32[]{:S(2)}, u32[]{:S(2)}) %collective-permute-start.21) | collective-permute-done | bytes 196640 | tf_op jit(solution)/shard_map/while/body/eval_jaxpr/ppermute | solution.py:68
  130.5 3.7 %collective-permute-done.3 = bf16[2,384,128]{2,1,0:T(8,128)(2,1)S(1)} collective-permute-done((bf16[2,384,128]{2,1,0:T(8,128)(2,1)S(1)}, bf16[2,384,128]{2,1,0:T(8,128)(2,1)S(1)}, u32[]{:S(2)}, u32[]{:S(2)}) %collective-permute-start.3) | collective-permute-done | bytes 196640 | tf_op jit(solution)/shard_map/while/body/eval_jaxpr/ppermute | solution.py:68
  134.5 1.6 collective-permute-start.10
  136.6 1.3 collective-permute-done.4
  137.9 3.2 %collective-permute-start.26 = (bf16[2,384,128]{2,1,0:T(8,128)(2,1)S(1)}, bf16[2,384,128]{2,1,0:T(8,128)(2,1)S(1)}, u32[]{:S(2)}, u32[]{:S(2)}) collective-permute-start(bf16[2,384,128]{2,1,0:T(8,128)(2,1)S(1)} %collective-permute-done.21.refs_22_), channel_id=1, source_target_pairs={{0,112},{1,113},{2,114},{3,115},{4,116},{5,117},{6,118},{7,119},{8... | collective-permute-start | bytes 589832 | tf_op jit(solution)/shard_map/while/body/eval_jaxpr/ppermute | solution.py:68
  141.2 8.4 %collective-permute-done.15.refs_11_ = bf16[2,384,128]{2,1,0:T(8,128)(2,1)S(1)} collective-permute-done((bf16[2,384,128]{2,1,0:T(8,128)(2,1)S(1)}, bf16[2,384,128]{2,1,0:T(8,128)(2,1)S(1)}, u32[]{:S(2)}, u32[]{:S(2)}) %collective-permute-start.15) | collective-permute-done | bytes 196640 | tf_op jit(solution)/shard_map/while/body/eval_jaxpr/ppermute | solution.py:68
  149.6 1.8 collective-permute-start.8
  151.9 1.7 collective-permute-start.17
  154.0 3.6 %collective-permute-done.23.refs_21_ = bf16[2,384,128]{2,1,0:T(8,128)(2,1)S(1)} collective-permute-done((bf16[2,384,128]{2,1,0:T(8,128)(2,1)S(1)}, bf16[2,384,128]{2,1,0:T(8,128)(2,1)S(1)}, u32[]{:S(2)}, u32[]{:S(2)}) %collective-permute-start.23) | collective-permute-done | bytes 196640 | tf_op jit(solution)/shard_map/while/body/eval_jaxpr/ppermute | solution.py:68
  157.6 1.5 collective-permute-start.27
  159.1 1.8 collective-permute-done.17.refs_13_
  161.3 1.9 collective-permute-done.18.refs_14_
  163.6 1.3 collective-permute-start.9
  164.9 1.9 collective-permute-start.19
  167.5 1.5 collective-permute-done.24.refs_19_
  169.0 1.5 collective-permute-start.25
  170.5 2.4 %collective-permute-done.19.refs_15_ = bf16[2,384,128]{2,1,0:T(8,128)(2,1)S(1)} collective-permute-done((bf16[2,384,128]{2,1,0:T(8,128)(2,1)S(1)}, bf16[2,384,128]{2,1,0:T(8,128)(2,1)S(1)}, u32[]{:S(2)}, u32[]{:S(2)}) %collective-permute-start.19) | collective-permute-done | bytes 196640 | tf_op jit(solution)/shard_map/while/body/eval_jaxpr/ppermute | solution.py:68
  172.9 2.1 %collective-permute-done.20.refs_16_ = bf16[2,384,128]{2,1,0:T(8,128)(2,1)S(1)} collective-permute-done((bf16[2,384,128]{2,1,0:T(8,128)(2,1)S(1)}, bf16[2,384,128]{2,1,0:T(8,128)(2,1)S(1)}, u32[]{:S(2)}, u32[]{:S(2)}) %collective-permute-start.20) | collective-permute-done | bytes 196640 | tf_op jit(solution)/shard_map/while/body/eval_jaxpr/ppermute | solution.py:68
  176.5 5.5 %eval_jaxpr.17 = (f32[384,128]{1,0:T(8,128)}, f32[384,128]{1,0:T(8,128)}) custom-call(s32[4]{0:T(128)S(1)} %get-tuple-element.343.place, s32[1]{0:T(128)} %bitcast.59.sweep, bf16[2,384,6144]{2,1,0:T(8,128)(2,1)} %get-tuple-element.344.factors, bf16[4,384,128]{2,1,0:T(8,128)(2,1)} %copy-done, bf16[4,384,128]{2,1,0:T(8,128)(2,1)} %copy-done.1, ...), custom_call_target="tpu_custom_call" | custom-call | tf_op jit(solution)/shard_map/while/body/eval_jaxpr/pallas_call | solution.py:142
  182.2 5.6 %eval_jaxpr.16 = (f32[384,128]{1,0:T(8,128)}, f32[384,128]{1,0:T(8,128)}) custom-call(s32[4]{0:T(128)S(1)} %get-tuple-element.343.place, s32[1]{0:T(128)} %bitcast.59.sweep, bf16[2,384,6144]{2,1,0:T(8,128)(2,1)} %get-tuple-element.344.factors, bf16[4,384,128]{2,1,0:T(8,128)(2,1)} %copy-done, bf16[4,384,128]{2,1,0:T(8,128)(2,1)} %copy-done.1, ...), custom_call_target="tpu_custom_call" | custom-call | tf_op jit(solution)/shard_map/while/body/eval_jaxpr/pallas_call | solution.py:142
  187.8 2.9 %collective-permute-start.28 = (f32[384,128]{1,0:T(8,128)}, f32[384,128]{1,0:T(8,128)S(1)}, u32[]{:S(2)}, u32[]{:S(2)}) collective-permute-start(f32[384,128]{1,0:T(8,128)} %get-tuple-element.307), channel_id=1, source_target_pairs={{0,2},{1,3},{2,0},{3,1},{4,6},{5,7},{6,4},{7,5},{8,10},{9,11},{10,... | collective-permute-start | bytes 589832 | tf_op jit(solution)/shard_map/while/body/eval_jaxpr/ppermute | solution.py:68
  190.9 5.7 %collective-permute-done.28 = f32[384,128]{1,0:T(8,128)S(1)} collective-permute-done((f32[384,128]{1,0:T(8,128)}, f32[384,128]{1,0:T(8,128)S(1)}, u32[]{:S(2)}, u32[]{:S(2)}) %collective-permute-start.28) | collective-permute-done | bytes 196640 | tf_op jit(solution)/shard_map/while/body/eval_jaxpr/ppermute | solution.py:68
  196.6 3.8 %collective-permute-done.29 = f32[384,128]{1,0:T(8,128)S(1)} collective-permute-done((f32[384,128]{1,0:T(8,128)}, f32[384,128]{1,0:T(8,128)S(1)}, u32[]{:S(2)}, u32[]{:S(2)}) %collective-permute-start.29) | collective-permute-done | bytes 196640 | tf_op jit(solution)/shard_map/while/body/eval_jaxpr/ppermute | solution.py:68
  (221 shorter events, 20.1 us)
Async XLA Ops:
  3.8 15.1 %collective-permute-start = (bf16[384,128]{1,0:T(8,128)(2,1)S(1)}, bf16[384,128]{1,0:T(8,128)(2,1)S(1)}, u32[]{:S(2)}, u32[]{:S(2)}) collective-permute-start(bf16[384,128]{1,0:T(8,128)(2,1)S(1)} %get-tuple-element.326), channel_id=1, source_target_pairs={{0,32},{1,48},{2,160},{3,176},{4,36},{5,52},{6,164},{7,180},{8,40}... | collective-permute-start | bytes 294920 | tf_op jit(solution)/shard_map/while/body/eval_jaxpr/ppermute | solution.py:68
  7.0 11.8 %collective-permute-start.1 = (bf16[384,128]{1,0:T(8,128)(2,1)S(1)}, bf16[384,128]{1,0:T(8,128)(2,1)S(1)}, u32[]{:S(2)}, u32[]{:S(2)}) collective-permute-start(bf16[384,128]{1,0:T(8,128)(2,1)S(1)} %get-tuple-element.326), channel_id=1, source_target_pairs={{0,96},{1,112},{2,224},{3,240},{4,100},{5,116},{6,228},{7,244},{8,... | collective-permute-start | bytes 294920 | tf_op jit(solution)/shard_map/while/body/eval_jaxpr/ppermute | solution.py:68
  12.0 9.1 %collective-permute-start.11 = (bf16[384,128]{1,0:T(8,128)(2,1)S(1)}, bf16[384,128]{1,0:T(8,128)(2,1)S(1)}, u32[]{:S(2)}, u32[]{:S(2)}) collective-permute-start(bf16[384,128]{1,0:T(8,128)(2,1)S(1)} %get-tuple-element.326), channel_id=1, source_target_pairs={{0,232},{1,248},{2,104},{3,120},{4,236},{5,252},{6,108},{7,124},{8... | collective-permute-start | bytes 294920 | tf_op jit(solution)/shard_map/while/body/eval_jaxpr/ppermute | solution.py:68
  17.9 5.8 %collective-permute-start.12 = (bf16[384,128]{1,0:T(8,128)(2,1)S(1)}, bf16[384,128]{1,0:T(8,128)(2,1)S(1)}, u32[]{:S(2)}, u32[]{:S(2)}) collective-permute-start(bf16[384,128]{1,0:T(8,128)(2,1)S(1)} %get-tuple-element.326), channel_id=1, source_target_pairs={{0,224},{1,240},{2,96},{3,112},{4,228},{5,244},{6,100},{7,116},{8,... | collective-permute-start | bytes 294920 | tf_op jit(solution)/shard_map/while/body/eval_jaxpr/ppermute | solution.py:68
  18.9 12.0 %collective-permute-start.2 = (bf16[2,384,128]{2,1,0:T(8,128)(2,1)S(1)}, bf16[2,384,128]{2,1,0:T(8,128)(2,1)S(1)}, u32[]{:S(2)}, u32[]{:S(2)}) collective-permute-start(bf16[2,384,128]{2,1,0:T(8,128)(2,1)S(1)} %pad_maximum_fusion.6), channel_id=1, source_target_pairs={{0,16},{1,17},{2,18},{3,19},{4,20},{5,21},{6,22},{7,23},{8,24},{9,... | collective-permute-start | bytes 589832 | tf_op jit(solution)/shard_map/while/body/eval_jaxpr/ppermute | solution.py:68
  23.7 55.8 %copy-start.2 = (bf16[2,384,128]{2,1,0:T(8,128)(2,1)}, bf16[2,384,128]{2,1,0:T(8,128)(2,1)S(1)}, u32[]{:S(2)}) copy-start(bf16[2,384,128]{2,1,0:T(8,128)(2,1)S(1)} %pad_maximum_fusion.8.refs_8_) | copy-start | bytes 589828 | tf_op jit(solution)/shard_map/while
  23.7 9.2 %collective-permute-start.21 = (bf16[2,384,128]{2,1,0:T(8,128)(2,1)S(1)}, bf16[2,384,128]{2,1,0:T(8,128)(2,1)S(1)}, u32[]{:S(2)}, u32[]{:S(2)}) collective-permute-start(bf16[2,384,128]{2,1,0:T(8,128)(2,1)S(1)} %pad_maximum_fusion.8.refs_8_), channel_id=1, source_target_pairs={{0,112},{1,113},{2,114},{3,115},{4,116},{5,117},{6,118},{7,119},{8... | collective-permute-start | bytes 589832 | tf_op jit(solution)/shard_map/while/body/eval_jaxpr/ppermute | solution.py:68
  27.6 8.1 %collective-permute-start.3 = (bf16[2,384,128]{2,1,0:T(8,128)(2,1)S(1)}, bf16[2,384,128]{2,1,0:T(8,128)(2,1)S(1)}, u32[]{:S(2)}, u32[]{:S(2)}) collective-permute-start(bf16[2,384,128]{2,1,0:T(8,128)(2,1)S(1)} %pad_maximum_fusion.6), channel_id=1, source_target_pairs={{0,112},{1,113},{2,114},{3,115},{4,116},{5,117},{6,118},{7,119},{8... | collective-permute-start | bytes 589832 | tf_op jit(solution)/shard_map/while/body/eval_jaxpr/ppermute | solution.py:68
  27.9 9.0 %collective-permute-start.14 = (bf16[2,384,128]{2,1,0:T(8,128)(2,1)S(1)}, bf16[2,384,128]{2,1,0:T(8,128)(2,1)S(1)}, u32[]{:S(2)}, u32[]{:S(2)}) collective-permute-start(bf16[2,384,128]{2,1,0:T(8,128)(2,1)S(1)} %pad_maximum_fusion.8.refs_8_), channel_id=1, source_target_pairs={{0,16},{1,17},{2,18},{3,19},{4,20},{5,21},{6,22},{7,23},{8,24},{9,... | collective-permute-start | bytes 589832 | tf_op jit(solution)/shard_map/while/body/eval_jaxpr/ppermute | solution.py:68
  29.6 8.7 %collective-permute-start.13 = (bf16[2,384,128]{2,1,0:T(8,128)(2,1)S(1)}, bf16[2,384,128]{2,1,0:T(8,128)(2,1)S(1)}, u32[]{:S(2)}, u32[]{:S(2)}) collective-permute-start(bf16[2,384,128]{2,1,0:T(8,128)(2,1)S(1)} %pad_maximum_fusion.8.refs_8_), channel_id=1, source_target_pairs={{0,4},{1,5},{2,6},{3,7},{4,8},{5,9},{6,10},{7,11},{8,12},{9,13},{1... | collective-permute-start | bytes 589832 | tf_op jit(solution)/shard_map/while/body/eval_jaxpr/ppermute | solution.py:68
  31.0 9.6 %collective-permute-start.4 = (bf16[2,384,128]{2,1,0:T(8,128)(2,1)S(1)}, bf16[2,384,128]{2,1,0:T(8,128)(2,1)S(1)}, u32[]{:S(2)}, u32[]{:S(2)}) collective-permute-start(bf16[2,384,128]{2,1,0:T(8,128)(2,1)S(1)} %collective-permute-done.2), channel_id=1, source_target_pairs={{0,16},{1,17},{2,18},{3,19},{4,20},{5,21},{6,22},{7,23},{8,24},{9,... | collective-permute-start | bytes 589832 | tf_op jit(solution)/shard_map/while/body/eval_jaxpr/ppermute | solution.py:68
  32.9 7.7 %collective-permute-start.22 = (bf16[2,384,128]{2,1,0:T(8,128)(2,1)S(1)}, bf16[2,384,128]{2,1,0:T(8,128)(2,1)S(1)}, u32[]{:S(2)}, u32[]{:S(2)}) collective-permute-start(bf16[2,384,128]{2,1,0:T(8,128)(2,1)S(1)} %collective-permute-done.21.refs_22_), channel_id=1, source_target_pairs={{0,12},{1,13},{2,14},{3,15},{4,0},{5,1},{6,2},{7,3},{8,4},{9,5},{1... | collective-permute-start | bytes 589832 | tf_op jit(solution)/shard_map/while/body/eval_jaxpr/ppermute | solution.py:68
  35.7 19.9 %collective-permute-start.5 = (bf16[4,384,128]{2,1,0:T(8,128)(2,1)S(1)}, bf16[4,384,128]{2,1,0:T(8,128)(2,1)S(1)}, u32[]{:S(2)}, u32[]{:S(2)}) collective-permute-start(bf16[4,384,128]{2,1,0:T(8,128)(2,1)S(1)} %pad_maximum_fusion.7.refs_0_), channel_id=1, source_target_pairs={{0,4},{1,5},{2,6},{3,7},{4,8},{5,9},{6,10},{7,11},{8,12},{9,13},{1... | collective-permute-start | bytes 1179656 | tf_op jit(solution)/shard_map/while/body/eval_jaxpr/ppermute | solution.py:68
  36.8 18.8 %collective-permute-start.10 = (bf16[4,384,128]{2,1,0:T(8,128)(2,1)S(1)}, bf16[4,384,128]{2,1,0:T(8,128)(2,1)S(1)}, u32[]{:S(2)}, u32[]{:S(2)}) collective-permute-start(bf16[4,384,128]{2,1,0:T(8,128)(2,1)S(1)} %pad_maximum_fusion.7.refs_0_), channel_id=1, source_target_pairs={{0,12},{1,13},{2,14},{3,15},{4,0},{5,1},{6,2},{7,3},{8,4},{9,5},{1... | collective-permute-start | bytes 1179656 | tf_op jit(solution)/shard_map/while/body/eval_jaxpr/ppermute | solution.py:68
  38.3 12.8 %collective-permute-start.15 = (bf16[2,384,128]{2,1,0:T(8,128)(2,1)S(1)}, bf16[2,384,128]{2,1,0:T(8,128)(2,1)S(1)}, u32[]{:S(2)}, u32[]{:S(2)}) collective-permute-start(bf16[2,384,128]{2,1,0:T(8,128)(2,1)S(1)} %collective-permute-done.14.refs_10_), channel_id=1, source_target_pairs={{0,4},{1,5},{2,6},{3,7},{4,8},{5,9},{6,10},{7,11},{8,12},{9,13},{1... | collective-permute-start | bytes 589832 | tf_op jit(solution)/shard_map/while/body/eval_jaxpr/ppermute | solution.py:68
  40.6 12.9 %collective-permute-start.16 = (bf16[2,384,128]{2,1,0:T(8,128)(2,1)S(1)}, bf16[2,384,128]{2,1,0:T(8,128)(2,1)S(1)}, u32[]{:S(2)}, u32[]{:S(2)}) collective-permute-start(bf16[2,384,128]{2,1,0:T(8,128)(2,1)S(1)} %collective-permute-done.14.refs_10_), channel_id=1, source_target_pairs={{0,16},{1,17},{2,18},{3,19},{4,20},{5,21},{6,22},{7,23},{8,24},{9,... | collective-permute-start | bytes 589832 | tf_op jit(solution)/shard_map/while/body/eval_jaxpr/ppermute | solution.py:68
  40.6 12.9 %collective-permute-start.26 = (bf16[2,384,128]{2,1,0:T(8,128)(2,1)S(1)}, bf16[2,384,128]{2,1,0:T(8,128)(2,1)S(1)}, u32[]{:S(2)}, u32[]{:S(2)}) collective-permute-start(bf16[2,384,128]{2,1,0:T(8,128)(2,1)S(1)} %collective-permute-done.21.refs_22_), channel_id=1, source_target_pairs={{0,112},{1,113},{2,114},{3,115},{4,116},{5,117},{6,118},{7,119},{8... | collective-permute-start | bytes 589832 | tf_op jit(solution)/shard_map/while/body/eval_jaxpr/ppermute | solution.py:68
  51.1 16.7 %collective-permute-start.8 = (bf16[4,384,128]{2,1,0:T(8,128)(2,1)S(1)}, bf16[4,384,128]{2,1,0:T(8,128)(2,1)S(1)}, u32[]{:S(2)}, u32[]{:S(2)}) collective-permute-start(bf16[4,384,128]{2,1,0:T(8,128)(2,1)S(1)} %constant_dynamic-update-slice_fusion.5.refs_1_), channel_id=1, source_target_pairs={{0,12},{1,13},{2,14},{3,15},{4,0},{5,1},{6,2},{7,3},{8,4},{9,5},{1... | collective-permute-start | bytes 1179656 | tf_op jit(solution)/shard_map/while/body/eval_jaxpr/ppermute | solution.py:68
  53.5 16.2 %collective-permute-start.6 = (bf16[4,384,128]{2,1,0:T(8,128)(2,1)S(1)}, bf16[4,384,128]{2,1,0:T(8,128)(2,1)S(1)}, u32[]{:S(2)}, u32[]{:S(2)}) collective-permute-start(bf16[4,384,128]{2,1,0:T(8,128)(2,1)S(1)} %constant_dynamic-update-slice_fusion.5.refs_1_), channel_id=1, source_target_pairs={{0,4},{1,5},{2,6},{3,7},{4,8},{5,9},{6,10},{7,11},{8,12},{9,13},{1... | collective-permute-start | bytes 1179656 | tf_op jit(solution)/shard_map/while/body/eval_jaxpr/ppermute | solution.py:68
  53.5 6.0 %collective-permute-start.23 = (bf16[2,384,128]{2,1,0:T(8,128)(2,1)S(1)}, bf16[2,384,128]{2,1,0:T(8,128)(2,1)S(1)}, u32[]{:S(2)}, u32[]{:S(2)}) collective-permute-start(bf16[2,384,128]{2,1,0:T(8,128)(2,1)S(1)} %collective-permute-done.22.refs_23_), channel_id=1, source_target_pairs={{0,112},{1,113},{2,114},{3,115},{4,116},{5,117},{6,118},{7,119},{8... | collective-permute-start | bytes 589832 | tf_op jit(solution)/shard_map/while/body/eval_jaxpr/ppermute | solution.py:68
  55.6 8.4 %collective-permute-start.17 = (bf16[2,384,128]{2,1,0:T(8,128)(2,1)S(1)}, bf16[2,384,128]{2,1,0:T(8,128)(2,1)S(1)}, u32[]{:S(2)}, u32[]{:S(2)}) collective-permute-start(bf16[2,384,128]{2,1,0:T(8,128)(2,1)S(1)} %collective-permute-done.15.refs_11_), channel_id=1, source_target_pairs={{0,16},{1,17},{2,18},{3,19},{4,20},{5,21},{6,22},{7,23},{8,24},{9,... | collective-permute-start | bytes 589832 | tf_op jit(solution)/shard_map/while/body/eval_jaxpr/ppermute | solution.py:68
  55.6 10.4 %collective-permute-start.18 = (bf16[2,384,128]{2,1,0:T(8,128)(2,1)S(1)}, bf16[2,384,128]{2,1,0:T(8,128)(2,1)S(1)}, u32[]{:S(2)}, u32[]{:S(2)}) collective-permute-start(bf16[2,384,128]{2,1,0:T(8,128)(2,1)S(1)} %collective-permute-done.16.refs_12_), channel_id=1, source_target_pairs={{0,16},{1,17},{2,18},{3,19},{4,20},{5,21},{6,22},{7,23},{8,24},{9,... | collective-permute-start | bytes 589832 | tf_op jit(solution)/shard_map/while/body/eval_jaxpr/ppermute | solution.py:68
  59.5 9.9 %collective-permute-start.27 = (bf16[2,384,128]{2,1,0:T(8,128)(2,1)S(1)}, bf16[2,384,128]{2,1,0:T(8,128)(2,1)S(1)}, u32[]{:S(2)}, u32[]{:S(2)}) collective-permute-start(bf16[2,384,128]{2,1,0:T(8,128)(2,1)S(1)} %collective-permute-done.26.refs_20_), channel_id=1, source_target_pairs={{0,112},{1,113},{2,114},{3,115},{4,116},{5,117},{6,118},{7,119},{8... | collective-permute-start | bytes 589832 | tf_op jit(solution)/shard_map/while/body/eval_jaxpr/ppermute | solution.py:68
  63.9 14.9 %collective-permute-start.7 = (bf16[4,384,128]{2,1,0:T(8,128)(2,1)S(1)}, bf16[4,384,128]{2,1,0:T(8,128)(2,1)S(1)}, u32[]{:S(2)}, u32[]{:S(2)}) collective-permute-start(bf16[4,384,128]{2,1,0:T(8,128)(2,1)S(1)} %collective-permute-done.5.refs_2_), channel_id=1, source_target_pairs={{0,4},{1,5},{2,6},{3,7},{4,8},{5,9},{6,10},{7,11},{8,12},{9,13},{1... | collective-permute-start | bytes 1179656 | tf_op jit(solution)/shard_map/while/body/eval_jaxpr/ppermute | solution.py:68
  66.0 6.5 %collective-permute-start.24 = (bf16[2,384,128]{2,1,0:T(8,128)(2,1)S(1)}, bf16[2,384,128]{2,1,0:T(8,128)(2,1)S(1)}, u32[]{:S(2)}, u32[]{:S(2)}) collective-permute-start(bf16[2,384,128]{2,1,0:T(8,128)(2,1)S(1)} %collective-permute-done.23.refs_21_), channel_id=1, source_target_pairs={{0,112},{1,113},{2,114},{3,115},{4,116},{5,117},{6,118},{7,119},{8... | collective-permute-start | bytes 589832 | tf_op jit(solution)/shard_map/while/body/eval_jaxpr/ppermute | solution.py:68
  67.8 11.0 %collective-permute-start.9 = (bf16[4,384,128]{2,1,0:T(8,128)(2,1)S(1)}, bf16[4,384,128]{2,1,0:T(8,128)(2,1)S(1)}, u32[]{:S(2)}, u32[]{:S(2)}) collective-permute-start(bf16[4,384,128]{2,1,0:T(8,128)(2,1)S(1)} %collective-permute-done.8.refs_7_), channel_id=1, source_target_pairs={{0,12},{1,13},{2,14},{3,15},{4,0},{5,1},{6,2},{7,3},{8,4},{9,5},{1... | collective-permute-start | bytes 1179656 | tf_op jit(solution)/shard_map/while/body/eval_jaxpr/ppermute | solution.py:68
  69.4 7.2 %collective-permute-start.19 = (bf16[2,384,128]{2,1,0:T(8,128)(2,1)S(1)}, bf16[2,384,128]{2,1,0:T(8,128)(2,1)S(1)}, u32[]{:S(2)}, u32[]{:S(2)}) collective-permute-start(bf16[2,384,128]{2,1,0:T(8,128)(2,1)S(1)} %collective-permute-done.17.refs_13_), channel_id=1, source_target_pairs={{0,16},{1,17},{2,18},{3,19},{4,20},{5,21},{6,22},{7,23},{8,24},{9,... | collective-permute-start | bytes 589832 | tf_op jit(solution)/shard_map/while/body/eval_jaxpr/ppermute | solution.py:68
  69.7 9.1 %collective-permute-start.20 = (bf16[2,384,128]{2,1,0:T(8,128)(2,1)S(1)}, bf16[2,384,128]{2,1,0:T(8,128)(2,1)S(1)}, u32[]{:S(2)}, u32[]{:S(2)}) collective-permute-start(bf16[2,384,128]{2,1,0:T(8,128)(2,1)S(1)} %collective-permute-done.18.refs_14_), channel_id=1, source_target_pairs={{0,16},{1,17},{2,18},{3,19},{4,20},{5,21},{6,22},{7,23},{8,24},{9,... | collective-permute-start | bytes 589832 | tf_op jit(solution)/shard_map/while/body/eval_jaxpr/ppermute | solution.py:68
  72.6 6.2 %collective-permute-start.25 = (bf16[2,384,128]{2,1,0:T(8,128)(2,1)S(1)}, bf16[2,384,128]{2,1,0:T(8,128)(2,1)S(1)}, u32[]{:S(2)}, u32[]{:S(2)}) collective-permute-start(bf16[2,384,128]{2,1,0:T(8,128)(2,1)S(1)} %collective-permute-done.24.refs_19_), channel_id=1, source_target_pairs={{0,112},{1,113},{2,114},{3,115},{4,116},{5,117},{6,118},{7,119},{8... | collective-permute-start | bytes 589832 | tf_op jit(solution)/shard_map/while/body/eval_jaxpr/ppermute | solution.py:68
  85.9 8.8 %collective-permute-start.30 = (f32[384,128]{1,0:T(8,128)}, f32[384,128]{1,0:T(8,128)S(1)}, u32[]{:S(2)}, u32[]{:S(2)}) collective-permute-start(f32[384,128]{1,0:T(8,128)} %get-tuple-element.310), channel_id=1, source_target_pairs={{0,1},{1,0},{2,3},{3,2},{4,5},{5,4},{6,7},{7,6},{8,9},{9,8},{10,11... | collective-permute-start | bytes 589832 | tf_op jit(solution)/shard_map/while/body/eval_jaxpr/ppermute | solution.py:68
  91.6 8.8 %collective-permute-start.28 = (f32[384,128]{1,0:T(8,128)}, f32[384,128]{1,0:T(8,128)S(1)}, u32[]{:S(2)}, u32[]{:S(2)}) collective-permute-start(f32[384,128]{1,0:T(8,128)} %get-tuple-element.307), channel_id=1, source_target_pairs={{0,2},{1,3},{2,0},{3,1},{4,6},{5,7},{6,4},{7,5},{8,10},{9,11},{10,... | collective-permute-start | bytes 589832 | tf_op jit(solution)/shard_map/while/body/eval_jaxpr/ppermute | solution.py:68
  94.4 9.7 %collective-permute-start.29 = (f32[384,128]{1,0:T(8,128)}, f32[384,128]{1,0:T(8,128)S(1)}, u32[]{:S(2)}, u32[]{:S(2)}) collective-permute-start(f32[384,128]{1,0:T(8,128)} %get-tuple-element.308), channel_id=1, source_target_pairs={{0,3},{1,2},{2,1},{3,0},{4,7},{5,6},{6,5},{7,4},{8,11},{9,10},{10,... | collective-permute-start | bytes 589832 | tf_op jit(solution)/shard_map/while/body/eval_jaxpr/ppermute | solution.py:68
  105.7 10.3 %collective-permute-start = (bf16[384,128]{1,0:T(8,128)(2,1)S(1)}, bf16[384,128]{1,0:T(8,128)(2,1)S(1)}, u32[]{:S(2)}, u32[]{:S(2)}) collective-permute-start(bf16[384,128]{1,0:T(8,128)(2,1)S(1)} %get-tuple-element.326), channel_id=1, source_target_pairs={{0,32},{1,48},{2,160},{3,176},{4,36},{5,52},{6,164},{7,180},{8,40}... | collective-permute-start | bytes 294920 | tf_op jit(solution)/shard_map/while/body/eval_jaxpr/ppermute | solution.py:68
  105.7 10.3 %collective-permute-start.1 = (bf16[384,128]{1,0:T(8,128)(2,1)S(1)}, bf16[384,128]{1,0:T(8,128)(2,1)S(1)}, u32[]{:S(2)}, u32[]{:S(2)}) collective-permute-start(bf16[384,128]{1,0:T(8,128)(2,1)S(1)} %get-tuple-element.326), channel_id=1, source_target_pairs={{0,96},{1,112},{2,224},{3,240},{4,100},{5,116},{6,228},{7,244},{8,... | collective-permute-start | bytes 294920 | tf_op jit(solution)/shard_map/while/body/eval_jaxpr/ppermute | solution.py:68
  109.5 9.8 %collective-permute-start.11 = (bf16[384,128]{1,0:T(8,128)(2,1)S(1)}, bf16[384,128]{1,0:T(8,128)(2,1)S(1)}, u32[]{:S(2)}, u32[]{:S(2)}) collective-permute-start(bf16[384,128]{1,0:T(8,128)(2,1)S(1)} %get-tuple-element.326), channel_id=1, source_target_pairs={{0,232},{1,248},{2,104},{3,120},{4,236},{5,252},{6,108},{7,124},{8... | collective-permute-start | bytes 294920 | tf_op jit(solution)/shard_map/while/body/eval_jaxpr/ppermute | solution.py:68
  116.0 6.1 %collective-permute-start.12 = (bf16[384,128]{1,0:T(8,128)(2,1)S(1)}, bf16[384,128]{1,0:T(8,128)(2,1)S(1)}, u32[]{:S(2)}, u32[]{:S(2)}) collective-permute-start(bf16[384,128]{1,0:T(8,128)(2,1)S(1)} %get-tuple-element.326), channel_id=1, source_target_pairs={{0,224},{1,240},{2,96},{3,112},{4,228},{5,244},{6,100},{7,116},{8,... | collective-permute-start | bytes 294920 | tf_op jit(solution)/shard_map/while/body/eval_jaxpr/ppermute | solution.py:68
  116.1 10.9 %collective-permute-start.2 = (bf16[2,384,128]{2,1,0:T(8,128)(2,1)S(1)}, bf16[2,384,128]{2,1,0:T(8,128)(2,1)S(1)}, u32[]{:S(2)}, u32[]{:S(2)}) collective-permute-start(bf16[2,384,128]{2,1,0:T(8,128)(2,1)S(1)} %pad_maximum_fusion.6), channel_id=1, source_target_pairs={{0,16},{1,17},{2,18},{3,19},{4,20},{5,21},{6,22},{7,23},{8,24},{9,... | collective-permute-start | bytes 589832 | tf_op jit(solution)/shard_map/while/body/eval_jaxpr/ppermute | solution.py:68
  122.2 53.6 %copy-start.2 = (bf16[2,384,128]{2,1,0:T(8,128)(2,1)}, bf16[2,384,128]{2,1,0:T(8,128)(2,1)S(1)}, u32[]{:S(2)}) copy-start(bf16[2,384,128]{2,1,0:T(8,128)(2,1)S(1)} %pad_maximum_fusion.8.refs_8_) | copy-start | bytes 589828 | tf_op jit(solution)/shard_map/while
  122.2 7.8 %collective-permute-start.21 = (bf16[2,384,128]{2,1,0:T(8,128)(2,1)S(1)}, bf16[2,384,128]{2,1,0:T(8,128)(2,1)S(1)}, u32[]{:S(2)}, u32[]{:S(2)}) collective-permute-start(bf16[2,384,128]{2,1,0:T(8,128)(2,1)S(1)} %pad_maximum_fusion.8.refs_8_), channel_id=1, source_target_pairs={{0,112},{1,113},{2,114},{3,115},{4,116},{5,117},{6,118},{7,119},{8... | collective-permute-start | bytes 589832 | tf_op jit(solution)/shard_map/while/body/eval_jaxpr/ppermute | solution.py:68
  124.4 9.7 %collective-permute-start.3 = (bf16[2,384,128]{2,1,0:T(8,128)(2,1)S(1)}, bf16[2,384,128]{2,1,0:T(8,128)(2,1)S(1)}, u32[]{:S(2)}, u32[]{:S(2)}) collective-permute-start(bf16[2,384,128]{2,1,0:T(8,128)(2,1)S(1)} %pad_maximum_fusion.6), channel_id=1, source_target_pairs={{0,112},{1,113},{2,114},{3,115},{4,116},{5,117},{6,118},{7,119},{8... | collective-permute-start | bytes 589832 | tf_op jit(solution)/shard_map/while/body/eval_jaxpr/ppermute | solution.py:68
  125.5 9.0 %collective-permute-start.14 = (bf16[2,384,128]{2,1,0:T(8,128)(2,1)S(1)}, bf16[2,384,128]{2,1,0:T(8,128)(2,1)S(1)}, u32[]{:S(2)}, u32[]{:S(2)}) collective-permute-start(bf16[2,384,128]{2,1,0:T(8,128)(2,1)S(1)} %pad_maximum_fusion.8.refs_8_), channel_id=1, source_target_pairs={{0,16},{1,17},{2,18},{3,19},{4,20},{5,21},{6,22},{7,23},{8,24},{9,... | collective-permute-start | bytes 589832 | tf_op jit(solution)/shard_map/while/body/eval_jaxpr/ppermute | solution.py:68
  126.5 9.7 %collective-permute-start.13 = (bf16[2,384,128]{2,1,0:T(8,128)(2,1)S(1)}, bf16[2,384,128]{2,1,0:T(8,128)(2,1)S(1)}, u32[]{:S(2)}, u32[]{:S(2)}) collective-permute-start(bf16[2,384,128]{2,1,0:T(8,128)(2,1)S(1)} %pad_maximum_fusion.8.refs_8_), channel_id=1, source_target_pairs={{0,4},{1,5},{2,6},{3,7},{4,8},{5,9},{6,10},{7,11},{8,12},{9,13},{1... | collective-permute-start | bytes 589832 | tf_op jit(solution)/shard_map/while/body/eval_jaxpr/ppermute | solution.py:68
  126.9 11.0 %collective-permute-start.4 = (bf16[2,384,128]{2,1,0:T(8,128)(2,1)S(1)}, bf16[2,384,128]{2,1,0:T(8,128)(2,1)S(1)}, u32[]{:S(2)}, u32[]{:S(2)}) collective-permute-start(bf16[2,384,128]{2,1,0:T(8,128)(2,1)S(1)} %collective-permute-done.2), channel_id=1, source_target_pairs={{0,16},{1,17},{2,18},{3,19},{4,20},{5,21},{6,22},{7,23},{8,24},{9,... | collective-permute-start | bytes 589832 | tf_op jit(solution)/shard_map/while/body/eval_jaxpr/ppermute | solution.py:68
  129.9 8.0 %collective-permute-start.22 = (bf16[2,384,128]{2,1,0:T(8,128)(2,1)S(1)}, bf16[2,384,128]{2,1,0:T(8,128)(2,1)S(1)}, u32[]{:S(2)}, u32[]{:S(2)}) collective-permute-start(bf16[2,384,128]{2,1,0:T(8,128)(2,1)S(1)} %collective-permute-done.21.refs_22_), channel_id=1, source_target_pairs={{0,12},{1,13},{2,14},{3,15},{4,0},{5,1},{6,2},{7,3},{8,4},{9,5},{1... | collective-permute-start | bytes 589832 | tf_op jit(solution)/shard_map/while/body/eval_jaxpr/ppermute | solution.py:68
  134.1 17.8 %collective-permute-start.5 = (bf16[4,384,128]{2,1,0:T(8,128)(2,1)S(1)}, bf16[4,384,128]{2,1,0:T(8,128)(2,1)S(1)}, u32[]{:S(2)}, u32[]{:S(2)}) collective-permute-start(bf16[4,384,128]{2,1,0:T(8,128)(2,1)S(1)} %pad_maximum_fusion.7.refs_0_), channel_id=1, source_target_pairs={{0,4},{1,5},{2,6},{3,7},{4,8},{5,9},{6,10},{7,11},{8,12},{9,13},{1... | collective-permute-start | bytes 1179656 | tf_op jit(solution)/shard_map/while/body/eval_jaxpr/ppermute | solution.py:68
  134.5 19.1 %collective-permute-start.10 = (bf16[4,384,128]{2,1,0:T(8,128)(2,1)S(1)}, bf16[4,384,128]{2,1,0:T(8,128)(2,1)S(1)}, u32[]{:S(2)}, u32[]{:S(2)}) collective-permute-start(bf16[4,384,128]{2,1,0:T(8,128)(2,1)S(1)} %pad_maximum_fusion.7.refs_0_), channel_id=1, source_target_pairs={{0,12},{1,13},{2,14},{3,15},{4,0},{5,1},{6,2},{7,3},{8,4},{9,5},{1... | collective-permute-start | bytes 1179656 | tf_op jit(solution)/shard_map/while/body/eval_jaxpr/ppermute | solution.py:68
  136.2 13.4 %collective-permute-start.15 = (bf16[2,384,128]{2,1,0:T(8,128)(2,1)S(1)}, bf16[2,384,128]{2,1,0:T(8,128)(2,1)S(1)}, u32[]{:S(2)}, u32[]{:S(2)}) collective-permute-start(bf16[2,384,128]{2,1,0:T(8,128)(2,1)S(1)} %collective-permute-done.14.refs_10_), channel_id=1, source_target_pairs={{0,4},{1,5},{2,6},{3,7},{4,8},{5,9},{6,10},{7,11},{8,12},{9,13},{1... | collective-permute-start | bytes 589832 | tf_op jit(solution)/shard_map/while/body/eval_jaxpr/ppermute | solution.py:68
  137.9 13.4 %collective-permute-start.16 = (bf16[2,384,128]{2,1,0:T(8,128)(2,1)S(1)}, bf16[2,384,128]{2,1,0:T(8,128)(2,1)S(1)}, u32[]{:S(2)}, u32[]{:S(2)}) collective-permute-start(bf16[2,384,128]{2,1,0:T(8,128)(2,1)S(1)} %collective-permute-done.14.refs_10_), channel_id=1, source_target_pairs={{0,16},{1,17},{2,18},{3,19},{4,20},{5,21},{6,22},{7,23},{8,24},{9,... | collective-permute-start | bytes 589832 | tf_op jit(solution)/shard_map/while/body/eval_jaxpr/ppermute | solution.py:68
  137.9 13.7 %collective-permute-start.26 = (bf16[2,384,128]{2,1,0:T(8,128)(2,1)S(1)}, bf16[2,384,128]{2,1,0:T(8,128)(2,1)S(1)}, u32[]{:S(2)}, u32[]{:S(2)}) collective-permute-start(bf16[2,384,128]{2,1,0:T(8,128)(2,1)S(1)} %collective-permute-done.21.refs_22_), channel_id=1, source_target_pairs={{0,112},{1,113},{2,114},{3,115},{4,116},{5,117},{6,118},{7,119},{8... | collective-permute-start | bytes 589832 | tf_op jit(solution)/shard_map/while/body/eval_jaxpr/ppermute | solution.py:68
  149.6 14.0 %collective-permute-start.8 = (bf16[4,384,128]{2,1,0:T(8,128)(2,1)S(1)}, bf16[4,384,128]{2,1,0:T(8,128)(2,1)S(1)}, u32[]{:S(2)}, u32[]{:S(2)}) collective-permute-start(bf16[4,384,128]{2,1,0:T(8,128)(2,1)S(1)} %constant_dynamic-update-slice_fusion.5.refs_1_), channel_id=1, source_target_pairs={{0,12},{1,13},{2,14},{3,15},{4,0},{5,1},{6,2},{7,3},{8,4},{9,5},{1... | collective-permute-start | bytes 1179656 | tf_op jit(solution)/shard_map/while/body/eval_jaxpr/ppermute | solution.py:68
  151.4 15.5 %collective-permute-start.6 = (bf16[4,384,128]{2,1,0:T(8,128)(2,1)S(1)}, bf16[4,384,128]{2,1,0:T(8,128)(2,1)S(1)}, u32[]{:S(2)}, u32[]{:S(2)}) collective-permute-start(bf16[4,384,128]{2,1,0:T(8,128)(2,1)S(1)} %constant_dynamic-update-slice_fusion.5.refs_1_), channel_id=1, source_target_pairs={{0,4},{1,5},{2,6},{3,7},{4,8},{5,9},{6,10},{7,11},{8,12},{9,13},{1... | collective-permute-start | bytes 1179656 | tf_op jit(solution)/shard_map/while/body/eval_jaxpr/ppermute | solution.py:68
  151.6 6.0 %collective-permute-start.23 = (bf16[2,384,128]{2,1,0:T(8,128)(2,1)S(1)}, bf16[2,384,128]{2,1,0:T(8,128)(2,1)S(1)}, u32[]{:S(2)}, u32[]{:S(2)}) collective-permute-start(bf16[2,384,128]{2,1,0:T(8,128)(2,1)S(1)} %collective-permute-done.22.refs_23_), channel_id=1, source_target_pairs={{0,112},{1,113},{2,114},{3,115},{4,116},{5,117},{6,118},{7,119},{8... | collective-permute-start | bytes 589832 | tf_op jit(solution)/shard_map/while/body/eval_jaxpr/ppermute | solution.py:68
  151.9 9.0 %collective-permute-start.17 = (bf16[2,384,128]{2,1,0:T(8,128)(2,1)S(1)}, bf16[2,384,128]{2,1,0:T(8,128)(2,1)S(1)}, u32[]{:S(2)}, u32[]{:S(2)}) collective-permute-start(bf16[2,384,128]{2,1,0:T(8,128)(2,1)S(1)} %collective-permute-done.15.refs_11_), channel_id=1, source_target_pairs={{0,16},{1,17},{2,18},{3,19},{4,20},{5,21},{6,22},{7,23},{8,24},{9,... | collective-permute-start | bytes 589832 | tf_op jit(solution)/shard_map/while/body/eval_jaxpr/ppermute | solution.py:68
  153.7 9.5 %collective-permute-start.18 = (bf16[2,384,128]{2,1,0:T(8,128)(2,1)S(1)}, bf16[2,384,128]{2,1,0:T(8,128)(2,1)S(1)}, u32[]{:S(2)}, u32[]{:S(2)}) collective-permute-start(bf16[2,384,128]{2,1,0:T(8,128)(2,1)S(1)} %collective-permute-done.16.refs_12_), channel_id=1, source_target_pairs={{0,16},{1,17},{2,18},{3,19},{4,20},{5,21},{6,22},{7,23},{8,24},{9,... | collective-permute-start | bytes 589832 | tf_op jit(solution)/shard_map/while/body/eval_jaxpr/ppermute | solution.py:68
  157.6 7.3 %collective-permute-start.27 = (bf16[2,384,128]{2,1,0:T(8,128)(2,1)S(1)}, bf16[2,384,128]{2,1,0:T(8,128)(2,1)S(1)}, u32[]{:S(2)}, u32[]{:S(2)}) collective-permute-start(bf16[2,384,128]{2,1,0:T(8,128)(2,1)S(1)} %collective-permute-done.26.refs_20_), channel_id=1, source_target_pairs={{0,112},{1,113},{2,114},{3,115},{4,116},{5,117},{6,118},{7,119},{8... | collective-permute-start | bytes 589832 | tf_op jit(solution)/shard_map/while/body/eval_jaxpr/ppermute | solution.py:68
  160.9 14.1 %collective-permute-start.7 = (bf16[4,384,128]{2,1,0:T(8,128)(2,1)S(1)}, bf16[4,384,128]{2,1,0:T(8,128)(2,1)S(1)}, u32[]{:S(2)}, u32[]{:S(2)}) collective-permute-start(bf16[4,384,128]{2,1,0:T(8,128)(2,1)S(1)} %collective-permute-done.5.refs_2_), channel_id=1, source_target_pairs={{0,4},{1,5},{2,6},{3,7},{4,8},{5,9},{6,10},{7,11},{8,12},{9,13},{1... | collective-permute-start | bytes 1179656 | tf_op jit(solution)/shard_map/while/body/eval_jaxpr/ppermute | solution.py:68
  163.2 5.8 %collective-permute-start.24 = (bf16[2,384,128]{2,1,0:T(8,128)(2,1)S(1)}, bf16[2,384,128]{2,1,0:T(8,128)(2,1)S(1)}, u32[]{:S(2)}, u32[]{:S(2)}) collective-permute-start(bf16[2,384,128]{2,1,0:T(8,128)(2,1)S(1)} %collective-permute-done.23.refs_21_), channel_id=1, source_target_pairs={{0,112},{1,113},{2,114},{3,115},{4,116},{5,117},{6,118},{7,119},{8... | collective-permute-start | bytes 589832 | tf_op jit(solution)/shard_map/while/body/eval_jaxpr/ppermute | solution.py:68
  163.6 11.4 %collective-permute-start.9 = (bf16[4,384,128]{2,1,0:T(8,128)(2,1)S(1)}, bf16[4,384,128]{2,1,0:T(8,128)(2,1)S(1)}, u32[]{:S(2)}, u32[]{:S(2)}) collective-permute-start(bf16[4,384,128]{2,1,0:T(8,128)(2,1)S(1)} %collective-permute-done.8.refs_7_), channel_id=1, source_target_pairs={{0,12},{1,13},{2,14},{3,15},{4,0},{5,1},{6,2},{7,3},{8,4},{9,5},{1... | collective-permute-start | bytes 1179656 | tf_op jit(solution)/shard_map/while/body/eval_jaxpr/ppermute | solution.py:68
  164.9 8.0 %collective-permute-start.19 = (bf16[2,384,128]{2,1,0:T(8,128)(2,1)S(1)}, bf16[2,384,128]{2,1,0:T(8,128)(2,1)S(1)}, u32[]{:S(2)}, u32[]{:S(2)}) collective-permute-start(bf16[2,384,128]{2,1,0:T(8,128)(2,1)S(1)} %collective-permute-done.17.refs_13_), channel_id=1, source_target_pairs={{0,16},{1,17},{2,18},{3,19},{4,20},{5,21},{6,22},{7,23},{8,24},{9,... | collective-permute-start | bytes 589832 | tf_op jit(solution)/shard_map/while/body/eval_jaxpr/ppermute | solution.py:68
  166.8 8.1 %collective-permute-start.20 = (bf16[2,384,128]{2,1,0:T(8,128)(2,1)S(1)}, bf16[2,384,128]{2,1,0:T(8,128)(2,1)S(1)}, u32[]{:S(2)}, u32[]{:S(2)}) collective-permute-start(bf16[2,384,128]{2,1,0:T(8,128)(2,1)S(1)} %collective-permute-done.18.refs_14_), channel_id=1, source_target_pairs={{0,16},{1,17},{2,18},{3,19},{4,20},{5,21},{6,22},{7,23},{8,24},{9,... | collective-permute-start | bytes 589832 | tf_op jit(solution)/shard_map/while/body/eval_jaxpr/ppermute | solution.py:68
  169.0 6.0 %collective-permute-start.25 = (bf16[2,384,128]{2,1,0:T(8,128)(2,1)S(1)}, bf16[2,384,128]{2,1,0:T(8,128)(2,1)S(1)}, u32[]{:S(2)}, u32[]{:S(2)}) collective-permute-start(bf16[2,384,128]{2,1,0:T(8,128)(2,1)S(1)} %collective-permute-done.24.refs_19_), channel_id=1, source_target_pairs={{0,112},{1,113},{2,114},{3,115},{4,116},{5,117},{6,118},{7,119},{8... | collective-permute-start | bytes 589832 | tf_op jit(solution)/shard_map/while/body/eval_jaxpr/ppermute | solution.py:68
  182.1 8.8 %collective-permute-start.30 = (f32[384,128]{1,0:T(8,128)}, f32[384,128]{1,0:T(8,128)S(1)}, u32[]{:S(2)}, u32[]{:S(2)}) collective-permute-start(f32[384,128]{1,0:T(8,128)} %get-tuple-element.310), channel_id=1, source_target_pairs={{0,1},{1,0},{2,3},{3,2},{4,5},{5,4},{6,7},{7,6},{8,9},{9,8},{10,11... | collective-permute-start | bytes 589832 | tf_op jit(solution)/shard_map/while/body/eval_jaxpr/ppermute | solution.py:68
  187.8 8.9 %collective-permute-start.28 = (f32[384,128]{1,0:T(8,128)}, f32[384,128]{1,0:T(8,128)S(1)}, u32[]{:S(2)}, u32[]{:S(2)}) collective-permute-start(f32[384,128]{1,0:T(8,128)} %get-tuple-element.307), channel_id=1, source_target_pairs={{0,2},{1,3},{2,0},{3,1},{4,6},{5,7},{6,4},{7,5},{8,10},{9,11},{10,... | collective-permute-start | bytes 589832 | tf_op jit(solution)/shard_map/while/body/eval_jaxpr/ppermute | solution.py:68
  190.7 9.7 %collective-permute-start.29 = (f32[384,128]{1,0:T(8,128)}, f32[384,128]{1,0:T(8,128)S(1)}, u32[]{:S(2)}, u32[]{:S(2)}) collective-permute-start(f32[384,128]{1,0:T(8,128)} %get-tuple-element.308), channel_id=1, source_target_pairs={{0,3},{1,2},{2,1},{3,0},{4,7},{5,6},{6,5},{7,4},{8,11},{9,10},{10,... | collective-permute-start | bytes 589832 | tf_op jit(solution)/shard_map/while/body/eval_jaxpr/ppermute | solution.py:68
  (61 other events, 1114.9 us)
